TPU v7x, 256 devices: a whole 4x4x8 slice. The times are simulated.
256 devices in a mesh: sub: 16 (over z, core), dom: 16 (over y, x).
Axes of the slice: x: 4, y: 4, z: 8, core: 2. Of those that a mesh axis runs over, the one named last changes fastest.
Arguments:
- start_vectors: float32 [16, 3, 64, 16, 16, 128], P('sub', None, None, 'dom'), may hold values from -6 to 6
- face_x: float32 [16, 16, 16, 128], P('sub', 'dom'), may hold values from 0.1 to 10
- face_y: float32 [16, 16, 16, 128], P('sub', 'dom'), may hold values from 0.1 to 10
- face_z: float32 [16, 16, 16, 128], P('sub', 'dom'), may hold values from 0.1 to 10
- masses: float32 [16, 16, 16, 128], P('sub', 'dom'), may hold values from 0.5 to 2
- active: int32 [16], P('sub'), may hold values from 8 to 16, as said below
Outputs:
- deflation: bfloat16 [16, 3, 64, 16, 16, 128], P('sub', None, None, 'dom')
- coarse_diag: float32 [16, 64, 64], P('sub')
- coarse_off: float32 [16, 64, 64], P('sub')
Inputs may be any that keep to these rules, and one draw needn't show every extreme that they name: `active`: some subdomain has all 16 planes.
All inputs are finite; a program needn't handle non-finite values.
Results may differ from a plain program's by a relative error of at most 0.001.
Values sent between devices are 32-bit elements; how exact they have to be, the bound alone decides.
No kernel may reach another device: no remote copies, remote signals or barrier semaphores. Data moves between devices by JAX's collectives and lax.ppermute only.
A program may use at most 64 MiB of HBM per device.

v0:
```python
import jax
import jax.numpy as jnp
from jax import lax
from jax.sharding import PartitionSpec as P

OV = 4
STEPS = 2


def from_behind(value, axis, steps):
    count = lax.axis_size(axis)
    leading, last = (max(0, -steps), min(count, count - steps))
    return lax.ppermute(value, axis, [(source, source + steps) for source in range(leading, last)])


def with_halo(cells, sides, width):
    for axis, dim in sides:
        count = lax.axis_size(axis)
        ends = count - 1
        head = lax.slice_in_dim(cells, 0, width, axis=dim)
        tail = lax.slice_in_dim(cells, cells.shape[dim] - width, cells.shape[dim], axis=dim)
        cells = jnp.concatenate(
            [
                lax.ppermute(tail, axis, [(i, (i + 1) % count) for i in range(ends)]),
                cells,
                lax.ppermute(head, axis, [((i + 1) % count, i) for i in range(ends)]),
            ],
            axis=dim,
        )
    return cells


def gram_of(left, right):
    return jnp.einsum("ckyxz,clyxz->kl", left, right, precision=lax.Precision.HIGHEST)


def mix_cols(values, matrix):
    return jnp.einsum("ckyxz,kl->clyxz", values, matrix, precision=lax.Precision.HIGHEST)


def inverse_factor(gram_b):
    factor = jnp.linalg.cholesky(gram_b)
    identity = jnp.eye(gram_b.shape[0], dtype=jnp.float32)
    return lax.linalg.triangular_solve(factor, identity, left_side=True, lower=True)


def face_terms(values, weights, along):
    length = values.shape[along]
    head_part = lax.slice_in_dim(values, 0, length - 1, axis=along)
    tail_part = lax.slice_in_dim(values, 1, length, axis=along)
    fluxes = lax.slice_in_dim(weights, 0, length - 1, axis=along - 2)[None, None] * (
        head_part - tail_part
    )
    pad_after = [(0, 0)] * 5
    pad_after[along] = (0, 1)
    pad_before = [(0, 0)] * 5
    pad_before[along] = (1, 0)
    return jnp.pad(fluxes, pad_after) - jnp.pad(fluxes, pad_before)


def lower_faces(weights, along):
    length = weights.shape[along]
    widths = [(0, 0)] * 3
    widths[along] = (1, 0)
    return jnp.pad(lax.slice_in_dim(weights, 0, length - 1, axis=along), widths)


def on_device(start_vectors, face_x, face_y, face_z, masses, active):
    start = start_vectors[0]
    own_x = face_x[0]
    own_y = face_y[0]
    own_z = face_z[0]
    own_mass = masses[0]
    active_now = active[0]
    rows_local = own_y.shape[0]
    planes_all = own_y.shape[1]
    depth_all = own_y.shape[2]
    rows_total = rows_local * lax.axis_size("dom")
    row_index = lax.axis_index("dom") * rows_local + jnp.arange(rows_local, dtype=jnp.int32)
    plane_index = jnp.arange(planes_all, dtype=jnp.int32)
    depth_index = jnp.arange(depth_all, dtype=jnp.int32)
    inside = (plane_index < active_now)[None, :, None]
    keep_x = (plane_index + 1 < active_now)[None, :, None]
    keep_y = inside & (row_index + 1 < rows_total)[:, None, None]
    keep_z = inside & (depth_index + 1 < depth_all)[None, None, :]
    live_x = own_x * keep_x.astype(jnp.float32)
    live_y = own_y * keep_y.astype(jnp.float32)
    live_z = own_z * keep_z.astype(jnp.float32)
    below_row = from_behind(live_y, "dom", 1)
    lower_y = jnp.concatenate([below_row, live_y[:-1]], axis=0)
    diagonal = (
        live_x
        + lower_faces(live_x, 1)
        + live_y
        + lower_y
        + live_z
        + lower_faces(live_z, 2)
        + own_mass
    )
    unity = jnp.clip(
        jnp.minimum(plane_index + 1, active_now - plane_index).astype(jnp.float32) / (OV + 1),
        0.0,
        1.0,
    )[None, :, None]
    b_weight = (own_mass * unity * unity)[None, None]

    def operate(values):
        padded = with_halo(values, (("dom", 2),), 1)
        result = live_y[None, None] * (values - padded[:, :, 2:]) + lower_y[None, None] * (
            values - padded[:, :, :-2]
        )
        return result + face_terms(values, live_x, 3) + face_terms(values, live_z, 4)

    vectors = start * inside.astype(jnp.float32)[None, None]

    def normalize(values):
        gram_b = lax.psum(gram_of(values, b_weight * values), "dom")
        return mix_cols(values, inverse_factor(gram_b).T)

    for repeat in range(STEPS):
        ortho = normalize(vectors)
        image = operate(ortho)
        rayleigh = lax.psum(gram_of(ortho, image), "dom")
        residual = image - mix_cols(b_weight * ortho, rayleigh)
        vectors = ortho - 0.5 * residual / diagonal[None, None]
    deflate = unity[None, None] * normalize(vectors)
    image = operate(deflate)
    planes = lax.dynamic_slice_in_dim(image, active_now - OV, OV, axis=3)
    neighbour = from_behind(planes, "sub", 1)
    coarse_diag, coarse_off = lax.psum(
        (gram_of(deflate, image), gram_of(deflate[:, :, :, :OV], neighbour)), "dom"
    )
    return (deflate.astype(jnp.bfloat16)[None], coarse_diag[None], coarse_off[None])


def solution(mesh):
    placed = (
        P("sub", None, None, "dom", None, None),
        P("sub", "dom", None, None),
        P("sub", "dom", None, None),
        P("sub", "dom", None, None),
        P("sub", "dom", None, None),
        P("sub"),
    )
    return jax.shard_map(
        on_device,
        mesh=mesh,
        in_specs=placed,
        out_specs=(
            P("sub", None, None, "dom", None, None),
            P("sub", None, None),
            P("sub", None, None),
        ),
        check_vma=False,
    )
```

profile of v0, /device:TPU:128, one launch (start us, length us, event | category | flops | bytes accessed | tf_op | source)
XLA Modules:
  0.0 587.5 jit_solution(13905922017482201523)
XLA Ops:
  1.3 0.8 fusion.104
  2.1 1.7 bitcast_multiply_fusion.1
  4.3 2.2 fusion.50
  6.5 74.6 %psum.49 = f32[64,64]{0,1:T(8,128)S(1)} all-reduce(f32[64,64]{0,1:T(8,128)S(1)} %fusion.50), channel_id=1, replica_groups=mesh['sub'=16,'dom'=16] {'dom'}, use_global_device_ids=true, to_apply=%region_0.1 | all-reduce | flops 4096 | bytes 32768 | tf_op jit(solution)/shard_map/psum | solution.py:117
  81.2 5.8 cholesky.59
  87.1 0.6 compare_reduce_fusion.2
  87.7 0.7 fusion.88
  88.4 4.9 custom-call.7
  93.6 1.9 fusion.32
  95.4 1.3 collective-permute-start
  96.7 5.7 collective-permute-start.2
  102.5 1.3 collective-permute-start.1
  104.8 16.0 %collective-permute-done.1 = f32[1,16,128]{2,1,0:T(8,128)S(1)} collective-permute-done((f32[1,16,128]{2,1,0:T(8,128)S(1)}, f32[1,16,128]{2,1,0:T(8,128)S(1)}, u32[]{:S(2)}, u32[]{:S(2)}) %collective-permute-start.1) | collective-permute-done | bytes 8224 | tf_op jit(solution)/shard_map/ppermute | solution.py:13
  120.9 4.1 fusion.65
  125.0 71.9 %psum.50 = f32[64,64]{0,1:T(8,128)S(1)} all-reduce(f32[64,64]{0,1:T(8,128)S(1)} %fusion.65), channel_id=1, replica_groups=mesh['sub'=16,'dom'=16] {'dom'}, use_global_device_ids=true, to_apply=%region_3.6 | all-reduce | flops 4096 | bytes 32768 | tf_op jit(solution)/shard_map/psum | solution.py:123
  196.9 6.0 %fusion.12 = f32[3,64,1,16,128]{4,1,3,0,2:T(8,128)S(1)} fusion(f32[16,128]{1,0:T(8,128)S(1)} %fusion.103, f32[16,128]{1,0:T(8,128)S(1)} %fusion.104, f32[64,64]{0,1:T(8,128)S(1)} %psum.50, f32[64,3,16,128]{3,0,2,1:T(8,128)S(1)} %fusion.32, f32[3,64,1,16,127]{4,1,3,0,2:T(8,128)} %copy-done.1, f32[3,64,1,15,128]{4,1,3,0,2:T(8,128)} %copy-done.3, ...), kind=kOutput, calls=%fused_computation.17 | convolution fusion | flops 307494912 | bytes 9375744 | tf_op jit(solution)/shard_map/ckyxz,kl->clyxz/dot_general | solution.py:38
  202.9 1.4 fusion.55
  204.4 69.5 %psum.51 = f32[64,64]{0,1:T(8,128)S(1)} all-reduce(f32[64,64]{0,1:T(8,128)S(1)} %fusion.55), channel_id=1, replica_groups=mesh['sub'=16,'dom'=16] {'dom'}, use_global_device_ids=true, to_apply=%region_4.7 | all-reduce | flops 4096 | bytes 32768 | tf_op jit(solution)/shard_map/psum | solution.py:117
  274.0 5.8 cholesky.70
  279.9 0.6 compare_reduce_fusion.1
  280.5 0.7 fusion.89
  281.2 4.9 custom-call.8
  286.4 1.5 fusion.26
  287.9 1.3 collective-permute-start.3
  289.2 4.6 collective-permute-start.4
  294.5 15.8 %collective-permute-done.3 = f32[3,64,1,16,128]{4,1,3,0,2:T(8,128)S(1)} collective-permute-done((f32[3,64,1,16,128]{4,1,3,0,2:T(8,128)S(1)}, f32[3,64,1,16,128]{4,1,3,0,2:T(8,128)S(1)}, u32[]{:S(2)}, u32[]{:S(2)}) %collective-permute-start.3) | collective-permute-done | bytes 1572896 | tf_op jit(solution)/shard_map/ppermute | solution.py:26
  310.3 1.5 collective-permute-done.4
  311.9 1.1 copy-done.7
  313.0 2.1 fusion.70
  315.1 71.9 %psum.52 = f32[64,64]{0,1:T(8,128)S(1)} all-reduce(f32[64,64]{0,1:T(8,128)S(1)} %fusion.70), channel_id=1, replica_groups=mesh['sub'=16,'dom'=16] {'dom'}, use_global_device_ids=true, to_apply=%region_5.8 | all-reduce | flops 4096 | bytes 32768 | tf_op jit(solution)/shard_map/psum | solution.py:123
  387.0 5.8 fusion.7
  392.8 1.4 fusion.60
  394.3 69.5 %psum.53 = f32[64,64]{0,1:T(8,128)S(1)} all-reduce(f32[64,64]{0,1:T(8,128)S(1)} %fusion.60), channel_id=1, replica_groups=mesh['sub'=16,'dom'=16] {'dom'}, use_global_device_ids=true, to_apply=%region_6.9 | all-reduce | flops 4096 | bytes 32768 | tf_op jit(solution)/shard_map/psum | solution.py:117
  463.9 5.8 cholesky.81
  469.8 0.6 compare_reduce_fusion
  470.4 0.7 fusion.90
  471.1 4.9 custom-call.9
  476.2 1.5 bitcast_multiply_fusion
  477.8 1.3 collective-permute-start.5
  479.1 5.7 collective-permute-start.6
  485.4 14.6 %collective-permute-done.5 = f32[3,64,1,16,128]{4,1,3,0,2:T(8,128)S(1)} collective-permute-done((f32[3,64,1,16,128]{4,1,3,0,2:T(8,128)S(1)}, f32[3,64,1,16,128]{4,1,3,0,2:T(8,128)S(1)}, u32[]{:S(2)}, u32[]{:S(2)}) %collective-permute-start.5) | collective-permute-done | bytes 1572896 | tf_op jit(solution)/shard_map/ppermute | solution.py:26
  500.1 1.5 collective-permute-done.6
  501.5 2.5 subtract_add_fusion
  504.1 1.9 collective-permute-start.7
  506.1 1.4 copy.18
  507.5 1.4 fusion.75
  508.9 5.4 collective-permute-done.7
  514.8 72.7 %all-reduce.14 = (f32[1,64,64]{2,1,0:T(8,128)}, f32[1,64,64]{2,1,0:T(8,128)}) all-reduce(f32[1,64,64]{2,1,0:T(8,128)S(1)} %fusion.75, f32[1,64,64]{2,1,0:T(8,128)S(1)} %convolution_bitcast_fusion), channel_id=1, replica_groups=mesh['sub'=16,'dom'=16] {'dom'}, use_global_device_ids=true, to_apply=%region_7.10 | all-reduce | flops 8192 | bytes 65536 | tf_op jit(solution)/shard_map/psum | solution.py:130
  (59 shorter events, 4.6 us)
Async XLA Ops:
  2.1 1.9 copy-start
  93.5 8.9 %copy-start.8 = (f32[1,1,16,128]{3,2,1,0:T(8,128)S(1)}, f32[1,1,16,128]{3,2,1,0:T(8,128)}, u32[]{:S(2)}) copy-start(f32[1,1,16,128]{3,2,1,0:T(8,128)} %param.11) | copy-start | bytes 24580
  93.5 10.3 %copy-start.10 = (f32[1,1,16,128]{3,2,1,0:T(8,128)S(1)}, f32[1,1,16,128]{3,2,1,0:T(8,128)}, u32[]{:S(2)}) copy-start(f32[1,1,16,128]{3,2,1,0:T(8,128)} %param.12) | copy-start | bytes 24580
  93.6 10.4 %copy-start.11 = (f32[1,1,16,128]{3,2,1,0:T(8,128)S(1)}, f32[1,1,16,128]{3,2,1,0:T(8,128)}, u32[]{:S(2)}) copy-start(f32[1,1,16,128]{3,2,1,0:T(8,128)} %param.10) | copy-start | bytes 24580
  95.4 25.4 %collective-permute-start = (f32[3,64,1,16,128]{4,1,3,0,2:T(8,128)S(1)}, f32[3,64,1,16,128]{4,1,3,0,2:T(8,128)S(1)}, u32[]{:S(2)}, u32[]{:S(2)}) collective-permute-start(f32[3,64,1,16,128]{4,1,3,0,2:T(8,128)S(1)} %bitcast.253), channel_id=1, source_target_pairs={{1,0},{2,1},{3,2},{4,3},{5,4},{6,5},{7,6},{8,7},{9,8},{10,9},{11,1... | collective-permute-start | bytes 4718600 | tf_op jit(solution)/shard_map/ppermute | solution.py:26
  96.7 24.1 %collective-permute-start.2 = (f32[3,64,1,16,128]{4,1,3,0,2:T(8,128)S(1)}, f32[3,64,1,16,128]{4,1,3,0,2:T(8,128)}, u32[]{:S(2)}, u32[]{:S(2)}) collective-permute-start(f32[3,64,1,16,128]{4,1,3,0,2:T(8,128)S(1)} %bitcast.254), channel_id=1, source_target_pairs={{0,1},{1,2},{2,3},{3,4},{4,5},{5,6},{6,7},{7,8},{8,9},{9,10},{10,1... | collective-permute-start | bytes 4718600 | tf_op jit(solution)/shard_map/ppermute | solution.py:24
  102.5 18.2 %collective-permute-start.1 = (f32[1,16,128]{2,1,0:T(8,128)S(1)}, f32[1,16,128]{2,1,0:T(8,128)S(1)}, u32[]{:S(2)}, u32[]{:S(2)}) collective-permute-start(f32[1,16,128]{2,1,0:T(8,128)S(1)} %bitcast_multiply_fusion.3), channel_id=1, source_target_pairs={{0,1},{1,2},{2,3},{3,4},{4,5},{5,6},{6,7},{7,8},{8,9},{9,10},{10,1... | collective-permute-start | bytes 24584 | tf_op jit(solution)/shard_map/ppermute | solution.py:13
  104.2 16.7 %copy-start.3 = (f32[3,64,1,15,128]{4,1,3,0,2:T(8,128)}, f32[3,64,1,15,128]{4,1,3,0,2:T(8,128)S(1)}, u32[]{:S(2)}) copy-start(f32[3,64,1,15,128]{4,1,3,0,2:T(8,128)S(1)} %fusion.49) | copy-start | bytes 4423684
  104.2 16.6 %copy-start.9 = (f32[1,1,16,128]{3,2,1,0:T(8,128)S(1)}, f32[1,1,16,128]{3,2,1,0:T(8,128)}, u32[]{:S(2)}) copy-start(f32[1,1,16,128]{3,2,1,0:T(8,128)} %param.13) | copy-start | bytes 24580
  104.7 16.2 %copy-start.1 = (f32[3,64,1,16,127]{4,1,3,0,2:T(8,128)}, f32[3,64,1,16,127]{4,1,3,0,2:T(8,128)S(1)}, u32[]{:S(2)}) copy-start(f32[3,64,1,16,127]{4,1,3,0,2:T(8,128)S(1)} %fusion.2) | copy-start | bytes 4681732
  120.9 4.1 copy-start.5
  287.9 22.5 %collective-permute-start.3 = (f32[3,64,1,16,128]{4,1,3,0,2:T(8,128)S(1)}, f32[3,64,1,16,128]{4,1,3,0,2:T(8,128)S(1)}, u32[]{:S(2)}, u32[]{:S(2)}) collective-permute-start(f32[3,64,1,16,128]{4,1,3,0,2:T(8,128)S(1)} %bitcast.257), channel_id=1, source_target_pairs={{1,0},{2,1},{3,2},{4,3},{5,4},{6,5},{7,6},{8,7},{9,8},{10,9},{11,1... | collective-permute-start | bytes 4718600 | tf_op jit(solution)/shard_map/ppermute | solution.py:26
  289.2 22.7 %collective-permute-start.4 = (f32[3,64,1,16,128]{4,1,3,0,2:T(8,128)S(1)}, f32[3,64,1,16,128]{4,1,3,0,2:T(8,128)S(1)}, u32[]{:S(2)}, u32[]{:S(2)}) collective-permute-start(f32[3,64,1,16,128]{4,1,3,0,2:T(8,128)S(1)} %bitcast.258), channel_id=1, source_target_pairs={{0,1},{1,2},{2,3},{3,4},{4,5},{5,6},{6,7},{7,8},{8,9},{9,10},{10,1... | collective-permute-start | bytes 4718600 | tf_op jit(solution)/shard_map/ppermute | solution.py:24
  294.0 17.9 %copy-start.4 = (f32[3,64,1,15,128]{4,1,3,0,2:T(8,128)}, f32[3,64,1,15,128]{4,1,3,0,2:T(8,128)S(1)}, u32[]{:S(2)}) copy-start(f32[3,64,1,15,128]{4,1,3,0,2:T(8,128)S(1)} %fusion.48) | copy-start | bytes 4423684
  294.5 17.4 %copy-start.2 = (f32[3,64,1,16,127]{4,1,3,0,2:T(8,128)}, f32[3,64,1,16,127]{4,1,3,0,2:T(8,128)S(1)}, u32[]{:S(2)}) copy-start(f32[3,64,1,16,127]{4,1,3,0,2:T(8,128)S(1)} %fusion.1) | copy-start | bytes 4681732
  310.3 1.5 copy-start.6
  311.9 1.1 copy-start.7
  477.8 22.3 %collective-permute-start.5 = (f32[3,64,1,16,128]{4,1,3,0,2:T(8,128)S(1)}, f32[3,64,1,16,128]{4,1,3,0,2:T(8,128)S(1)}, u32[]{:S(2)}, u32[]{:S(2)}) collective-permute-start(f32[3,64,1,16,128]{4,1,3,0,2:T(8,128)S(1)} %bitcast.248), channel_id=1, source_target_pairs={{1,0},{2,1},{3,2},{4,3},{5,4},{6,5},{7,6},{8,7},{9,8},{10,9},{11,1... | collective-permute-start | bytes 4718600 | tf_op jit(solution)/shard_map/ppermute | solution.py:26
  479.1 22.5 %collective-permute-start.6 = (f32[3,64,1,16,128]{4,1,3,0,2:T(8,128)S(1)}, f32[3,64,1,16,128]{4,1,3,0,2:T(8,128)}, u32[]{:S(2)}, u32[]{:S(2)}) collective-permute-start(f32[3,64,1,16,128]{4,1,3,0,2:T(8,128)S(1)} %bitcast.249), channel_id=1, source_target_pairs={{0,1},{1,2},{2,3},{3,4},{4,5},{5,6},{6,7},{7,8},{8,9},{9,10},{10,1... | collective-permute-start | bytes 4718600 | tf_op jit(solution)/shard_map/ppermute | solution.py:24
  504.1 10.3 %collective-permute-start.7 = (f32[3,64,1,4,128]{4,1,3,0,2:T(8,128)S(1)}, f32[3,64,1,4,128]{4,1,3,0,2:T(8,128)S(1)}, u32[]{:S(2)}, u32[]{:S(2)}) collective-permute-start(f32[3,64,1,4,128]{4,1,3,0,2:T(8,128)S(1)} %constant_dynamic-slice_fusion), channel_id=1, source_target_pairs={{0,16},{16,32},{32,48},{48,64},{64,80},{80,96},{96,112},{112,128},... | collective-permute-start | bytes 1179656 | tf_op jit(solution)/shard_map/ppermute | solution.py:13
where the time goes:
time: 588 us
  blocking collectives  430 us (73%)
  waiting for transfers between devices  54.9 us (9%)
  other arithmetic  44.1 us (8%)
  matrix products  30.6 us (5%)
  starting transfers between devices  23.1 us (4%)
    psum x3, blocking collectives, normalize(): gram_b = lax.psum(gram_of(values, b_weight * values), 'dom')  214 us
    psum x2, blocking collectives, on_device(): rayleigh = lax.psum(gram_of(ortho, image), 'dom')  144 us
    psum x1, blocking collectives, on_device(): lax.psum((gram_of(deflate, image), gram_of(deflate[:, :, :, :OV], neighbo...  72.7 us
    ppermute x3, waiting for transfers between devices, with_halo(): lax.ppermute(head, axis, [((i + 1) % count, i) for i in range(ends)])  30.5 us
    ppermute x2, waiting for transfers between devices, from_behind(): lax.ppermute(value, axis, [(source, source + steps) for source in range(l...  21.4 us
    another operation x9, other arithmetic, inverse_factor(): factor = jnp.linalg.cholesky(gram_b)  19.6 us
    dot_general x5, matrix products, mix_cols(): jnp.einsum('ckyxz,kl->clyxz', values, matrix, precision=lax.Precision.HIG...  16.7 us
    another operation x6, other arithmetic, inverse_factor(): lax.linalg.triangular_solve(factor, identity, left_side=True, lower=True)  16.6 us
  transfers between devices with their start and end apart: 8, of which 6 were waited for; matrix products, arithmetic and copies ran while one was open for 1% of the time, Pallas kernels for 0%

commit v1 on v0

v1 whole, which is shorter than its diff:
```python
import functools

import jax
import jax.numpy as jnp
from jax import lax
from jax.experimental import pallas as pl
from jax.experimental.pallas import tpu as pltpu
from jax.sharding import PartitionSpec as P

OV = 4
STEPS = 2
K = 64
NX = 16
LANES = 128
SLABS = 3 * NX
GROUPS = SLABS // 4
YROWS = GROUPS * K + NX
ZROWS = 2 * K + NX
F32 = jnp.float32
BF16 = jnp.bfloat16

VM = pl.BlockSpec(memory_space=pltpu.VMEM)
SM = pl.BlockSpec(memory_space=pltpu.SMEM)
PARAMS = pltpu.CompilerParams(vmem_limit_bytes=48 << 20)

FX, FXL, FY, FYL, FZ, FZL, DINV, BW, MASS, UN = range(10)


def f32(*shape):
    return jax.ShapeDtypeStruct(shape, F32)


def lanes(rows):
    return lax.broadcasted_iota(jnp.int32, (rows, LANES), 1)


def roll(x, shift):
    if isinstance(shift, int):
        shift = shift % LANES
        return x if shift == 0 else pltpu.roll(x, shift, 1)
    return pltpu.roll(x, shift, 1)


def unity_of(plane, active):
    value = jnp.minimum(plane + 1, active - plane).astype(F32) / (OV + 1)
    return jnp.clip(value, 0.0, 1.0)


def halves(x):
    high = x.astype(BF16)
    return high, (x - high.astype(F32)).astype(BF16)


def slab(ref, index):
    return ref[pl.ds(pl.multiple_of(index * K, K), K), :]


def put(ref, index, value):
    ref[pl.ds(pl.multiple_of(index * K, K), K), :] = value


def pack_kernel(scal, v_ref, fx, fy, fz, m, p0, p1, p2, p3):
    active, px, row = scal[0], scal[1], scal[2]
    outs_ref = (p0, p1, p2, p3)
    back = ((4 - px) & 3) * 32
    block = lanes(K) >> 5

    def body(t, carry):
        c, big = t >> 2, t & 3
        outs = [None] * 4
        for xx in range(4):
            plane = big * 4 + xx
            s = v_ref[pl.ds(c * (K * NX) + plane, K, stride=NX), :]
            s = jnp.where(plane < active, s, 0.0)
            s = roll(s, back)
            for d in range(4):
                moved = roll(s, 32 * (xx - d))
                outs[d] = moved if xx == 0 else jnp.where(block == xx, moved, outs[d])
        for d in range(4):
            put(outs_ref[d], t, outs[d])
        return carry

    lax.fori_loop(0, GROUPS, body, 0)
    plane = lax.broadcasted_iota(jnp.int32, (NX, LANES), 0)
    depth = lanes(NX)
    small = depth >> 5
    inside = plane < active
    fields = (
        jnp.where(plane + 1 < active, fx[...], 0.0),
        jnp.where(inside & (row + 1 < 16), fy[...], 0.0),
        jnp.where(inside & (depth + 1 < LANES), fz[...], 0.0),
        m[...],
    )
    for d in range(4):
        out = None
        for j in range(4):
            moved = roll(roll(fields[j], back), 32 * (j - d))
            out = moved if j == 0 else jnp.where(small == j, moved, out)
        outs_ref[d][pl.ds(GROUPS * K, NX), :] = out


def edges(t, values, y_up, y_dn, z_up, z_dn):
    lane = lanes(K)
    block = lane >> 5
    up = dn = None
    for xx in range(4):
        above = roll(values[xx], 32 * (xx - 3))
        below = roll(values[xx], 32 * xx)
        up = above if xx == 0 else jnp.where(block == xx, above, up)
        dn = below if xx == 0 else jnp.where(block == xx, below, dn)
    put(y_up, t, up)
    put(y_dn, t, dn)
    c, big = t >> 2, t & 3
    group = c >> 1
    spot = (c & 1) * NX + big * 4
    high, low = slab(z_up, group), slab(z_dn, group)
    for xx in range(4):
        here = (lane & 31) == spot + xx
        high = jnp.where(here, roll(values[xx], spot + (xx + LANES - 31)), high)
        low = jnp.where(here, roll(values[xx], spot + xx), low)
    put(z_up, group, high)
    put(z_dn, group, low)


def unpack_kernel(scal, r0, r1, r2, r3, b_ref, fields, y_up, y_dn, z_up, z_dn):
    px = scal[1]
    refs = (r0, r1, r2, r3)
    block = lanes(K) >> 5
    z_up[...] = jnp.zeros_like(z_up)
    z_dn[...] = jnp.zeros_like(z_dn)

    def body(t, carry):
        got = [slab(r, t) for r in refs]
        values = []
        for xx in range(4):
            out = None
            for d in range(4):
                moved = roll(got[d], 32 * (-d - xx))
                out = moved if d == 0 else jnp.where(block == (-d) % 4, moved, out)
            out = roll(out, px * 32)
            values.append(out)
            put(b_ref, t * 4 + xx, out)
        edges(t, values, y_up, y_dn, z_up, z_dn)
        return carry

    lax.fori_loop(0, GROUPS, body, 0)
    small = lanes(NX) >> 5
    got = [r[pl.ds(GROUPS * K, NX), :] for r in refs]
    done = []
    for j in range(4):
        out = None
        for d in range(4):
            moved = roll(got[d], 32 * (-d - j))
            out = moved if d == 0 else jnp.where(small == (-d) % 4, moved, out)
        out = roll(out, px * 32)
        done.append(out)
        fields[pl.ds(j * NX, NX), :] = out
    y_up[pl.ds(GROUPS * K, NX), :] = roll(done[1], 32)
    y_dn[pl.ds(GROUPS * K, NX), :] = jnp.zeros((NX, LANES), F32)
    z_up[pl.ds(2 * K, NX), :] = roll(done[2], -31)


def line(fld, which, plane):
    return fld[pl.ds(which * NX + plane, 1), :]


def stencil(t, xx, v_ref, fld, h_up, h_dn, h_zp, h_zm):
    c, big = t >> 2, t & 3
    plane = big * 4 + xx
    at = t * 4 + xx
    lane = lanes(K)
    v = slab(v_ref, at)
    spot = (c & 1) * NX + plane
    group = c >> 1
    up = jnp.where(lane >= 96, roll(slab(h_up, t), 32 * (3 - xx)), roll(v, -32))
    dn = jnp.where(lane < 32, roll(slab(h_dn, t), -32 * xx), roll(v, 32))
    part = lane & 31
    zp = jnp.where(part == 31, roll(slab(h_zp, group), 31 - spot), roll(v, -1))
    zm = jnp.where(part == 0, roll(slab(h_zm, group), LANES - spot), roll(v, 1))
    lo = jnp.maximum(at - 1, 0)
    hi = jnp.minimum(at + 1, SLABS - 1)
    out = line(fld, FY, plane) * (v - up) + line(fld, FYL, plane) * (v - dn)
    out += line(fld, FX, plane) * (v - slab(v_ref, hi)) + line(fld, FXL, plane) * (v - slab(v_ref, lo))
    out += line(fld, FZ, plane) * (v - zp) + line(fld, FZL, plane) * (v - zm)
    return v, out


def add_gram(acc, lefts, mids, rights):
    for pair in (0, 2):
        left, right = [], []
        for xx in (pair, pair + 1):
            left.append(jnp.concatenate(halves(lefts[xx]), axis=0))
            right.append(jnp.concatenate(halves(mids[xx]) + halves(rights[xx]), axis=0))
        acc[...] += lax.dot_general(
            jnp.concatenate(left, axis=1),
            jnp.concatenate(right, axis=1),
            (((1,), (1,)), ((), ())),
            preferred_element_type=F32,
        )


def finish_gram(acc, out):
    half = acc[0:K, :] + acc[K : 2 * K, :]
    out[0:K, :] = half[:, 0:K] + half[:, K : 2 * K]
    out[K : 2 * K, :] = half[:, 2 * K : 3 * K] + half[:, 3 * K : 4 * K]


def edge_fields(fld, y_up, y_dn, z_up, z_dn):
    dinv = fld[DINV * NX : DINV * NX + NX, :]
    weight = fld[BW * NX : BW * NX + NX, :]
    lane = lanes(NX)
    y_up[pl.ds(GROUPS * K, NX), :] = jnp.where(lane < 32, roll(dinv, 32), roll(weight, 64))
    y_dn[pl.ds(GROUPS * K, NX), :] = jnp.where(lane < 32, dinv, roll(weight, 32))
    z_up[pl.ds(2 * K, NX), :] = jnp.where((lane & 31) == 0, roll(dinv, -31), roll(weight, -30))
    z_dn[pl.ds(2 * K, NX), :] = jnp.where((lane & 31) == 0, dinv, roll(weight, 1))


def first_kernel(scal, v_ref, raw, h_up, h_dn, h_zp, h_zm, av_ref, fld, grams, y_up, y_dn, z_up, z_dn, acc):
    active = scal[0]
    lane = lanes(NX)
    plane = lax.broadcasted_iota(jnp.int32, (NX, LANES), 0)
    fx, fy, fz, m = (raw[j * NX : (j + 1) * NX, :] for j in range(4))
    fxl = jnp.where(plane == 0, 0.0, pltpu.roll(fx, 1, 0))
    fyl = jnp.where(lane < 32, h_dn[GROUPS * K : GROUPS * K + NX, :], roll(fy, 32))
    fzl = jnp.where((lane & 31) == 0, h_zm[2 * K : 2 * K + NX, :], roll(fz, 1))
    dinv = 1.0 / (fx + fxl + fy + fyl + fz + fzl + m)
    u = unity_of(plane, active)
    for j, value in enumerate((fx, fxl, fy, fyl, fz, fzl, dinv, m * u * u, m, u)):
        fld[j * NX : (j + 1) * NX, :] = value
    z_up[...] = jnp.zeros_like(z_up)
    z_dn[...] = jnp.zeros_like(z_dn)
    acc[...] = jnp.zeros_like(acc)

    def body(t, carry):
        vs, bs, avs = [], [], []
        for xx in range(4):
            v, av = stencil(t, xx, v_ref, fld, h_up, h_dn, h_zp, h_zm)
            put(av_ref, t * 4 + xx, av)
            vs.append(v)
            avs.append(av)
            bs.append(v * line(fld, BW, (t & 3) * 4 + xx))
        edges(t, avs, y_up, y_dn, z_up, z_dn)
        add_gram(acc, vs, bs, avs)
        return carry

    lax.fori_loop(0, GROUPS, body, 0)
    edge_fields(fld, y_up, y_dn, z_up, z_dn)
    finish_gram(acc, grams)


def mixed(matrix, v, av, dinv, weight):
    y = v - 0.5 * (av * dinv)
    w = v * (weight * dinv)
    both = lax.dot_general(
        matrix,
        jnp.concatenate(halves(y) + halves(w), axis=0),
        (((1,), (0,)), ((), ())),
        preferred_element_type=F32,
    )
    return both[0:K, :] + both[K : 2 * K, :]


def step_kernel(last, scal, *refs):
    ins, refs = refs[:12], refs[12:]
    v_ref, av_ref, fld, mat = ins[:4]
    hv, ha = ins[4:8], ins[8:12]
    hf, refs = refs[:4], refs[4:]
    if last:
        w_ref, img_ref, grams, p0, p1, p2, p3, acc, rows_y, rows_z, n_up, n_dn, n_zp, n_zm = refs
        new_ref = w_ref
    else:
        new_ref, out_ref, grams, n_up, n_dn, n_zp, n_zm, y_up, y_dn, z_up, z_dn, acc, rows_y, rows_z = refs
    active, px = scal[0], scal[1]
    matrix = mat[...]
    one = lanes(1)
    for side in range(2):
        for big in range(4):
            for which in range(2):
                out = None
                for xx in range(4):
                    at = GROUPS * K + big * 4 + xx
                    moved = roll(hf[side][at : at + 1, :], 32 * (xx - which))
                    out = moved if xx == 0 else jnp.where((one >> 5) == xx, moved, out)
                at = (side * 4 + big) * 2 + which
                rows_y[at : at + 1, :] = out
        for which in range(2):
            out = None
            for e in range(2 * NX):
                at = 2 * K + e % NX
                moved = roll(hf[2 + side][at : at + 1, :], e - which)
                out = moved if e == 0 else jnp.where((one & 31) == e, moved, out)
            at = side * 2 + which
            rows_z[at : at + 1, :] = out
    acc[...] = jnp.zeros_like(acc)

    def new_own(t, carry):
        for xx in range(4):
            plane = (t & 3) * 4 + xx
            at = t * 4 + xx
            value = mixed(matrix, slab(v_ref, at), slab(av_ref, at), line(fld, DINV, plane), line(fld, BW, plane))
            if last:
                value = value * line(fld, UN, plane)
            put(new_ref, at, value)
        return carry

    lax.fori_loop(0, GROUPS, new_own, 0)
    block = lanes(1) >> 5

    def new_side(t, carry):
        big = t & 3
        for side, target in ((0, n_up), (1, n_dn)):
            at = (side * 4 + big) * 2
            value = mixed(
                matrix, slab(hv[side], t), slab(ha[side], t), rows_y[pl.ds(at, 1), :], rows_y[pl.ds(at + 1, 1), :]
            )
            if last:
                value = value * unity_of(big * 4 + block, active)
            put(target, t, value)
        return carry

    lax.fori_loop(0, GROUPS, new_side, 0)
    for side, target in ((0, n_zp), (1, n_zm)):
        for group in range(2):
            at = side * 2
            value = mixed(
                matrix,
                slab(hv[2 + side], group),
                slab(ha[2 + side], group),
                rows_z[at : at + 1, :],
                rows_z[at + 1 : at + 2, :],
            )
            if last:
                value = value * unity_of(one & 15, active)
            put(target, group, value)

    if not last:
        z_up[...] = jnp.zeros_like(z_up)
        z_dn[...] = jnp.zeros_like(z_dn)
    outs_ref = (p0, p1, p2, p3) if last else ()
    back = ((4 - px) & 3) * 32
    wide = lanes(K) >> 5

    def body(t, carry):
        vs, bs, avs = [], [], []
        for xx in range(4):
            plane = (t & 3) * 4 + xx
            v, av = stencil(t, xx, new_ref, fld, n_up, n_dn, n_zp, n_zm)
            vs.append(v)
            avs.append(av)
            bs.append(v * line(fld, MASS if last else BW, plane))
            if not last:
                put(out_ref, t * 4 + xx, av)
            else:
                place = plane - (active - OV)

                @pl.when((place >= 0) & (place < OV))
                def _():
                    put(img_ref, (t >> 2) * OV + place, av)

        if last:
            outs = [None] * 4
            for xx in range(4):
                s = roll(vs[xx], back)
                for d in range(4):
                    moved = roll(s, 32 * (xx - d))
                    outs[d] = moved if xx == 0 else jnp.where(wide == xx, moved, outs[d])
            for d in range(4):
                put(outs_ref[d], t, outs[d])
        else:
            edges(t, avs, y_up, y_dn, z_up, z_dn)
        add_gram(acc, vs, bs, avs)
        return carry

    lax.fori_loop(0, GROUPS, body, 0)
    finish_gram(acc, grams)


def small_dot(a, b, dims=((1,), (0,))):
    return lax.dot_general(a, b, (dims, ((), ())), precision=lax.Precision.HIGHEST, preferred_element_type=F32)


def inverse_factor(gram):
    row = lax.broadcasted_iota(jnp.int32, (8, LANES), 0)
    lane = lanes(8)
    parts = []
    for g in range(8):
        left = jnp.concatenate([gram[g * 8 : g * 8 + 8, :], jnp.zeros((8, K), F32)], axis=1)
        parts.append(jnp.where(lane == row + (g * 8 + K), 1.0, left))
    pivots = [None] * 8
    for j in range(K):
        g0, s0 = j // 8, j % 8
        pivot_row = jnp.broadcast_to(parts[g0][s0 : s0 + 1, :], (8, LANES))
        pivot = jnp.broadcast_to(pivot_row[:, j : j + 1], (8, LANES))
        scaled = pivot_row * (1.0 / pivot)
        pivots[g0] = pivot if s0 == 0 else jnp.where(row == s0, pivot, pivots[g0])
        for g in range(g0, 8):
            column = jnp.broadcast_to(parts[g][:, j : j + 1], (8, LANES))
            if g == g0:
                column = jnp.where(row > s0, column, 0.0)
            parts[g] = parts[g] - column * scaled
    return jnp.concatenate([(parts[g] * lax.rsqrt(pivots[g]))[:, K:] for g in range(8)], axis=0)


def matrix_kernel(grams, mat):
    factor = inverse_factor(grams[0:K, :])
    image = small_dot(factor, grams[K : 2 * K, :])
    rayleigh = small_dot(image, factor, ((1,), (1,)))
    other = 0.5 * small_dot(rayleigh, factor, ((0,), (0,)))
    fh, fl = halves(factor)
    oh, ol = halves(other)
    mat[...] = jnp.concatenate(
        [jnp.concatenate([fh, fh, oh, oh], axis=1), jnp.concatenate([fl, fl, ol, ol], axis=1)], axis=0
    )


def factor_kernel(grams, factor_ref, diag_ref):
    factor = inverse_factor(grams[0:K, :])
    factor_ref[...] = factor
    image = small_dot(factor, grams[K : 2 * K, :])
    diag_ref[...] = small_dot(image, factor, ((1,), (1,)))


def cross_kernel(factor, other, raw, out):
    out[...] = small_dot(small_dot(factor[...], raw[...]), other[...], ((1,), (1,)))


def off_kernel(w_ref, img_ref, out):
    acc = jnp.zeros((2 * K, 2 * K), F32)
    for c in range(3):
        for pair in (0, 2):
            left, right = [], []
            for j in (pair, pair + 1):
                left.append(jnp.concatenate(halves(slab(w_ref, c * NX + j)), axis=0))
                right.append(jnp.concatenate(halves(slab(img_ref, c * OV + j)), axis=0))
            acc += lax.dot_general(
                jnp.concatenate(left, axis=1),
                jnp.concatenate(right, axis=1),
                (((1,), (1,)), ((), ())),
                preferred_element_type=F32,
            )
    half = acc[0:K, :] + acc[K : 2 * K, :]
    out[...] = half[:, 0:K] + half[:, K : 2 * K]


def out_kernel(scal, factor, r0, r1, r2, r3, out_ref, hold):
    px = scal[1]
    refs = (r0, r1, r2, r3)
    block = lanes(K) >> 5
    fh, fl = halves(factor[...])
    matrix = jnp.concatenate([jnp.concatenate([fh, fh], axis=1), jnp.concatenate([fl, fl], axis=1)], axis=0)

    def body(t, carry):
        c, big = t >> 2, t & 3
        got = [slab(r, t) for r in refs]
        for xx in range(4):
            out = None
            for d in range(4):
                moved = roll(got[d], 32 * (-d - xx))
                out = moved if d == 0 else jnp.where(block == (-d) % 4, moved, out)
            out = roll(out, px * 32)
            both = lax.dot_general(
                matrix, jnp.concatenate(halves(out), axis=0), (((1,), (0,)), ((), ())), preferred_element_type=F32
            )
            hold[pl.ds(c * (K * NX) + big * 4 + xx, K, stride=NX), :] = both[0:K, :] + both[K : 2 * K, :]
        return carry

    lax.fori_loop(0, GROUPS, body, 0)

    def cast(i, carry):
        at = pl.ds(pl.multiple_of(i * 128, 128), 128)
        out_ref[at, :] = hold[at, :].astype(BF16)
        return carry

    lax.fori_loop(0, 3 * K * NX // 128, cast, 0)


def call(kernel, n_in, shapes, scratch=(), first=VM, name=None):
    return pl.pallas_call(
        kernel,
        out_shape=shapes,
        in_specs=[first] + [VM] * (n_in - 1),
        out_specs=jax.tree.map(lambda _: VM, shapes),
        scratch_shapes=list(scratch),
        compiler_params=PARAMS,
        name=name,
    )


def shift_x(value, d):
    return lax.ppermute(value, "dom", [(i, (i & 12) + ((i + d) & 3)) for i in range(16)])


def halo(y_up, y_dn, z_up, z_dn):
    h_dn = lax.ppermute(y_up, "dom", [(i, i + 4) for i in range(12)])
    h_up = lax.ppermute(y_dn, "dom", [(i + 4, i) for i in range(12)])
    h_zm = lax.ppermute(z_up, "dom", [(i, i + 1) for i in range(16) if i & 3 < 3])
    h_zp = lax.ppermute(z_dn, "dom", [(i + 1, i) for i in range(16) if i & 3 < 3])
    return h_up, h_dn, h_zp, h_zm


def total(value):
    for near in ((1, 0, 3, 2), (3, 2, 1, 0)):
        value = value + lax.ppermute(value, "dom", [(i, (i & 12) + near[i & 3]) for i in range(16)])
    for near in ((1, 0, 3, 2), (3, 2, 1, 0)):
        value = value + lax.ppermute(value, "dom", [(i, near[i >> 2] * 4 + (i & 3)) for i in range(16)])
    return value


def on_device(start_vectors, face_x, face_y, face_z, masses, active):
    row = lax.axis_index("dom").astype(jnp.int32)
    scal = jnp.stack([active[0], row & 3, row]).astype(jnp.int32)
    start = start_vectors.reshape(3 * K * NX, LANES)
    fields = [f.reshape(NX, LANES) for f in (face_x, face_y, face_z, masses)]
    msg = f32(YROWS, LANES)
    zmsg = f32(ZROWS, LANES)
    whole = f32(SLABS * K, LANES)
    gram2 = f32(2 * K, K)
    rows4 = (msg,) * 4
    side4 = (msg, msg, zmsg, zmsg)
    packed = call(pack_kernel, 6, rows4, first=SM, name="pack")(scal, start, *fields)
    got = [packed[0]] + [shift_x(packed[d], d) for d in (1, 2, 3)]
    v, raw, *side = call(unpack_kernel, 5, (whole, f32(4 * NX, LANES)) + side4, first=SM, name="unpack")(scal, *got)
    hv = halo(*side)
    acc = pltpu.VMEM((2 * K, 4 * K), F32)
    av, fld, grams, *side = call(
        first_kernel, 7, (whole, f32(10 * NX, LANES), gram2) + side4, (acc,), first=SM, name="first"
    )(scal, v, raw, *hv)
    ha = halo(*side)
    hf = ha
    mat_shape = jax.ShapeDtypeStruct((2 * K, 4 * K), BF16)
    rows = (pltpu.VMEM((16, LANES), F32), pltpu.VMEM((8, LANES), F32))
    for repeat in range(STEPS):
        mat = call(matrix_kernel, 1, mat_shape, name="matrix")(total(grams))
        ops = (scal, v, av, fld, mat, *hv, *ha, *hf)
        if repeat + 1 < STEPS:
            v, av, grams, *rest = call(
                functools.partial(step_kernel, False),
                17,
                (whole, whole, gram2) + side4 + side4,
                (acc,) + rows,
                first=SM,
                name="step",
            )(*ops)
            hv = tuple(rest[:4])
            ha = halo(*rest[4:])
        else:
            w, img, grams, *packed = call(
                functools.partial(step_kernel, True),
                17,
                (whole, f32(3 * OV * K, LANES), gram2) + rows4,
                (acc,) + rows + (pltpu.VMEM((YROWS, LANES), F32),) * 2 + (pltpu.VMEM((ZROWS, LANES), F32),) * 2,
                first=SM,
                name="last",
            )(*ops)
    got = [packed[0]] + [shift_x(packed[d], d) for d in (1, 2, 3)]
    behind = [(i, i + 1) for i in range(15)]
    before = lax.ppermute(img, "sub", behind)
    raw_off = call(off_kernel, 2, f32(K, K), name="off")(w, before)
    factor, diag = call(factor_kernel, 1, (f32(K, K), f32(K, K)), name="factor")(total(grams))
    off = call(cross_kernel, 3, f32(K, K), name="cross")(factor, lax.ppermute(factor, "sub", behind), total(raw_off))
    out = call(
        out_kernel,
        6,
        jax.ShapeDtypeStruct((3 * K * NX, LANES), BF16),
        (pltpu.VMEM((3 * K * NX, LANES), F32),),
        first=SM,
        name="rows",
    )(scal, factor, *got)
    return (out.reshape(1, 3, K, 1, NX, LANES), diag[None], off[None])


def solution(mesh):
    placed = (
        P("sub", None, None, "dom", None, None),
        P("sub", "dom", None, None),
        P("sub", "dom", None, None),
        P("sub", "dom", None, None),
        P("sub", "dom", None, None),
        P("sub"),
    )
    return jax.shard_map(
        on_device,
        mesh=mesh,
        in_specs=placed,
        out_specs=(
            P("sub", None, None, "dom", None, None),
            P("sub", None, None),
            P("sub", None, None),
        ),
        check_vma=False,
    )
```

time: 588 us -> 237 us (0.40)
  blocking collectives: 430 us -> 0 us
  Pallas kernels: 0 us -> 86.2 us
  other arithmetic: 44.1 us -> 0.21 us
  starting transfers between devices: 23.1 us -> 65.4 us
  matrix products: 30.6 us -> 0 us
  waiting for transfers between devices: 54.9 us -> 71.7 us
    psum x6 -> x0, blocking collectives: 430 us -> none  [the longest x3 214 us: normalize(): gram_b = lax.psum(gram_of(values, b_weight * values), 'dom')]
    pallas_call x0 -> x11, Pallas kernels: none -> 86.2 us  [the longest x1 18.8 us: on_device(): call(functools.partial(step_kernel, True), 17, (whole, f32(3 * OV * K, LA...]
    ppermute x8 -> x36, starting transfers between devices: 23.1 us -> 65.4 us  [the longest x3 13.7 us: halo(): h_dn = lax.ppermute(y_up, 'dom', [(i, i + 4) for i in range(12)])]
    another operation x15 -> x1, other arithmetic: 36.2 us -> 0.08 us  [on_device(): scal = jnp.stack([active[0], row & 3, row]).astype(jnp.int32)]
    dot_general x12 -> x0, matrix products: 29.8 us -> none  [the longest x5 16.7 us: mix_cols(): jnp.einsum('ckyxz,kl->clyxz', values, matrix, precision=lax.Precision.HIG...]
    ppermute x8 -> x36, waiting for transfers between devices: 54.9 us -> 71.7 us  [the longest x8 36.5 us: total(): lax.ppermute(value, 'dom', [(i, (i & 12) + near[i & 3]) for i in range(16)])]
  transfers between devices with their start and end apart: 8 -> 36, of which waited for: 6 -> 15; matrix products, arithmetic and copies ran while one was open for 1% -> 0% of each run, Pallas kernels for 0% -> 15%
where the time goes in v1:
time: 237 us; the launch traced here: 233 us
  Pallas kernels  86.2 us (36%)
  waiting for transfers between devices  71.7 us (30%)
  starting transfers between devices  65.4 us (28%)
  local copies, waits for them, and re-layouts  7.9 us (3%)
    ppermute x8, waiting for transfers between devices, total(): lax.ppermute(value, 'dom', [(i, (i & 12) + near[i & 3]) for i in range(16)])  36.5 us
    pallas_call x1, Pallas kernels, on_device(): call(functools.partial(step_kernel, True), 17, (whole, f32(3 * OV * K, LA...  18.8 us
    pallas_call x2, Pallas kernels, on_device(): mat = call(matrix_kernel, 1, mat_shape, name='matrix')(total(grams))  18.2 us
    ppermute x8, waiting for transfers between devices, total(): lax.ppermute(value, 'dom', [(i, near[i >> 2] * 4 + (i & 3)) for i in rang...  17 us
    ppermute x6, waiting for transfers between devices, shift_x(): lax.ppermute(value, 'dom', [(i, (i & 12) + (i + d & 3)) for i in range(16)])  16.2 us
    pallas_call x1, Pallas kernels, on_device(): call(functools.partial(step_kernel, False), 17, (whole, whole, gram2) + s...  14.5 us
    ppermute x3, starting transfers between devices, halo(): h_dn = lax.ppermute(y_up, 'dom', [(i, i + 4) for i in range(12)])  13.7 us
    ppermute x3, starting transfers between devices, halo(): lax.ppermute(z_up, 'dom', [(i, i + 1) for i in range(16) if i & 3 < 3])  13.7 us
  transfers between devices with their start and end apart: 36, of which 15 were waited for; matrix products, arithmetic and copies ran while one was open for 0% of the time, Pallas kernels for 15%

profile of v1, /device:TPU:128, one launch (start us, length us, event | category | flops | bytes accessed | tf_op | source)
XLA Modules:
  0.0 233.1 jit_solution(13269354583529133068)
XLA Ops:
  1.4 1.4 copy-done.1
  5.6 4.1 %pack.1 = (f32[784,128]{1,0:T(8,128)S(1)}, f32[784,128]{1,0:T(8,128)S(1)}, f32[784,128]{1,0:T(8,128)S(1)}, f32[784,128]{1,0:T(8,128)S(1)}) custom-call(s32[3]{0:T(128)S(1)} %pad_add_fusion.scal, f32[3072,128]{1,0:T(8,128)S(1)} %bitcast.12, f32[16,128]{1,0:T(8,128)S(1)} %bitcast.13, f32[16,128]{1,0:T(8,128)S(1)} %bitcast.14, f32[16,128]{1,0:T(8,128)S(1)} %bitcast.15, ...), custom_call_target="tpu_custom_call" | custom-call | tf_op jit(solution)/shard_map/pack/pallas_call | solution.py:520
  9.7 1.6 collective-permute-start
  11.3 2.7 %collective-permute-start.1 = (f32[784,128]{1,0:T(8,128)S(1)}, f32[784,128]{1,0:T(8,128)S(1)}, u32[]{:S(2)}, u32[]{:S(2)}) collective-permute-start(f32[784,128]{1,0:T(8,128)S(1)} %get-tuple-element.42), channel_id=1, source_target_pairs={{0,2},{1,3},{2,0},{3,1},{4,6},{5,7},{6,4},{7,5},{8,10},{9,11},{10,... | collective-permute-start | bytes 1204232 | tf_op jit(solution)/shard_map/ppermute | solution.py:490
  14.0 1.4 collective-permute-start.2
  15.4 6.7 %collective-permute-done.r1 = f32[784,128]{1,0:T(8,128)S(1)} collective-permute-done((f32[784,128]{1,0:T(8,128)S(1)}, f32[784,128]{1,0:T(8,128)S(1)}, u32[]{:S(2)}, u32[]{:S(2)}) %collective-permute-start) | collective-permute-done | bytes 401440 | tf_op jit(solution)/shard_map/ppermute | solution.py:490
  22.2 9.4 %collective-permute-done.1.r2 = f32[784,128]{1,0:T(8,128)S(1)} collective-permute-done((f32[784,128]{1,0:T(8,128)S(1)}, f32[784,128]{1,0:T(8,128)S(1)}, u32[]{:S(2)}, u32[]{:S(2)}) %collective-permute-start.1) | collective-permute-done | bytes 401440 | tf_op jit(solution)/shard_map/ppermute | solution.py:490
  31.6 6.8 %unpack.1 = (f32[3072,128]{1,0:T(8,128)S(1)}, f32[64,128]{1,0:T(8,128)S(1)}, f32[784,128]{1,0:T(8,128)S(1)}, f32[784,128]{1,0:T(8,128)S(1)}, f32[144,128]{1,0:T(8,128)S(1)}, /*index=5*/f32[144,128]{1,0:T(8,128)S(1)}) custom-call(s32[3]{0:T(128)S(1)} %pad_add_fusion.scal, f32[784,128]{1,0:T(8,128)S(1)} %get-tuple-element.40.r0, ...), custom_call_target="tpu_custom_call" | custom-call | tf_op jit(solution)/shard_map/unpack/pallas_call | solution.py:522
  38.4 1.3 collective-permute-start.3
  39.7 4.6 %collective-permute-start.4 = (f32[784,128]{1,0:T(8,128)S(1)}, f32[784,128]{1,0:T(8,128)S(1)}, u32[]{:S(2)}, u32[]{:S(2)}) collective-permute-start(f32[784,128]{1,0:T(8,128)S(1)} %get-tuple-element.47), channel_id=1, source_target_pairs={{0,4},{1,5},{2,6},{3,7},{4,8},{5,9},{6,10},{7,11},{8,12},{9,13},{1... | collective-permute-start | bytes 1204232 | tf_op jit(solution)/shard_map/ppermute | solution.py:494
  44.2 1.3 collective-permute-start.5
  45.5 4.5 %collective-permute-start.6 = (f32[144,128]{1,0:T(8,128)S(1)}, f32[144,128]{1,0:T(8,128)S(1)}, u32[]{:S(2)}, u32[]{:S(2)}) collective-permute-start(f32[144,128]{1,0:T(8,128)S(1)} %get-tuple-element.49), channel_id=1, source_target_pairs={{0,1},{1,2},{2,3},{4,5},{5,6},{6,7},{8,9},{9,10},{10,11},{12,13},{... | collective-permute-start | bytes 221192 | tf_op jit(solution)/shard_map/ppermute | solution.py:496
  50.5 1.6 collective-permute-done.6.h_zm.refs_7_
  52.1 6.8 %first.1 = (f32[3072,128]{1,0:T(8,128)S(1)}, f32[160,128]{1,0:T(8,128)S(1)}, f32[128,64]{1,0:T(8,128)S(1)}, f32[784,128]{1,0:T(8,128)S(1)}, f32[784,128]{1,0:T(8...) custom-call(s32[3]{0:T(128)S(1)} %pad_add_fusion.scal, f32[3072,128]{1,0:T(8,128)S(1)} %get-tuple-element.44.v_ref.refs_0_, ...), custom_call_target="tpu_custom_call" | custom-call | tf_op jit(solution)/shard_map/first/pallas_call | solution.py:525
  60.0 1.3 collective-permute-start.11
  61.3 4.6 %collective-permute-start.12 = (f32[784,128]{1,0:T(8,128)S(1)}, f32[784,128]{1,0:T(8,128)S(1)}, u32[]{:S(2)}, u32[]{:S(2)}) collective-permute-start(f32[784,128]{1,0:T(8,128)S(1)} %get-tuple-element.54), channel_id=1, source_target_pairs={{0,4},{1,5},{2,6},{3,7},{4,8},{5,9},{6,10},{7,11},{8,12},{9,13},{1... | collective-permute-start | bytes 1204232 | tf_op jit(solution)/shard_map/ppermute | solution.py:494
  65.9 2.4 %collective-permute-start.7 = (f32[128,64]{1,0:T(8,128)S(1)}, f32[128,64]{1,0:T(8,128)S(1)}, u32[]{:S(2)}, u32[]{:S(2)}) collective-permute-start(f32[128,64]{1,0:T(8,128)S(1)} %get-tuple-element.52), channel_id=1, source_target_pairs={{0,1},{1,0},{2,3},{3,2},{4,5},{5,4},{6,7},{7,6},{8,9},{9,8},{10,11... | collective-permute-start | bytes 98312 | tf_op jit(solution)/shard_map/ppermute | solution.py:503
  68.4 2.2 collective-permute-done.7
  70.6 3.3 %collective-permute-start.8 = (f32[128,64]{1,0:T(8,128)S(1)}, f32[128,64]{1,0:T(8,128)S(1)}, u32[]{:S(2)}, u32[]{:S(2)}) collective-permute-start(f32[128,64]{1,0:T(8,128)S(1)} %add.48), channel_id=1, source_target_pairs={{0,3},{1,2},{2,1},{3,0},{4,7},{5,6},{6,5},{7,4},{8,11},{9,10},{10,... | collective-permute-start | bytes 98312 | tf_op jit(solution)/shard_map/ppermute | solution.py:503
  73.9 1.3 collective-permute-start.13
  75.2 4.5 %collective-permute-start.14 = (f32[144,128]{1,0:T(8,128)S(1)}, f32[144,128]{1,0:T(8,128)S(1)}, u32[]{:S(2)}, u32[]{:S(2)}) collective-permute-start(f32[144,128]{1,0:T(8,128)S(1)} %get-tuple-element.56), channel_id=1, source_target_pairs={{0,1},{1,2},{2,3},{4,5},{5,6},{6,7},{8,9},{9,10},{10,11},{12,13},{... | collective-permute-start | bytes 221192 | tf_op jit(solution)/shard_map/ppermute | solution.py:496
  79.8 1.8 collective-permute-start.9
  81.6 2.5 %collective-permute-done.9 = f32[128,64]{1,0:T(8,128)S(1)} collective-permute-done((f32[128,64]{1,0:T(8,128)S(1)}, f32[128,64]{1,0:T(8,128)S(1)}, u32[]{:S(2)}, u32[]{:S(2)}) %collective-permute-start.9) | collective-permute-done | bytes 32800 | tf_op jit(solution)/shard_map/ppermute | solution.py:505
  84.2 2.0 collective-permute-start.10
  86.2 3.6 %collective-permute-done.10 = f32[128,64]{1,0:T(8,128)S(1)} collective-permute-done((f32[128,64]{1,0:T(8,128)S(1)}, f32[128,64]{1,0:T(8,128)S(1)}, u32[]{:S(2)}, u32[]{:S(2)}) %collective-permute-start.10) | collective-permute-done | bytes 32800 | tf_op jit(solution)/shard_map/ppermute | solution.py:505
  89.8 9.1 %matrix.2.refs_3_ = bf16[128,256]{1,0:T(8,128)(2,1)S(1)} custom-call(f32[128,64]{1,0:T(8,128)S(1)} %add.51.grams), custom_call_target="tpu_custom_call" | custom-call | tf_op jit(solution)/shard_map/matrix/pallas_call | solution.py:533
  98.9 14.5 %step.1 = (f32[3072,128]{1,0:T(8,128)S(1)}, f32[3072,128]{1,0:T(8,128)}, f32[128,64]{1,0:T(8,128)S(1)}, f32[784,128]{1,0:T(8,128)S(1)}, f32[784,128]{1,0:T(8,128...) custom-call(s32[3]{0:T(128)S(1)} %pad_add_fusion.scal, ...), custom_call_target="tpu_custom_call" | custom-call | tf_op jit(solution)/shard_map/step/pallas_call | solution.py:536
  114.5 1.3 collective-permute-start.19
  115.8 4.6 %collective-permute-start.20 = (f32[784,128]{1,0:T(8,128)S(1)}, f32[784,128]{1,0:T(8,128)S(1)}, u32[]{:S(2)}, u32[]{:S(2)}) collective-permute-start(f32[784,128]{1,0:T(8,128)S(1)} %get-tuple-element.65), channel_id=1, source_target_pairs={{0,4},{1,5},{2,6},{3,7},{4,8},{5,9},{6,10},{7,11},{8,12},{9,13},{1... | collective-permute-start | bytes 1204232 | tf_op jit(solution)/shard_map/ppermute | solution.py:494
  120.6 4.1 %collective-permute-done.15 = f32[128,64]{1,0:T(8,128)S(1)} collective-permute-done((f32[128,64]{1,0:T(8,128)S(1)}, f32[128,64]{1,0:T(8,128)S(1)}, u32[]{:S(2)}, u32[]{:S(2)}) %collective-permute-start.15) | collective-permute-done | bytes 32800 | tf_op jit(solution)/shard_map/ppermute | solution.py:503
  124.9 1.3 collective-permute-start.21
  126.2 4.5 %collective-permute-start.22 = (f32[144,128]{1,0:T(8,128)S(1)}, f32[144,128]{1,0:T(8,128)S(1)}, u32[]{:S(2)}, u32[]{:S(2)}) collective-permute-start(f32[144,128]{1,0:T(8,128)S(1)} %get-tuple-element.67), channel_id=1, source_target_pairs={{0,1},{1,2},{2,3},{4,5},{5,6},{6,7},{8,9},{9,10},{10,11},{12,13},{... | collective-permute-start | bytes 221192 | tf_op jit(solution)/shard_map/ppermute | solution.py:496
  131.3 3.8 %collective-permute-done.17 = f32[128,64]{1,0:T(8,128)S(1)} collective-permute-done((f32[128,64]{1,0:T(8,128)S(1)}, f32[128,64]{1,0:T(8,128)S(1)}, u32[]{:S(2)}, u32[]{:S(2)}) %collective-permute-start.17) | collective-permute-done | bytes 32800 | tf_op jit(solution)/shard_map/ppermute | solution.py:505
  136.1 4.8 %collective-permute-done.18 = f32[128,64]{1,0:T(8,128)S(1)} collective-permute-done((f32[128,64]{1,0:T(8,128)S(1)}, f32[128,64]{1,0:T(8,128)S(1)}, u32[]{:S(2)}, u32[]{:S(2)}) %collective-permute-start.18) | collective-permute-done | bytes 32800 | tf_op jit(solution)/shard_map/ppermute | solution.py:505
  140.9 9.1 %matrix.3.refs_3_ = bf16[128,256]{1,0:T(8,128)(2,1)S(1)} custom-call(f32[128,64]{1,0:T(8,128)S(1)} %add.55.grams), custom_call_target="tpu_custom_call" | custom-call | tf_op jit(solution)/shard_map/matrix/pallas_call | solution.py:533
  150.0 18.8 %last.1 = (f32[3072,128]{1,0:T(8,128)}, f32[768,128]{1,0:T(8,128)S(1)}, f32[128,64]{1,0:T(8,128)S(1)}, f32[784,128]{1,0:T(8,128)S(1)}, f32[784,128]{1,0:T(8,128)...) custom-call(s32[3]{0:T(128)S(1)} %pad_add_fusion.scal, f32[3072,128]{1,0:T(8,128)} %copy-done.3, ...), custom_call_target="tpu_custom_call" | custom-call | tf_op jit(solution)/shard_map/last/pallas_call | solution.py:547
  168.8 1.9 collective-permute-start.31
  171.8 1.3 collective-permute-start.28
  173.0 2.5 %collective-permute-start.29 = (f32[784,128]{1,0:T(8,128)S(1)}, f32[784,128]{1,0:T(8,128)S(1)}, u32[]{:S(2)}, u32[]{:S(2)}) collective-permute-start(f32[784,128]{1,0:T(8,128)S(1)} %get-tuple-element.73), channel_id=1, source_target_pairs={{0,3},{1,0},{2,1},{3,2},{4,7},{5,4},{6,5},{7,6},{8,11},{9,8},{10,9... | collective-permute-start | bytes 1204232 | tf_op jit(solution)/shard_map/ppermute | solution.py:490
  175.6 19.3 %collective-permute-done.23 = f32[128,64]{1,0:T(8,128)S(1)} collective-permute-done((f32[128,64]{1,0:T(8,128)S(1)}, f32[128,64]{1,0:T(8,128)S(1)}, u32[]{:S(2)}, u32[]{:S(2)}) %collective-permute-start.23) | collective-permute-done | bytes 32800 | tf_op jit(solution)/shard_map/ppermute | solution.py:503
  195.3 5.2 %collective-permute-done.24 = f32[128,64]{1,0:T(8,128)S(1)} collective-permute-done((f32[128,64]{1,0:T(8,128)S(1)}, f32[128,64]{1,0:T(8,128)S(1)}, u32[]{:S(2)}, u32[]{:S(2)}) %collective-permute-start.24) | collective-permute-done | bytes 32800 | tf_op jit(solution)/shard_map/ppermute | solution.py:503
  200.6 1.4 copy-done.2
  202.5 2.4 %collective-permute-done.25 = f32[128,64]{1,0:T(8,128)S(1)} collective-permute-done((f32[128,64]{1,0:T(8,128)S(1)}, f32[128,64]{1,0:T(8,128)S(1)}, u32[]{:S(2)}, u32[]{:S(2)}) %collective-permute-start.25) | collective-permute-done | bytes 32800 | tf_op jit(solution)/shard_map/ppermute | solution.py:505
  206.6 4.8 %collective-permute-done.33 = f32[64,64]{1,0:T(8,128)S(1)} collective-permute-done((f32[64,64]{1,0:T(8,128)S(1)}, f32[64,64]{1,0:T(8,128)S(1)}, u32[]{:S(2)}, u32[]{:S(2)}) %collective-permute-start.33) | collective-permute-done | bytes 16416 | tf_op jit(solution)/shard_map/ppermute | solution.py:503
  211.5 2.0 collective-permute-start.34
  213.5 9.4 %factor.1 = (f32[64,64]{1,0:T(8,128)S(1)}, f32[64,64]{1,0:T(8,128)}) custom-call(f32[128,64]{1,0:T(8,128)S(1)} %add.59.grams), custom_call_target="tpu_custom_call" | custom-call | tf_op jit(solution)/shard_map/factor/pallas_call | solution.py:559
  223.7 1.9 collective-permute-start.30
  225.6 6.4 %rows.1 = bf16[3072,128]{1,0:T(8,128)(2,1)} custom-call(s32[3]{0:T(128)S(1)} %pad_add_fusion.scal, f32[64,64]{1,0:T(8,128)S(1)} %get-tuple-element.69.factor, f32[784,128]{1,0:T(8,128)S(1)} %get-tuple-element.70.r0, f32[784,128]{1,0:T(8,128)S(1)} %collective-permute-done.27.r1, f32[784,128]{1,0:T(8,128)S(1)} %collective-permute-done.28.r2, ...), custom_call_target="tpu_custom_call" | custom-call | tf_op jit(solution)/shard_map/rows/pallas_call | solution.py:561
  (70 shorter events, 13.2 us)
Async XLA Ops:
  1.4 1.4 copy-start.1
  2.8 0.7 copy-start.5
  3.5 0.7 copy-start.6
  4.2 0.7 copy-start.7
  4.9 0.7 copy-start.8
  9.7 12.5 %collective-permute-start = (f32[784,128]{1,0:T(8,128)S(1)}, f32[784,128]{1,0:T(8,128)S(1)}, u32[]{:S(2)}, u32[]{:S(2)}) collective-permute-start(f32[784,128]{1,0:T(8,128)S(1)} %get-tuple-element.41), channel_id=1, source_target_pairs={{0,1},{1,2},{2,3},{3,0},{4,5},{5,6},{6,7},{7,4},{8,9},{9,10},{10,1... | collective-permute-start | bytes 1204232 | tf_op jit(solution)/shard_map/ppermute | solution.py:490
  11.3 20.3 %collective-permute-start.1 = (f32[784,128]{1,0:T(8,128)S(1)}, f32[784,128]{1,0:T(8,128)S(1)}, u32[]{:S(2)}, u32[]{:S(2)}) collective-permute-start(f32[784,128]{1,0:T(8,128)S(1)} %get-tuple-element.42), channel_id=1, source_target_pairs={{0,2},{1,3},{2,0},{3,1},{4,6},{5,7},{6,4},{7,5},{8,10},{9,11},{10,... | collective-permute-start | bytes 1204232 | tf_op jit(solution)/shard_map/ppermute | solution.py:490
  14.0 17.6 %collective-permute-start.2 = (f32[784,128]{1,0:T(8,128)S(1)}, f32[784,128]{1,0:T(8,128)S(1)}, u32[]{:S(2)}, u32[]{:S(2)}) collective-permute-start(f32[784,128]{1,0:T(8,128)S(1)} %get-tuple-element.43), channel_id=1, source_target_pairs={{0,3},{1,0},{2,1},{3,2},{4,7},{5,4},{6,5},{7,6},{8,11},{9,8},{10,9... | collective-permute-start | bytes 1204232 | tf_op jit(solution)/shard_map/ppermute | solution.py:490
  38.4 45.8 %copy-start = (f32[3072,128]{1,0:T(8,128)}, f32[3072,128]{1,0:T(8,128)S(1)}, u32[]{:S(2)}) copy-start(f32[3072,128]{1,0:T(8,128)S(1)} %get-tuple-element.44.v_ref.refs_0_) | copy-start | bytes 4718596
  38.4 13.7 %collective-permute-start.3 = (f32[784,128]{1,0:T(8,128)S(1)}, f32[784,128]{1,0:T(8,128)S(1)}, u32[]{:S(2)}, u32[]{:S(2)}) collective-permute-start(f32[784,128]{1,0:T(8,128)S(1)} %get-tuple-element.46), channel_id=1, source_target_pairs={{4,0},{5,1},{6,2},{7,3},{8,4},{9,5},{10,6},{11,7},{12,8},{13,9},{1... | collective-permute-start | bytes 1204232 | tf_op jit(solution)/shard_map/ppermute | solution.py:495
  39.7 12.4 %collective-permute-start.4 = (f32[784,128]{1,0:T(8,128)S(1)}, f32[784,128]{1,0:T(8,128)S(1)}, u32[]{:S(2)}, u32[]{:S(2)}) collective-permute-start(f32[784,128]{1,0:T(8,128)S(1)} %get-tuple-element.47), channel_id=1, source_target_pairs={{0,4},{1,5},{2,6},{3,7},{4,8},{5,9},{6,10},{7,11},{8,12},{9,13},{1... | collective-permute-start | bytes 1204232 | tf_op jit(solution)/shard_map/ppermute | solution.py:494
  44.2 6.2 %collective-permute-start.5 = (f32[144,128]{1,0:T(8,128)S(1)}, f32[144,128]{1,0:T(8,128)S(1)}, u32[]{:S(2)}, u32[]{:S(2)}) collective-permute-start(f32[144,128]{1,0:T(8,128)S(1)} %get-tuple-element.48), channel_id=1, source_target_pairs={{1,0},{2,1},{3,2},{5,4},{6,5},{7,6},{9,8},{10,9},{11,10},{13,12},{... | collective-permute-start | bytes 221192 | tf_op jit(solution)/shard_map/ppermute | solution.py:497
  45.5 6.5 %collective-permute-start.6 = (f32[144,128]{1,0:T(8,128)S(1)}, f32[144,128]{1,0:T(8,128)S(1)}, u32[]{:S(2)}, u32[]{:S(2)}) collective-permute-start(f32[144,128]{1,0:T(8,128)S(1)} %get-tuple-element.49), channel_id=1, source_target_pairs={{0,1},{1,2},{2,3},{4,5},{5,6},{6,7},{8,9},{9,10},{10,11},{12,13},{... | collective-permute-start | bytes 221192 | tf_op jit(solution)/shard_map/ppermute | solution.py:496
  58.9 1.2 copy-start.4
  60.0 38.8 %collective-permute-start.11 = (f32[784,128]{1,0:T(8,128)S(1)}, f32[784,128]{1,0:T(8,128)S(1)}, u32[]{:S(2)}, u32[]{:S(2)}) collective-permute-start(f32[784,128]{1,0:T(8,128)S(1)} %get-tuple-element.53), channel_id=1, source_target_pairs={{4,0},{5,1},{6,2},{7,3},{8,4},{9,5},{10,6},{11,7},{12,8},{13,9},{1... | collective-permute-start | bytes 1204232 | tf_op jit(solution)/shard_map/ppermute | solution.py:495
  61.3 37.6 %collective-permute-start.12 = (f32[784,128]{1,0:T(8,128)S(1)}, f32[784,128]{1,0:T(8,128)S(1)}, u32[]{:S(2)}, u32[]{:S(2)}) collective-permute-start(f32[784,128]{1,0:T(8,128)S(1)} %get-tuple-element.54), channel_id=1, source_target_pairs={{0,4},{1,5},{2,6},{3,7},{4,8},{5,9},{6,10},{7,11},{8,12},{9,13},{1... | collective-permute-start | bytes 1204232 | tf_op jit(solution)/shard_map/ppermute | solution.py:494
  65.9 4.7 %collective-permute-start.7 = (f32[128,64]{1,0:T(8,128)S(1)}, f32[128,64]{1,0:T(8,128)S(1)}, u32[]{:S(2)}, u32[]{:S(2)}) collective-permute-start(f32[128,64]{1,0:T(8,128)S(1)} %get-tuple-element.52), channel_id=1, source_target_pairs={{0,1},{1,0},{2,3},{3,2},{4,5},{5,4},{6,7},{7,6},{8,9},{9,8},{10,11... | collective-permute-start | bytes 98312 | tf_op jit(solution)/shard_map/ppermute | solution.py:503
  70.6 9.2 %collective-permute-start.8 = (f32[128,64]{1,0:T(8,128)S(1)}, f32[128,64]{1,0:T(8,128)S(1)}, u32[]{:S(2)}, u32[]{:S(2)}) collective-permute-start(f32[128,64]{1,0:T(8,128)S(1)} %add.48), channel_id=1, source_target_pairs={{0,3},{1,2},{2,1},{3,0},{4,7},{5,6},{6,5},{7,4},{8,11},{9,10},{10,... | collective-permute-start | bytes 98312 | tf_op jit(solution)/shard_map/ppermute | solution.py:503
  73.9 24.9 %collective-permute-start.13 = (f32[144,128]{1,0:T(8,128)S(1)}, f32[144,128]{1,0:T(8,128)S(1)}, u32[]{:S(2)}, u32[]{:S(2)}) collective-permute-start(f32[144,128]{1,0:T(8,128)S(1)} %get-tuple-element.55), channel_id=1, source_target_pairs={{1,0},{2,1},{3,2},{5,4},{6,5},{7,6},{9,8},{10,9},{11,10},{13,12},{... | collective-permute-start | bytes 221192 | tf_op jit(solution)/shard_map/ppermute | solution.py:497
  75.2 23.6 %collective-permute-start.14 = (f32[144,128]{1,0:T(8,128)S(1)}, f32[144,128]{1,0:T(8,128)S(1)}, u32[]{:S(2)}, u32[]{:S(2)}) collective-permute-start(f32[144,128]{1,0:T(8,128)S(1)} %get-tuple-element.56), channel_id=1, source_target_pairs={{0,1},{1,2},{2,3},{4,5},{5,6},{6,7},{8,9},{9,10},{10,11},{12,13},{... | collective-permute-start | bytes 221192 | tf_op jit(solution)/shard_map/ppermute | solution.py:496
  79.8 4.4 %collective-permute-start.9 = (f32[128,64]{1,0:T(8,128)S(1)}, f32[128,64]{1,0:T(8,128)S(1)}, u32[]{:S(2)}, u32[]{:S(2)}) collective-permute-start(f32[128,64]{1,0:T(8,128)S(1)} %add.49), channel_id=1, source_target_pairs={{0,4},{1,5},{2,6},{3,7},{4,0},{5,1},{6,2},{7,3},{8,12},{9,13},{10,... | collective-permute-start | bytes 98312 | tf_op jit(solution)/shard_map/ppermute | solution.py:505
  84.2 5.6 %collective-permute-start.10 = (f32[128,64]{1,0:T(8,128)S(1)}, f32[128,64]{1,0:T(8,128)S(1)}, u32[]{:S(2)}, u32[]{:S(2)}) collective-permute-start(f32[128,64]{1,0:T(8,128)S(1)} %add.50), channel_id=1, source_target_pairs={{0,12},{1,13},{2,14},{3,15},{4,8},{5,9},{6,10},{7,11},{8,4},{9,5},... | collective-permute-start | bytes 98312 | tf_op jit(solution)/shard_map/ppermute | solution.py:505
  113.4 1.1 copy-start.3
  114.5 35.5 %collective-permute-start.19 = (f32[784,128]{1,0:T(8,128)S(1)}, f32[784,128]{1,0:T(8,128)S(1)}, u32[]{:S(2)}, u32[]{:S(2)}) collective-permute-start(f32[784,128]{1,0:T(8,128)S(1)} %get-tuple-element.64), channel_id=1, source_target_pairs={{4,0},{5,1},{6,2},{7,3},{8,4},{9,5},{10,6},{11,7},{12,8},{13,9},{1... | collective-permute-start | bytes 1204232 | tf_op jit(solution)/shard_map/ppermute | solution.py:495
  115.8 34.2 %collective-permute-start.20 = (f32[784,128]{1,0:T(8,128)S(1)}, f32[784,128]{1,0:T(8,128)S(1)}, u32[]{:S(2)}, u32[]{:S(2)}) collective-permute-start(f32[784,128]{1,0:T(8,128)S(1)} %get-tuple-element.65), channel_id=1, source_target_pairs={{0,4},{1,5},{2,6},{3,7},{4,8},{5,9},{6,10},{7,11},{8,12},{9,13},{1... | collective-permute-start | bytes 1204232 | tf_op jit(solution)/shard_map/ppermute | solution.py:494
  120.4 4.4 %collective-permute-start.15 = (f32[128,64]{1,0:T(8,128)S(1)}, f32[128,64]{1,0:T(8,128)S(1)}, u32[]{:S(2)}, u32[]{:S(2)}) collective-permute-start(f32[128,64]{1,0:T(8,128)S(1)} %get-tuple-element.59), channel_id=1, source_target_pairs={{0,1},{1,0},{2,3},{3,2},{4,5},{5,4},{6,7},{7,6},{8,9},{9,8},{10,11... | collective-permute-start | bytes 98312 | tf_op jit(solution)/shard_map/ppermute | solution.py:503
  124.8 6.0 %collective-permute-start.16 = (f32[128,64]{1,0:T(8,128)S(1)}, f32[128,64]{1,0:T(8,128)S(1)}, u32[]{:S(2)}, u32[]{:S(2)}) collective-permute-start(f32[128,64]{1,0:T(8,128)S(1)} %add.52), channel_id=1, source_target_pairs={{0,3},{1,2},{2,1},{3,0},{4,7},{5,6},{6,5},{7,4},{8,11},{9,10},{10,... | collective-permute-start | bytes 98312 | tf_op jit(solution)/shard_map/ppermute | solution.py:503
  124.9 25.1 %collective-permute-start.21 = (f32[144,128]{1,0:T(8,128)S(1)}, f32[144,128]{1,0:T(8,128)S(1)}, u32[]{:S(2)}, u32[]{:S(2)}) collective-permute-start(f32[144,128]{1,0:T(8,128)S(1)} %get-tuple-element.66), channel_id=1, source_target_pairs={{1,0},{2,1},{3,2},{5,4},{6,5},{7,6},{9,8},{10,9},{11,10},{13,12},{... | collective-permute-start | bytes 221192 | tf_op jit(solution)/shard_map/ppermute | solution.py:497
  126.2 23.8 %collective-permute-start.22 = (f32[144,128]{1,0:T(8,128)S(1)}, f32[144,128]{1,0:T(8,128)S(1)}, u32[]{:S(2)}, u32[]{:S(2)}) collective-permute-start(f32[144,128]{1,0:T(8,128)S(1)} %get-tuple-element.67), channel_id=1, source_target_pairs={{0,1},{1,2},{2,3},{4,5},{5,6},{6,7},{8,9},{9,10},{10,11},{12,13},{... | collective-permute-start | bytes 221192 | tf_op jit(solution)/shard_map/ppermute | solution.py:496
  130.7 4.4 %collective-permute-start.17 = (f32[128,64]{1,0:T(8,128)S(1)}, f32[128,64]{1,0:T(8,128)S(1)}, u32[]{:S(2)}, u32[]{:S(2)}) collective-permute-start(f32[128,64]{1,0:T(8,128)S(1)} %add.53), channel_id=1, source_target_pairs={{0,4},{1,5},{2,6},{3,7},{4,0},{5,1},{6,2},{7,3},{8,12},{9,13},{10,... | collective-permute-start | bytes 98312 | tf_op jit(solution)/shard_map/ppermute | solution.py:505
  135.1 5.7 %collective-permute-start.18 = (f32[128,64]{1,0:T(8,128)S(1)}, f32[128,64]{1,0:T(8,128)S(1)}, u32[]{:S(2)}, u32[]{:S(2)}) collective-permute-start(f32[128,64]{1,0:T(8,128)S(1)} %add.54), channel_id=1, source_target_pairs={{0,12},{1,13},{2,14},{3,15},{4,8},{5,9},{6,10},{7,11},{8,4},{9,5},... | collective-permute-start | bytes 98312 | tf_op jit(solution)/shard_map/ppermute | solution.py:505
  168.8 31.8 %collective-permute-start.31 = (f32[768,128]{1,0:T(8,128)S(1)}, f32[768,128]{1,0:T(8,128)S(1)}, u32[]{:S(2)}, u32[]{:S(2)}) collective-permute-start(f32[768,128]{1,0:T(8,128)S(1)} %get-tuple-element.76), channel_id=1, source_target_pairs={{0,16},{16,32},{32,48},{48,64},{64,80},{80,96},{96,112},{112,128},... | collective-permute-start | bytes 1179656 | tf_op jit(solution)/shard_map/ppermute | solution.py:557
  170.7 54.9 %collective-permute-start.27 = (f32[784,128]{1,0:T(8,128)S(1)}, f32[784,128]{1,0:T(8,128)S(1)}, u32[]{:S(2)}, u32[]{:S(2)}) collective-permute-start(f32[784,128]{1,0:T(8,128)S(1)} %get-tuple-element.71), channel_id=1, source_target_pairs={{0,1},{1,2},{2,3},{3,0},{4,5},{5,6},{6,7},{7,4},{8,9},{9,10},{10,1... | collective-permute-start | bytes 1204232 | tf_op jit(solution)/shard_map/ppermute | solution.py:490
  171.8 53.9 %collective-permute-start.28 = (f32[784,128]{1,0:T(8,128)S(1)}, f32[784,128]{1,0:T(8,128)S(1)}, u32[]{:S(2)}, u32[]{:S(2)}) collective-permute-start(f32[784,128]{1,0:T(8,128)S(1)} %get-tuple-element.72), channel_id=1, source_target_pairs={{0,2},{1,3},{2,0},{3,1},{4,6},{5,7},{6,4},{7,5},{8,10},{9,11},{10,... | collective-permute-start | bytes 1204232 | tf_op jit(solution)/shard_map/ppermute | solution.py:490
  173.0 52.6 %collective-permute-start.29 = (f32[784,128]{1,0:T(8,128)S(1)}, f32[784,128]{1,0:T(8,128)S(1)}, u32[]{:S(2)}, u32[]{:S(2)}) collective-permute-start(f32[784,128]{1,0:T(8,128)S(1)} %get-tuple-element.73), channel_id=1, source_target_pairs={{0,3},{1,0},{2,1},{3,2},{4,7},{5,4},{6,5},{7,6},{8,11},{9,8},{10,9... | collective-permute-start | bytes 1204232 | tf_op jit(solution)/shard_map/ppermute | solution.py:490
  175.5 19.3 %collective-permute-start.23 = (f32[128,64]{1,0:T(8,128)S(1)}, f32[128,64]{1,0:T(8,128)S(1)}, u32[]{:S(2)}, u32[]{:S(2)}) collective-permute-start(f32[128,64]{1,0:T(8,128)S(1)} %get-tuple-element.68), channel_id=1, source_target_pairs={{0,1},{1,0},{2,3},{3,2},{4,5},{5,4},{6,7},{7,6},{8,9},{9,8},{10,11... | collective-permute-start | bytes 98312 | tf_op jit(solution)/shard_map/ppermute | solution.py:503
  194.9 5.6 %collective-permute-start.24 = (f32[128,64]{1,0:T(8,128)S(1)}, f32[128,64]{1,0:T(8,128)S(1)}, u32[]{:S(2)}, u32[]{:S(2)}) collective-permute-start(f32[128,64]{1,0:T(8,128)S(1)} %add.56), channel_id=1, source_target_pairs={{0,3},{1,2},{2,1},{3,0},{4,7},{5,6},{6,5},{7,4},{8,11},{9,10},{10,... | collective-permute-start | bytes 98312 | tf_op jit(solution)/shard_map/ppermute | solution.py:503
  200.5 4.4 %collective-permute-start.25 = (f32[128,64]{1,0:T(8,128)S(1)}, f32[128,64]{1,0:T(8,128)S(1)}, u32[]{:S(2)}, u32[]{:S(2)}) collective-permute-start(f32[128,64]{1,0:T(8,128)S(1)} %add.57), channel_id=1, source_target_pairs={{0,4},{1,5},{2,6},{3,7},{4,0},{5,1},{6,2},{7,3},{8,12},{9,13},{10,... | collective-permute-start | bytes 98312 | tf_op jit(solution)/shard_map/ppermute | solution.py:505
  200.6 1.4 copy-start.2
  202.4 4.0 %collective-permute-start.32 = (f32[64,64]{1,0:T(8,128)S(1)}, f32[64,64]{1,0:T(8,128)S(1)}, u32[]{:S(2)}, u32[]{:S(2)}) collective-permute-start(f32[64,64]{1,0:T(8,128)S(1)} %off.1), channel_id=1, source_target_pairs={{0,1},{1,0},{2,3},{3,2},{4,5},{5,4},{6,7},{7,6},{8,9},{9,8},{10,11... | collective-permute-start | bytes 49160 | tf_op jit(solution)/shard_map/ppermute | solution.py:503
  204.8 8.7 %collective-permute-start.26 = (f32[128,64]{1,0:T(8,128)S(1)}, f32[128,64]{1,0:T(8,128)S(1)}, u32[]{:S(2)}, u32[]{:S(2)}) collective-permute-start(f32[128,64]{1,0:T(8,128)S(1)} %add.58), channel_id=1, source_target_pairs={{0,12},{1,13},{2,14},{3,15},{4,8},{5,9},{6,10},{7,11},{8,4},{9,5},... | collective-permute-start | bytes 98312 | tf_op jit(solution)/shard_map/ppermute | solution.py:505
  206.4 5.1 %collective-permute-start.33 = (f32[64,64]{1,0:T(8,128)S(1)}, f32[64,64]{1,0:T(8,128)S(1)}, u32[]{:S(2)}, u32[]{:S(2)}) collective-permute-start(f32[64,64]{1,0:T(8,128)S(1)} %add.60), channel_id=1, source_target_pairs={{0,3},{1,2},{2,1},{3,0},{4,7},{5,6},{6,5},{7,4},{8,11},{9,10},{10,... | collective-permute-start | bytes 49160 | tf_op jit(solution)/shard_map/ppermute | solution.py:503
  211.5 11.4 %collective-permute-start.34 = (f32[64,64]{1,0:T(8,128)S(1)}, f32[64,64]{1,0:T(8,128)S(1)}, u32[]{:S(2)}, u32[]{:S(2)}) collective-permute-start(f32[64,64]{1,0:T(8,128)S(1)} %add.61), channel_id=1, source_target_pairs={{0,4},{1,5},{2,6},{3,7},{4,0},{5,1},{6,2},{7,3},{8,12},{9,13},{10,... | collective-permute-start | bytes 49160 | tf_op jit(solution)/shard_map/ppermute | solution.py:505
  222.9 9.2 %collective-permute-start.35 = (f32[64,64]{1,0:T(8,128)S(1)}, f32[64,64]{1,0:T(8,128)S(1)}, u32[]{:S(2)}, u32[]{:S(2)}) collective-permute-start(f32[64,64]{1,0:T(8,128)S(1)} %add.62), channel_id=1, source_target_pairs={{0,12},{1,13},{2,14},{3,15},{4,8},{5,9},{6,10},{7,11},{8,4},{9,5},... | collective-permute-start | bytes 49160 | tf_op jit(solution)/shard_map/ppermute | solution.py:505
  223.7 8.4 %collective-permute-start.30 = (f32[64,64]{1,0:T(8,128)S(1)}, f32[64,64]{1,0:T(8,128)S(1)}, u32[]{:S(2)}, u32[]{:S(2)}) collective-permute-start(f32[64,64]{1,0:T(8,128)S(1)} %get-tuple-element.69.factor), channel_id=1, source_target_pairs={{0,16},{16,32},{32,48},{48,64},{64,80},{80,96},{96,112},{112,128},... | collective-permute-start | bytes 49160 | tf_op jit(solution)/shard_map/ppermute | solution.py:560

commit v2 on v1

--- a/solution.py
+++ b/solution.py
@@ -21,7 +21,7 @@
 
 VM = pl.BlockSpec(memory_space=pltpu.VMEM)
 SM = pl.BlockSpec(memory_space=pltpu.SMEM)
-PARAMS = pltpu.CompilerParams(vmem_limit_bytes=48 << 20)
+PARAMS = pltpu.CompilerParams(vmem_limit_bytes=20 << 20)
 
 FX, FXL, FY, FYL, FZ, FZL, DINV, BW, MASS, UN = range(10)
 
@@ -59,8 +59,21 @@
     ref[pl.ds(pl.multiple_of(index * K, K), K), :] = value
 
 
-def pack_kernel(scal, v_ref, fx, fy, fz, m, p0, p1, p2, p3):
+def pack_kernel(scal, v_hbm, fx_hbm, fy_hbm, fz_hbm, m_hbm, p0, p1, p2, p3, v_ref, fx, fy, fz, m, v_sem, f_sem):
     active, px, row = scal[0], scal[1], scal[2]
+    whole = K * NX
+
+    def v_copy(c):
+        return pltpu.make_async_copy(v_hbm.at[pl.ds(c * whole, whole), :], v_ref.at[pl.ds(c * whole, whole), :], v_sem.at[c])
+
+    for c in range(3):
+        v_copy(c).start()
+    copies = [
+        pltpu.make_async_copy(src, dst, f_sem.at[j])
+        for j, (src, dst) in enumerate(((fx_hbm, fx), (fy_hbm, fy), (fz_hbm, fz), (m_hbm, m)))
+    ]
+    for copy in copies:
+        copy.start()
     outs_ref = (p0, p1, p2, p3)
     back = ((4 - px) & 3) * 32
     block = lanes(K) >> 5
@@ -80,7 +93,11 @@
             put(outs_ref[d], t, outs[d])
         return carry
 
-    lax.fori_loop(0, GROUPS, body, 0)
+    for c in range(3):
+        v_copy(c).wait()
+        lax.fori_loop(c * 4, c * 4 + 4, body, 0)
+    for copy in copies:
+        copy.wait()
     plane = lax.broadcasted_iota(jnp.int32, (NX, LANES), 0)
     depth = lanes(NX)
     small = depth >> 5
@@ -122,7 +139,7 @@
     put(z_dn, group, low)
 
 
-def unpack_kernel(scal, r0, r1, r2, r3, b_ref, fields, y_up, y_dn, z_up, z_dn):
+def unpack_kernel(scal, r0, r1, r2, r3, b_ref, fields, y_up, y_dn, near, far, z_up, z_dn):
     px = scal[1]
     refs = (r0, r1, r2, r3)
     block = lanes(K) >> 5
@@ -158,6 +175,7 @@
     y_up[pl.ds(GROUPS * K, NX), :] = roll(done[1], 32)
     y_dn[pl.ds(GROUPS * K, NX), :] = jnp.zeros((NX, LANES), F32)
     z_up[pl.ds(2 * K, NX), :] = roll(done[2], -31)
+    by_parity(scal, near, far, z_up, z_dn)
 
 
 def line(fld, which, plane):
@@ -199,10 +217,17 @@
         )
 
 
+def by_parity(scal, near, far, z_up, z_dn):
+    odd = (scal[1] & 1) == 1
+    up, dn = z_up[...], z_dn[...]
+    near[...] = jnp.where(odd, dn, up)
+    far[...] = jnp.where(odd, up, dn)
+
+
 def finish_gram(acc, out):
     half = acc[0:K, :] + acc[K : 2 * K, :]
-    out[0:K, :] = half[:, 0:K] + half[:, K : 2 * K]
-    out[K : 2 * K, :] = half[:, 2 * K : 3 * K] + half[:, 3 * K : 4 * K]
+    out[0:K, 0:K] = half[:, 0:K] + half[:, K : 2 * K]
+    out[0:K, K : 2 * K] = half[:, 2 * K : 3 * K] + half[:, 3 * K : 4 * K]
 
 
 def edge_fields(fld, y_up, y_dn, z_up, z_dn):
@@ -215,7 +240,18 @@
     z_dn[pl.ds(2 * K, NX), :] = jnp.where((lane & 31) == 0, dinv, roll(weight, 1))
 
 
-def first_kernel(scal, v_ref, raw, h_up, h_dn, h_zp, h_zm, av_ref, fld, grams, y_up, y_dn, z_up, z_dn, acc):
+def split_near(scal, h_near, h_far, h_zp, h_zm):
+    odd = (scal[1] & 1) == 1
+    one = h_near[pl.ds(h_near.shape[0] - ZROWS, ZROWS), :]
+    two = h_far[pl.ds(h_far.shape[0] - ZROWS, ZROWS), :]
+    h_zp[...] = jnp.where(odd, two, one)
+    h_zm[...] = jnp.where(odd, one, two)
+
+
+def first_kernel(
+    scal, v_ref, raw, h_up, h_dn, h_near, h_far, av_ref, fld, near, far, y_up, y_dn, acc, z_up, z_dn, h_zp, h_zm
+):
+    split_near(scal, h_near, h_far, h_zp, h_zm)
     active = scal[0]
     lane = lanes(NX)
     plane = lax.broadcasted_iota(jnp.int32, (NX, LANES), 0)
@@ -245,7 +281,8 @@
 
     lax.fori_loop(0, GROUPS, body, 0)
     edge_fields(fld, y_up, y_dn, z_up, z_dn)
-    finish_gram(acc, grams)
+    finish_gram(acc, near)
+    by_parity(scal, near.at[pl.ds(K, ZROWS), :], far, z_up, z_dn)
 
 
 def mixed(matrix, v, av, dinv, weight):
@@ -263,17 +300,23 @@
 def step_kernel(last, scal, *refs):
     ins, refs = refs[:12], refs[12:]
     v_ref, av_ref, fld, mat = ins[:4]
-    hv, ha = ins[4:8], ins[8:12]
-    hf, refs = refs[:4], refs[4:]
+    hv, ha = list(ins[4:8]), list(ins[8:12])
     if last:
-        w_ref, img_ref, grams, p0, p1, p2, p3, acc, rows_y, rows_z, n_up, n_dn, n_zp, n_zm = refs
+        r_y, r_z, w_ref, img_ref, grams, p0, p1, p2, p3, acc, a_zp, a_zm, n_up, n_dn, n_zp, n_zm = refs
         new_ref = w_ref
+        rows_y, rows_z = r_y, r_z
     else:
-        new_ref, out_ref, grams, n_up, n_dn, n_zp, n_zm, y_up, y_dn, z_up, z_dn, acc, rows_y, rows_z = refs
+        (new_ref, out_ref, near, far, n_up, n_dn, n_zp, n_zm, y_up, y_dn, rows_y, rows_z) = refs[:12]
+        acc, z_up, z_dn, v_zp, v_zm, a_zp, a_zm = refs[12:]
+        split_near(scal, hv[2], hv[3], v_zp, v_zm)
+        hv[2:] = [v_zp, v_zm]
+    split_near(scal, ha[2], ha[3], a_zp, a_zm)
+    ha[2:] = [a_zp, a_zm]
     active, px = scal[0], scal[1]
     matrix = mat[...]
     one = lanes(1)
-    for side in range(2):
+    hf = ha
+    for side in range(0 if last else 2):
         for big in range(4):
             for which in range(2):
                 out = None
@@ -372,7 +415,11 @@
         return carry
 
     lax.fori_loop(0, GROUPS, body, 0)
-    finish_gram(acc, grams)
+    if last:
+        finish_gram(acc, grams)
+    else:
+        finish_gram(acc, near)
+        by_parity(scal, near.at[pl.ds(K, ZROWS), :], far, z_up, z_dn)
 
 
 def small_dot(a, b, dims=((1,), (0,))):
@@ -382,28 +429,52 @@
 def inverse_factor(gram):
     row = lax.broadcasted_iota(jnp.int32, (8, LANES), 0)
     lane = lanes(8)
+
+    def one_row(x, at):
+        return jnp.broadcast_to(x[at : at + 1, :], (8, LANES))
+
+    def one_column(x, at):
+        return jnp.broadcast_to(x[:, at : at + 1], (8, LANES))
+
     parts = []
     for g in range(8):
         left = jnp.concatenate([gram[g * 8 : g * 8 + 8, :], jnp.zeros((8, K), F32)], axis=1)
         parts.append(jnp.where(lane == row + (g * 8 + K), 1.0, left))
     pivots = [None] * 8
-    for j in range(K):
-        g0, s0 = j // 8, j % 8
-        pivot_row = jnp.broadcast_to(parts[g0][s0 : s0 + 1, :], (8, LANES))
-        pivot = jnp.broadcast_to(pivot_row[:, j : j + 1], (8, LANES))
-        scaled = pivot_row * (1.0 / pivot)
-        pivots[g0] = pivot if s0 == 0 else jnp.where(row == s0, pivot, pivots[g0])
-        for g in range(g0, 8):
-            column = jnp.broadcast_to(parts[g][:, j : j + 1], (8, LANES))
-            if g == g0:
-                column = jnp.where(row > s0, column, 0.0)
-            parts[g] = parts[g] - column * scaled
+    for g0 in range(8):
+        top = parts[g0]
+        columns = [one_column(top, g0 * 8 + j) for j in range(8)]
+        inverse, lines, ahead = [], [], []
+        for j in range(8):
+            pivot = one_row(columns[j], j)
+            line_j = one_row(top, j)
+            pivots[g0] = pivot if j == 0 else jnp.where(row == j, pivot, pivots[g0])
+            inv = 1.0 / pivot
+            factor = jnp.where(row > j, columns[j] * inv, 0.0)
+            after = [one_row(columns[k], j) for k in range(j + 1, 8)]
+            for k in range(j + 1, 8):
+                columns[k] = columns[k] - factor * after[k - j - 1]
+            top = top - factor * line_j
+            inverse.append(inv)
+            lines.append(line_j)
+            ahead.append(after)
+        parts[g0] = top
+        for g in range(g0 + 1, 8):
+            part = parts[g]
+            columns = [one_column(part, g0 * 8 + j) for j in range(8)]
+            for j in range(8):
+                factor = columns[j] * inverse[j]
+                for k in range(j + 1, 8):
+                    columns[k] = columns[k] - factor * ahead[j][k - j - 1]
+                part = part - factor * lines[j]
+            parts[g] = part
     return jnp.concatenate([(parts[g] * lax.rsqrt(pivots[g]))[:, K:] for g in range(8)], axis=0)
 
 
 def matrix_kernel(grams, mat):
-    factor = inverse_factor(grams[0:K, :])
-    image = small_dot(factor, grams[K : 2 * K, :])
+    both = grams[0:K, :]
+    factor = inverse_factor(both[:, 0:K])
+    image = small_dot(factor, both[:, K : 2 * K])
     rayleigh = small_dot(image, factor, ((1,), (1,)))
     other = 0.5 * small_dot(rayleigh, factor, ((0,), (0,)))
     fh, fl = halves(factor)
@@ -414,9 +485,10 @@
 
 
 def factor_kernel(grams, factor_ref, diag_ref):
-    factor = inverse_factor(grams[0:K, :])
+    both = grams[...]
+    factor = inverse_factor(both[:, 0:K])
     factor_ref[...] = factor
-    image = small_dot(factor, grams[K : 2 * K, :])
+    image = small_dot(factor, both[:, K : 2 * K])
     diag_ref[...] = small_dot(image, factor, ((1,), (1,)))
 
 
@@ -474,11 +546,11 @@
     lax.fori_loop(0, 3 * K * NX // 128, cast, 0)
 
 
-def call(kernel, n_in, shapes, scratch=(), first=VM, name=None):
+def call(kernel, n_in, shapes, scratch=(), first=VM, name=None, rest=VM):
     return pl.pallas_call(
         kernel,
         out_shape=shapes,
-        in_specs=[first] + [VM] * (n_in - 1),
+        in_specs=[first] + [rest] * (n_in - 1),
         out_specs=jax.tree.map(lambda _: VM, shapes),
         scratch_shapes=list(scratch),
         compiler_params=PARAMS,
@@ -486,24 +558,46 @@
     )
 
 
+NEAR = ((1, 0, 3, 2), (3, 2, 1, 0))
+
+
 def shift_x(value, d):
     return lax.ppermute(value, "dom", [(i, (i & 12) + ((i + d) & 3)) for i in range(16)])
 
 
-def halo(y_up, y_dn, z_up, z_dn):
+def pair_x(value, which):
+    return lax.ppermute(value, "dom", [(i, (i & 12) + NEAR[which][i & 3]) for i in range(16)])
+
+
+def pair_y(value, which):
+    return lax.ppermute(value, "dom", [(i, NEAR[which][i >> 2] * 4 + (i & 3)) for i in range(16)])
+
+
+def halo_y(y_up, y_dn):
     h_dn = lax.ppermute(y_up, "dom", [(i, i + 4) for i in range(12)])
     h_up = lax.ppermute(y_dn, "dom", [(i + 4, i) for i in range(12)])
-    h_zm = lax.ppermute(z_up, "dom", [(i, i + 1) for i in range(16) if i & 3 < 3])
-    h_zp = lax.ppermute(z_dn, "dom", [(i + 1, i) for i in range(16) if i & 3 < 3])
-    return h_up, h_dn, h_zp, h_zm
-
-
-def total(value):
-    for near in ((1, 0, 3, 2), (3, 2, 1, 0)):
-        value = value + lax.ppermute(value, "dom", [(i, (i & 12) + near[i & 3]) for i in range(16)])
-    for near in ((1, 0, 3, 2), (3, 2, 1, 0)):
-        value = value + lax.ppermute(value, "dom", [(i, near[i >> 2] * 4 + (i & 3)) for i in range(16)])
+    return h_up, h_dn
+
+
+def total_y(value):
+    for which in range(2):
+        value = value + pair_y(value, which)
     return value
+
+
+def total_x(value):
+    for which in range(2):
+        value = value + pair_x(value, which)
+    return value
+
+
+def exchange(near, far, y_up, y_dn):
+    h_up, h_dn = halo_y(y_up, y_dn)
+    h_near = pair_x(near, 0)
+    grams = near[0:K] + h_near[0:K]
+    h_far = pair_x(jnp.concatenate([grams, far], axis=0), 1)
+    grams = grams + h_far[0:K]
+    return total_y(grams), (h_up, h_dn, h_near, h_far)
 
 
 def on_device(start_vectors, face_x, face_y, face_z, masses, active):
@@ -513,51 +607,67 @@
     fields = [f.reshape(NX, LANES) for f in (face_x, face_y, face_z, masses)]
     msg = f32(YROWS, LANES)
     zmsg = f32(ZROWS, LANES)
+    near = f32(K + ZROWS, LANES)
     whole = f32(SLABS * K, LANES)
-    gram2 = f32(2 * K, K)
-    rows4 = (msg,) * 4
-    side4 = (msg, msg, zmsg, zmsg)
-    packed = call(pack_kernel, 6, rows4, first=SM, name="pack")(scal, start, *fields)
+    plane = pltpu.VMEM((NX, LANES), F32)
+    columns = pltpu.VMEM((ZROWS, LANES), F32)
+    packed = call(
+        pack_kernel,
+        6,
+        (msg,) * 4,
+        (pltpu.VMEM((3 * K * NX, LANES), F32),)
+        + (plane,) * 4
+        + (pltpu.SemaphoreType.DMA((3,)), pltpu.SemaphoreType.DMA((4,))),
+        first=SM,
+        name="pack",
+        rest=pl.BlockSpec(memory_space=pl.ANY),
+    )(scal, start, *fields)
     got = [packed[0]] + [shift_x(packed[d], d) for d in (1, 2, 3)]
-    v, raw, *side = call(unpack_kernel, 5, (whole, f32(4 * NX, LANES)) + side4, first=SM, name="unpack")(scal, *got)
-    hv = halo(*side)
+    v, raw, y_up, y_dn, z_near, z_far = call(
+        unpack_kernel, 5, (whole, f32(4 * NX, LANES), msg, msg, zmsg, zmsg), (columns,) * 2, first=SM, name="unpack"
+    )(scal, *got)
+    hv = halo_y(y_up, y_dn) + (pair_x(z_near, 0), pair_x(z_far, 1))
     acc = pltpu.VMEM((2 * K, 4 * K), F32)
-    av, fld, grams, *side = call(
-        first_kernel, 7, (whole, f32(10 * NX, LANES), gram2) + side4, (acc,), first=SM, name="first"
+    av, fld, *sent = call(
+        first_kernel,
+        7,
+        (whole, f32(10 * NX, LANES), near, zmsg, msg, msg),
+        (acc,) + (columns,) * 4,
+        first=SM,
+        name="first",
     )(scal, v, raw, *hv)
-    ha = halo(*side)
-    hf = ha
     mat_shape = jax.ShapeDtypeStruct((2 * K, 4 * K), BF16)
-    rows = (pltpu.VMEM((16, LANES), F32), pltpu.VMEM((8, LANES), F32))
-    for repeat in range(STEPS):
-        mat = call(matrix_kernel, 1, mat_shape, name="matrix")(total(grams))
-        ops = (scal, v, av, fld, mat, *hv, *ha, *hf)
-        if repeat + 1 < STEPS:
-            v, av, grams, *rest = call(
-                functools.partial(step_kernel, False),
-                17,
-                (whole, whole, gram2) + side4 + side4,
-                (acc,) + rows,
-                first=SM,
-                name="step",
-            )(*ops)
-            hv = tuple(rest[:4])
-            ha = halo(*rest[4:])
-        else:
-            w, img, grams, *packed = call(
-                functools.partial(step_kernel, True),
-                17,
-                (whole, f32(3 * OV * K, LANES), gram2) + rows4,
-                (acc,) + rows + (pltpu.VMEM((YROWS, LANES), F32),) * 2 + (pltpu.VMEM((ZROWS, LANES), F32),) * 2,
-                first=SM,
-                name="last",
-            )(*ops)
-    got = [packed[0]] + [shift_x(packed[d], d) for d in (1, 2, 3)]
+    grams, ha = exchange(*sent)
+    mat = call(matrix_kernel, 1, mat_shape, name="matrix")(grams)
+    v, av, *rest = call(
+        functools.partial(step_kernel, False),
+        13,
+        (whole, whole, near, zmsg, msg, msg, zmsg, zmsg, msg, msg, f32(16, LANES), f32(8, LANES)),
+        (acc,) + (columns,) * 6,
+        first=SM,
+        name="step",
+    )(scal, v, av, fld, mat, *hv, *ha)
+    hv = tuple(rest[2:6])
+    lines = tuple(rest[8:])
+    grams, ha = exchange(rest[0], rest[1], rest[6], rest[7])
+    mat = call(matrix_kernel, 1, mat_shape, name="matrix")(grams)
+    w, img, grams, *packed = call(
+        functools.partial(step_kernel, True),
+        15,
+        (whole, f32(3 * OV * K, LANES), f32(K, LANES)) + (f32(GROUPS * K, LANES),) * 4,
+        (acc,) + (columns,) * 2 + (pltpu.VMEM((YROWS, LANES), F32),) * 2 + (columns,) * 2,
+        first=SM,
+        name="last",
+    )(scal, v, av, fld, mat, *hv, *ha, *lines)
     behind = [(i, i + 1) for i in range(15)]
     before = lax.ppermute(img, "sub", behind)
+    grams = total_x(grams)
+    grams, packed = lax.optimization_barrier((grams, packed))
+    got = [packed[0]] + [shift_x(packed[d], d) for d in (1, 2, 3)]
     raw_off = call(off_kernel, 2, f32(K, K), name="off")(w, before)
-    factor, diag = call(factor_kernel, 1, (f32(K, K), f32(K, K)), name="factor")(total(grams))
-    off = call(cross_kernel, 3, f32(K, K), name="cross")(factor, lax.ppermute(factor, "sub", behind), total(raw_off))
+    factor, diag = call(factor_kernel, 1, (f32(K, K), f32(K, K)), name="factor")(total_y(grams))
+    raw_off = total_x(total_y(raw_off))
+    off = call(cross_kernel, 3, f32(K, K), name="cross")(factor, lax.ppermute(factor, "sub", behind), raw_off)
     out = call(
         out_kernel,
         6,

time: 237 us -> 183 us (0.77)
  Pallas kernels: 86.2 us -> 62.3 us
  waiting for transfers between devices: 71.7 us -> 54.2 us
  starting transfers between devices: 65.4 us -> 59 us
  local copies, waits for them, and re-layouts: 7.9 us -> 4.19 us
    pallas_call x8, Pallas kernels: 78.5 us -> 54.5 us  [the longest x1 16.4 us: on_device(): call(functools.partial(step_kernel, True), 15, (whole, f32(3 * OV * K, LA...]
    ppermute x28 -> x24, waiting for transfers between devices: 55.5 us -> 36.2 us  [the longest x10 19.7 us: pair_x(): lax.ppermute(value, 'dom', [(i, (i & 12) + NEAR[which][i & 3]) for i in r...]
    ppermute x28 -> x24, starting transfers between devices: 50.9 us -> 45.2 us  [the longest x10 15.9 us: pair_x(): lax.ppermute(value, 'dom', [(i, (i & 12) + NEAR[which][i & 3]) for i in r...]
    unnamed x18 -> x10, local copies, waits for them, and re-layouts: 7.9 us -> 4.19 us
  transfers between devices with their start and end apart: 36 -> 32, of which waited for: 15 -> 18; matrix products, arithmetic and copies ran while one was open for 0% -> 0% of each run, Pallas kernels for 15% -> 5%
where the time goes in v2:
time: 183 us; the launch traced here: 181 us
  Pallas kernels  62.3 us (34%)
  starting transfers between devices  59 us (32%)
  waiting for transfers between devices  54.2 us (30%)
  local copies, waits for them, and re-layouts  4.19 us (2%)
    ppermute x10, waiting for transfers between devices, pair_x(): lax.ppermute(value, 'dom', [(i, (i & 12) + NEAR[which][i & 3]) for i in r...  19.7 us
    pallas_call x1, Pallas kernels, on_device(): call(functools.partial(step_kernel, True), 15, (whole, f32(3 * OV * K, LA...  16.4 us
    ppermute x6, waiting for transfers between devices, shift_x(): lax.ppermute(value, 'dom', [(i, (i & 12) + (i + d & 3)) for i in range(16)])  16.2 us
    ppermute x8, waiting for transfers between devices, pair_y(): lax.ppermute(value, 'dom', [(i, NEAR[which][i >> 2] * 4 + (i & 3)) for i...  16.2 us
    ppermute x10, starting transfers between devices, pair_x(): lax.ppermute(value, 'dom', [(i, (i & 12) + NEAR[which][i & 3]) for i in r...  15.9 us
    ppermute x3, starting transfers between devices, halo_y(): h_dn = lax.ppermute(y_up, 'dom', [(i, i + 4) for i in range(12)])  14.2 us
    pallas_call x1, Pallas kernels, on_device(): call(functools.partial(step_kernel, False), 13, (whole, whole, near, zmsg...  12.3 us
    ppermute x8, starting transfers between devices, pair_y(): lax.ppermute(value, 'dom', [(i, NEAR[which][i >> 2] * 4 + (i & 3)) for i...  11.3 us
  transfers between devices with their start and end apart: 32, of which 18 were waited for; matrix products, arithmetic and copies ran while one was open for 0% of the time, Pallas kernels for 5%

profile of v2, /device:TPU:128, one launch (start us, length us, event | category | flops | bytes accessed | tf_op | source)
XLA Modules:
  0.0 181.4 jit_solution(7093905256934399502)
XLA Ops:
  1.4 1.4 copy-done
  5.6 4.4 %pack.1 = (f32[784,128]{1,0:T(8,128)S(1)}, f32[784,128]{1,0:T(8,128)S(1)}, f32[784,128]{1,0:T(8,128)S(1)}, f32[784,128]{1,0:T(8,128)S(1)}) custom-call(s32[3]{0:T(128)S(1)} %pad_add_fusion.scal, f32[3072,128]{1,0:T(8,128)S(1)} %bitcast.12, f32[16,128]{1,0:T(8,128)S(1)} %bitcast.13, f32[16,128]{1,0:T(8,128)S(1)} %bitcast.14, f32[16,128]{1,0:T(8,128)S(1)} %bitcast.15, ...), custom_call_target="tpu_custom_call" | custom-call | tf_op jit(solution)/shard_map/pack/pallas_call | solution.py:614
  9.9 1.6 collective-permute-start
  11.5 2.7 %collective-permute-start.1 = (f32[784,128]{1,0:T(8,128)S(1)}, f32[784,128]{1,0:T(8,128)S(1)}, u32[]{:S(2)}, u32[]{:S(2)}) collective-permute-start(f32[784,128]{1,0:T(8,128)S(1)} %get-tuple-element.47), channel_id=1, source_target_pairs={{0,2},{1,3},{2,0},{3,1},{4,6},{5,7},{6,4},{7,5},{8,10},{9,11},{10,... | collective-permute-start | bytes 1204232 | tf_op jit(solution)/shard_map/ppermute | solution.py:565
  14.2 1.4 collective-permute-start.2
  15.7 6.7 %collective-permute-done.r1 = f32[784,128]{1,0:T(8,128)S(1)} collective-permute-done((f32[784,128]{1,0:T(8,128)S(1)}, f32[784,128]{1,0:T(8,128)S(1)}, u32[]{:S(2)}, u32[]{:S(2)}) %collective-permute-start) | collective-permute-done | bytes 401440 | tf_op jit(solution)/shard_map/ppermute | solution.py:565
  22.4 9.4 %collective-permute-done.1.r2 = f32[784,128]{1,0:T(8,128)S(1)} collective-permute-done((f32[784,128]{1,0:T(8,128)S(1)}, f32[784,128]{1,0:T(8,128)S(1)}, u32[]{:S(2)}, u32[]{:S(2)}) %collective-permute-start.1) | collective-permute-done | bytes 401440 | tf_op jit(solution)/shard_map/ppermute | solution.py:565
  31.8 6.8 %unpack.1 = (f32[3072,128]{1,0:T(8,128)S(1)}, f32[64,128]{1,0:T(8,128)S(1)}, f32[784,128]{1,0:T(8,128)S(1)}, f32[784,128]{1,0:T(8,128)S(1)}, f32[144,128]{1,0:T(8,128)S(1)}, /*index=5*/f32[144,128]{1,0:T(8,128)S(1)}) custom-call(s32[3]{0:T(128)S(1)} %pad_add_fusion.scal, f32[784,128]{1,0:T(8,128)S(1)} %get-tuple-element.45.r0, ...), custom_call_target="tpu_custom_call" | custom-call | tf_op jit(solution)/shard_map/unpack/pallas_call | solution.py:626
  38.6 1.3 collective-permute-start.3
  39.9 4.6 %collective-permute-start.4 = (f32[784,128]{1,0:T(8,128)S(1)}, f32[784,128]{1,0:T(8,128)S(1)}, u32[]{:S(2)}, u32[]{:S(2)}) collective-permute-start(f32[784,128]{1,0:T(8,128)S(1)} %get-tuple-element.52), channel_id=1, source_target_pairs={{0,4},{1,5},{2,6},{3,7},{4,8},{5,9},{6,10},{7,11},{8,12},{9,13},{1... | collective-permute-start | bytes 1204232 | tf_op jit(solution)/shard_map/ppermute | solution.py:577
  44.5 1.4 collective-permute-start.5
  45.9 1.9 %collective-permute-start.6 = (f32[144,128]{1,0:T(8,128)S(1)}, f32[144,128]{1,0:T(8,128)S(1)}, u32[]{:S(2)}, u32[]{:S(2)}) collective-permute-start(f32[144,128]{1,0:T(8,128)S(1)} %get-tuple-element.54), channel_id=1, source_target_pairs={{0,3},{1,2},{2,1},{3,0},{4,7},{5,6},{6,5},{7,4},{8,11},{9,10},{10,... | collective-permute-start | bytes 221192 | tf_op jit(solution)/shard_map/ppermute | solution.py:569
  48.9 2.5 %collective-permute-done.6.h_far.refs_7_ = f32[144,128]{1,0:T(8,128)S(1)} collective-permute-done((f32[144,128]{1,0:T(8,128)S(1)}, f32[144,128]{1,0:T(8,128)S(1)}, u32[]{:S(2)}, u32[]{:S(2)}) %collective-permute-start.6) | collective-permute-done | bytes 73760 | tf_op jit(solution)/shard_map/ppermute | solution.py:569
  51.8 6.9 %first.1 = (f32[3072,128]{1,0:T(8,128)S(1)}, f32[160,128]{1,0:T(8,128)S(1)}, f32[208,128]{1,0:T(8,128)S(1)}, f32[144,128]{1,0:T(8,128)S(1)}, f32[784,128]{1,0:T(8,128)S(1)}, /*index=5*/f32[784,128]{1,0:T(8,128)S(1)}) custom-call(s32[3]{0:T(128)S(1)} %pad_add_fusion.scal, f32[3072,128]{1,0:T(8,128)S(1)} %get-tuple-element.49.v_ref.refs_0_, ...), custom_call_target="tpu_custom_call" | custom-call | tf_op jit(solution)/shard_map/first/pallas_call | solution.py:631
  58.8 1.8 collective-permute-start.7
  60.5 1.3 collective-permute-start.11
  61.8 5.0 %collective-permute-start.12 = (f32[784,128]{1,0:T(8,128)S(1)}, f32[784,128]{1,0:T(8,128)S(1)}, u32[]{:S(2)}, u32[]{:S(2)}) collective-permute-start(f32[784,128]{1,0:T(8,128)S(1)} %get-tuple-element.60), channel_id=1, source_target_pairs={{0,4},{1,5},{2,6},{3,7},{4,8},{5,9},{6,10},{7,11},{8,12},{9,13},{1... | collective-permute-start | bytes 1204232 | tf_op jit(solution)/shard_map/ppermute | solution.py:577
  66.9 1.7 collective-permute-start.8
  68.6 4.3 %collective-permute-done.8.refs_11_ = f32[208,128]{1,0:T(8,128)S(1)} collective-permute-done((f32[208,128]{1,0:T(8,128)S(1)}, f32[208,128]{1,0:T(8,128)S(1)}, u32[]{:S(2)}, u32[]{:S(2)}) %collective-permute-start.8) | collective-permute-done | bytes 106528 | tf_op jit(solution)/shard_map/ppermute | solution.py:569
  72.9 2.0 %collective-permute-start.9 = (f32[64,128]{1,0:T(8,128)S(1)}, f32[64,128]{1,0:T(8,128)S(1)}, u32[]{:S(2)}, u32[]{:S(2)}) collective-permute-start(f32[64,128]{1,0:T(8,128)S(1)} %slice_add_fusion.2), channel_id=1, source_target_pairs={{0,4},{1,5},{2,6},{3,7},{4,0},{5,1},{6,2},{7,3},{8,12},{9,13},{10,... | collective-permute-start | bytes 98312 | tf_op jit(solution)/shard_map/ppermute | solution.py:573
  74.9 1.9 %collective-permute-done.9 = f32[64,128]{1,0:T(8,128)S(1)} collective-permute-done((f32[64,128]{1,0:T(8,128)S(1)}, f32[64,128]{1,0:T(8,128)S(1)}, u32[]{:S(2)}, u32[]{:S(2)}) %collective-permute-start.9) | collective-permute-done | bytes 32800 | tf_op jit(solution)/shard_map/ppermute | solution.py:573
  76.8 2.2 %collective-permute-start.10 = (f32[64,128]{1,0:T(8,128)S(1)}, f32[64,128]{1,0:T(8,128)S(1)}, u32[]{:S(2)}, u32[]{:S(2)}) collective-permute-start(f32[64,128]{1,0:T(8,128)S(1)} %add.50), channel_id=1, source_target_pairs={{0,12},{1,13},{2,14},{3,15},{4,8},{5,9},{6,10},{7,11},{8,4},{9,5},... | collective-permute-start | bytes 98312 | tf_op jit(solution)/shard_map/ppermute | solution.py:573
  79.0 3.0 %collective-permute-done.10 = f32[64,128]{1,0:T(8,128)S(1)} collective-permute-done((f32[64,128]{1,0:T(8,128)S(1)}, f32[64,128]{1,0:T(8,128)S(1)}, u32[]{:S(2)}, u32[]{:S(2)}) %collective-permute-start.10) | collective-permute-done | bytes 32800 | tf_op jit(solution)/shard_map/ppermute | solution.py:573
  82.0 2.5 %matrix.2.refs_3_ = bf16[128,256]{1,0:T(8,128)(2,1)S(1)} custom-call(f32[64,128]{1,0:T(8,128)S(1)} %add.51.grams), custom_call_target="tpu_custom_call" | custom-call | tf_op jit(solution)/shard_map/matrix/pallas_call | solution.py:641
  84.5 12.3 %step.1 = (f32[3072,128]{1,0:T(8,128)S(1)}, f32[3072,128]{1,0:T(8,128)S(1)}, f32[208,128]{1,0:T(8,128)S(1)}, f32[144,128]{1,0:T(8,128)S(1)}, f32[784,128]{1,0:T(...) custom-call(s32[3]{0:T(128)S(1)} %pad_add_fusion.scal, ...), custom_call_target="tpu_custom_call" | custom-call | tf_op jit(solution)/shard_map/step/pallas_call | solution.py:642
  96.9 1.3 collective-permute-start.17
  98.2 4.6 %collective-permute-start.18 = (f32[784,128]{1,0:T(8,128)S(1)}, f32[784,128]{1,0:T(8,128)S(1)}, u32[]{:S(2)}, u32[]{:S(2)}) collective-permute-start(f32[784,128]{1,0:T(8,128)S(1)} %get-tuple-element.70), channel_id=1, source_target_pairs={{0,4},{1,5},{2,6},{3,7},{4,8},{5,9},{6,10},{7,11},{8,12},{9,13},{1... | collective-permute-start | bytes 1204232 | tf_op jit(solution)/shard_map/ppermute | solution.py:577
  102.8 2.9 %collective-permute-start.14 = (f32[208,128]{1,0:T(8,128)S(1)}, f32[208,128]{1,0:T(8,128)S(1)}, u32[]{:S(2)}, u32[]{:S(2)}) collective-permute-start(f32[208,128]{1,0:T(8,128)S(1)} %pad_maximum_fusion.1), channel_id=1, source_target_pairs={{0,3},{1,2},{2,1},{3,0},{4,7},{5,6},{6,5},{7,4},{8,11},{9,10},{10,... | collective-permute-start | bytes 319496 | tf_op jit(solution)/shard_map/ppermute | solution.py:569
  105.7 3.1 %collective-permute-done.14.refs_11_ = f32[208,128]{1,0:T(8,128)S(1)} collective-permute-done((f32[208,128]{1,0:T(8,128)S(1)}, f32[208,128]{1,0:T(8,128)S(1)}, u32[]{:S(2)}, u32[]{:S(2)}) %collective-permute-start.14) | collective-permute-done | bytes 106528 | tf_op jit(solution)/shard_map/ppermute | solution.py:569
  109.6 3.1 %collective-permute-done.15 = f32[64,128]{1,0:T(8,128)S(1)} collective-permute-done((f32[64,128]{1,0:T(8,128)S(1)}, f32[64,128]{1,0:T(8,128)S(1)}, u32[]{:S(2)}, u32[]{:S(2)}) %collective-permute-start.15) | collective-permute-done | bytes 32800 | tf_op jit(solution)/shard_map/ppermute | solution.py:573
  113.7 4.2 %collective-permute-done.16 = f32[64,128]{1,0:T(8,128)S(1)} collective-permute-done((f32[64,128]{1,0:T(8,128)S(1)}, f32[64,128]{1,0:T(8,128)S(1)}, u32[]{:S(2)}, u32[]{:S(2)}) %collective-permute-start.16) | collective-permute-done | bytes 32800 | tf_op jit(solution)/shard_map/ppermute | solution.py:573
  117.9 2.5 %matrix.3.refs_3_ = bf16[128,256]{1,0:T(8,128)(2,1)S(1)} custom-call(f32[64,128]{1,0:T(8,128)S(1)} %add.55.grams), custom_call_target="tpu_custom_call" | custom-call | tf_op jit(solution)/shard_map/matrix/pallas_call | solution.py:653
  120.4 16.4 %last.1 = (f32[3072,128]{1,0:T(8,128)S(1)}, f32[768,128]{1,0:T(8,128)S(1)}, f32[64,128]{1,0:T(8,128)S(1)}, f32[768,128]{1,0:T(8,128)S(1)}, f32[768,128]{1,0:T(8,...) custom-call(s32[3]{0:T(128)S(1)} %pad_add_fusion.scal, f32[3072,128]{1,0:T(8,128)S(1)} %get-tuple-element.61.refs_0_, ...), custom_call_target="tpu_custom_call" | custom-call | tf_op jit(solution)/shard_map/last/pallas_call | solution.py:654
  137.6 1.9 %collective-permute-start.27 = (f32[768,128]{1,0:T(8,128)S(1)}, f32[768,128]{1,0:T(8,128)S(1)}, u32[]{:S(2)}, u32[]{:S(2)}) collective-permute-start(f32[768,128]{1,0:T(8,128)S(1)} %get-tuple-element.86), channel_id=1, source_target_pairs={{0,16},{16,32},{32,48},{48,64},{64,80},{80,96},{96,112},{112,128},... | collective-permute-start | bytes 1179656 | tf_op jit(solution)/shard_map/ppermute | solution.py:663
  140.7 2.8 %collective-permute-start.20 = (f32[64,128]{1,0:T(8,128)S(1)}, f32[64,128]{1,0:T(8,128)S(1)}, u32[]{:S(2)}, u32[]{:S(2)}) collective-permute-start(f32[64,128]{1,0:T(8,128)S(1)} %add.56), channel_id=1, source_target_pairs={{0,3},{1,2},{2,1},{3,0},{4,7},{5,6},{6,5},{7,4},{8,11},{9,10},{10,... | collective-permute-start | bytes 98312 | tf_op jit(solution)/shard_map/ppermute | solution.py:569
  143.5 2.3 %collective-permute-done.20 = f32[64,128]{1,0:T(8,128)S(1)} collective-permute-done((f32[64,128]{1,0:T(8,128)S(1)}, f32[64,128]{1,0:T(8,128)S(1)}, u32[]{:S(2)}, u32[]{:S(2)}) %collective-permute-start.20) | collective-permute-done | bytes 32800 | tf_op jit(solution)/shard_map/ppermute | solution.py:569
  145.9 4.2 %collective-permute-start.24 = (f32[768,128]{1,0:T(8,128)S(1)}, f32[768,128]{1,0:T(8,128)S(1)}, u32[]{:S(2)}, u32[]{:S(2)}) collective-permute-start(f32[768,128]{1,0:T(8,128)S(1)} %get-tuple-element.82), channel_id=1, source_target_pairs={{0,2},{1,3},{2,0},{3,1},{4,6},{5,7},{6,4},{7,5},{8,10},{9,11},{10,... | collective-permute-start | bytes 1179656 | tf_op jit(solution)/shard_map/ppermute | solution.py:565
  150.5 2.1 %collective-permute-start.28 = (f32[64,64]{1,0:T(8,128)S(1)}, f32[64,64]{1,0:T(8,128)S(1)}, u32[]{:S(2)}, u32[]{:S(2)}) collective-permute-start(f32[64,64]{1,0:T(8,128)S(1)} %off.1), channel_id=1, source_target_pairs={{0,4},{1,5},{2,6},{3,7},{4,0},{5,1},{6,2},{7,3},{8,12},{9,13},{10,... | collective-permute-start | bytes 49160 | tf_op jit(solution)/shard_map/ppermute | solution.py:573
  152.6 1.5 collective-permute-done.21
  154.7 2.7 %collective-permute-start.29 = (f32[64,64]{1,0:T(8,128)S(1)}, f32[64,64]{1,0:T(8,128)S(1)}, u32[]{:S(2)}, u32[]{:S(2)}) collective-permute-start(f32[64,64]{1,0:T(8,128)S(1)} %add.60), channel_id=1, source_target_pairs={{0,12},{1,13},{2,14},{3,15},{4,8},{5,9},{6,10},{7,11},{8,4},{9,5},... | collective-permute-start | bytes 49160 | tf_op jit(solution)/shard_map/ppermute | solution.py:573
  157.4 2.5 %collective-permute-done.29 = f32[64,64]{1,0:T(8,128)S(1)} collective-permute-done((f32[64,64]{1,0:T(8,128)S(1)}, f32[64,64]{1,0:T(8,128)S(1)}, u32[]{:S(2)}, u32[]{:S(2)}) %collective-permute-start.29) | collective-permute-done | bytes 16416 | tf_op jit(solution)/shard_map/ppermute | solution.py:573
  159.9 2.0 %collective-permute-start.30 = (f32[64,64]{1,0:T(8,128)S(1)}, f32[64,64]{1,0:T(8,128)S(1)}, u32[]{:S(2)}, u32[]{:S(2)}) collective-permute-start(f32[64,64]{1,0:T(8,128)S(1)} %add.61), channel_id=1, source_target_pairs={{0,1},{1,0},{2,3},{3,2},{4,5},{5,4},{6,7},{7,6},{8,9},{9,8},{10,11... | collective-permute-start | bytes 49160 | tf_op jit(solution)/shard_map/ppermute | solution.py:569
  161.9 2.8 %factor.1 = (f32[64,64]{1,0:T(8,128)S(1)}, f32[64,64]{1,0:T(8,128)}) custom-call(f32[64,128]{1,0:T(8,128)S(1)} %add.59.grams), custom_call_target="tpu_custom_call" | custom-call | tf_op jit(solution)/shard_map/factor/pallas_call | solution.py:668
  164.7 2.3 %collective-permute-done.30 = f32[64,64]{1,0:T(8,128)S(1)} collective-permute-done((f32[64,64]{1,0:T(8,128)S(1)}, f32[64,64]{1,0:T(8,128)S(1)}, u32[]{:S(2)}, u32[]{:S(2)}) %collective-permute-start.30) | collective-permute-done | bytes 16416 | tf_op jit(solution)/shard_map/ppermute | solution.py:569
  167.5 1.9 %collective-permute-start.26 = (f32[64,64]{1,0:T(8,128)S(1)}, f32[64,64]{1,0:T(8,128)S(1)}, u32[]{:S(2)}, u32[]{:S(2)}) collective-permute-start(f32[64,64]{1,0:T(8,128)S(1)} %get-tuple-element.79.factor), channel_id=1, source_target_pairs={{0,16},{16,32},{32,48},{48,64},{64,80},{80,96},{96,112},{112,128},... | collective-permute-start | bytes 49160 | tf_op jit(solution)/shard_map/ppermute | solution.py:670
  169.5 2.7 %collective-permute-done.31 = f32[64,64]{1,0:T(8,128)S(1)} collective-permute-done((f32[64,64]{1,0:T(8,128)S(1)}, f32[64,64]{1,0:T(8,128)S(1)}, u32[]{:S(2)}, u32[]{:S(2)}) %collective-permute-start.31) | collective-permute-done | bytes 16416 | tf_op jit(solution)/shard_map/ppermute | solution.py:569
  172.2 1.8 %collective-permute-done.26.other = f32[64,64]{1,0:T(8,128)S(1)} collective-permute-done((f32[64,64]{1,0:T(8,128)S(1)}, f32[64,64]{1,0:T(8,128)S(1)}, u32[]{:S(2)}, u32[]{:S(2)}) %collective-permute-start.26) | collective-permute-done | bytes 16416 | tf_op jit(solution)/shard_map/ppermute | solution.py:670
  175.0 6.4 %rows.1 = bf16[3072,128]{1,0:T(8,128)(2,1)} custom-call(s32[3]{0:T(128)S(1)} %pad_add_fusion.scal, f32[64,64]{1,0:T(8,128)S(1)} %get-tuple-element.79.factor, f32[768,128]{1,0:T(8,128)S(1)} %get-tuple-element.80.r0, f32[768,128]{1,0:T(8,128)S(1)} %collective-permute-done.23.r1, f32[768,128]{1,0:T(8,128)S(1)} %collective-permute-done.24.r2, ...), custom_call_target="tpu_custom_call" | custom-call | tf_op jit(solution)/shard_map/rows/pallas_call | solution.py:671
  (56 shorter events, 10.8 us)
Async XLA Ops:
  1.4 1.4 copy-start
  2.8 0.7 copy-start.1
  3.5 0.7 copy-start.2
  4.2 0.7 copy-start.3
  4.9 0.7 copy-start.4
  9.9 12.5 %collective-permute-start = (f32[784,128]{1,0:T(8,128)S(1)}, f32[784,128]{1,0:T(8,128)S(1)}, u32[]{:S(2)}, u32[]{:S(2)}) collective-permute-start(f32[784,128]{1,0:T(8,128)S(1)} %get-tuple-element.46), channel_id=1, source_target_pairs={{0,1},{1,2},{2,3},{3,0},{4,5},{5,6},{6,7},{7,4},{8,9},{9,10},{10,1... | collective-permute-start | bytes 1204232 | tf_op jit(solution)/shard_map/ppermute | solution.py:565
  11.5 20.3 %collective-permute-start.1 = (f32[784,128]{1,0:T(8,128)S(1)}, f32[784,128]{1,0:T(8,128)S(1)}, u32[]{:S(2)}, u32[]{:S(2)}) collective-permute-start(f32[784,128]{1,0:T(8,128)S(1)} %get-tuple-element.47), channel_id=1, source_target_pairs={{0,2},{1,3},{2,0},{3,1},{4,6},{5,7},{6,4},{7,5},{8,10},{9,11},{10,... | collective-permute-start | bytes 1204232 | tf_op jit(solution)/shard_map/ppermute | solution.py:565
  14.2 17.6 %collective-permute-start.2 = (f32[784,128]{1,0:T(8,128)S(1)}, f32[784,128]{1,0:T(8,128)S(1)}, u32[]{:S(2)}, u32[]{:S(2)}) collective-permute-start(f32[784,128]{1,0:T(8,128)S(1)} %get-tuple-element.48), channel_id=1, source_target_pairs={{0,3},{1,0},{2,1},{3,2},{4,7},{5,4},{6,5},{7,6},{8,11},{9,8},{10,9... | collective-permute-start | bytes 1204232 | tf_op jit(solution)/shard_map/ppermute | solution.py:565
  38.6 12.9 %collective-permute-start.3 = (f32[784,128]{1,0:T(8,128)S(1)}, f32[784,128]{1,0:T(8,128)S(1)}, u32[]{:S(2)}, u32[]{:S(2)}) collective-permute-start(f32[784,128]{1,0:T(8,128)S(1)} %get-tuple-element.51), channel_id=1, source_target_pairs={{4,0},{5,1},{6,2},{7,3},{8,4},{9,5},{10,6},{11,7},{12,8},{13,9},{1... | collective-permute-start | bytes 1204232 | tf_op jit(solution)/shard_map/ppermute | solution.py:578
  39.9 11.9 %collective-permute-start.4 = (f32[784,128]{1,0:T(8,128)S(1)}, f32[784,128]{1,0:T(8,128)S(1)}, u32[]{:S(2)}, u32[]{:S(2)}) collective-permute-start(f32[784,128]{1,0:T(8,128)S(1)} %get-tuple-element.52), channel_id=1, source_target_pairs={{0,4},{1,5},{2,6},{3,7},{4,8},{5,9},{6,10},{7,11},{8,12},{9,13},{1... | collective-permute-start | bytes 1204232 | tf_op jit(solution)/shard_map/ppermute | solution.py:577
  44.5 4.4 %collective-permute-start.5 = (f32[144,128]{1,0:T(8,128)S(1)}, f32[144,128]{1,0:T(8,128)S(1)}, u32[]{:S(2)}, u32[]{:S(2)}) collective-permute-start(f32[144,128]{1,0:T(8,128)S(1)} %get-tuple-element.53), channel_id=1, source_target_pairs={{0,1},{1,0},{2,3},{3,2},{4,5},{5,4},{6,7},{7,6},{8,9},{9,8},{10,11... | collective-permute-start | bytes 221192 | tf_op jit(solution)/shard_map/ppermute | solution.py:569
  45.9 5.6 %collective-permute-start.6 = (f32[144,128]{1,0:T(8,128)S(1)}, f32[144,128]{1,0:T(8,128)S(1)}, u32[]{:S(2)}, u32[]{:S(2)}) collective-permute-start(f32[144,128]{1,0:T(8,128)S(1)} %get-tuple-element.54), channel_id=1, source_target_pairs={{0,3},{1,2},{2,1},{3,0},{4,7},{5,6},{6,5},{7,4},{8,11},{9,10},{10,... | collective-permute-start | bytes 221192 | tf_op jit(solution)/shard_map/ppermute | solution.py:569
  58.8 8.1 %collective-permute-start.7 = (f32[208,128]{1,0:T(8,128)S(1)}, f32[208,128]{1,0:T(8,128)S(1)}, u32[]{:S(2)}, u32[]{:S(2)}) collective-permute-start(f32[208,128]{1,0:T(8,128)S(1)} %get-tuple-element.57), channel_id=1, source_target_pairs={{0,1},{1,0},{2,3},{3,2},{4,5},{5,4},{6,7},{7,6},{8,9},{9,8},{10,11... | collective-permute-start | bytes 319496 | tf_op jit(solution)/shard_map/ppermute | solution.py:569
  60.5 23.9 %collective-permute-start.11 = (f32[784,128]{1,0:T(8,128)S(1)}, f32[784,128]{1,0:T(8,128)S(1)}, u32[]{:S(2)}, u32[]{:S(2)}) collective-permute-start(f32[784,128]{1,0:T(8,128)S(1)} %get-tuple-element.59), channel_id=1, source_target_pairs={{4,0},{5,1},{6,2},{7,3},{8,4},{9,5},{10,6},{11,7},{12,8},{13,9},{1... | collective-permute-start | bytes 1204232 | tf_op jit(solution)/shard_map/ppermute | solution.py:578
  61.8 22.7 %collective-permute-start.12 = (f32[784,128]{1,0:T(8,128)S(1)}, f32[784,128]{1,0:T(8,128)S(1)}, u32[]{:S(2)}, u32[]{:S(2)}) collective-permute-start(f32[784,128]{1,0:T(8,128)S(1)} %get-tuple-element.60), channel_id=1, source_target_pairs={{0,4},{1,5},{2,6},{3,7},{4,8},{5,9},{6,10},{7,11},{8,12},{9,13},{1... | collective-permute-start | bytes 1204232 | tf_op jit(solution)/shard_map/ppermute | solution.py:577
  66.9 6.0 %collective-permute-start.8 = (f32[208,128]{1,0:T(8,128)S(1)}, f32[208,128]{1,0:T(8,128)S(1)}, u32[]{:S(2)}, u32[]{:S(2)}) collective-permute-start(f32[208,128]{1,0:T(8,128)S(1)} %pad_maximum_fusion), channel_id=1, source_target_pairs={{0,3},{1,2},{2,1},{3,0},{4,7},{5,6},{6,5},{7,4},{8,11},{9,10},{10,... | collective-permute-start | bytes 319496 | tf_op jit(solution)/shard_map/ppermute | solution.py:569
  72.9 3.9 %collective-permute-start.9 = (f32[64,128]{1,0:T(8,128)S(1)}, f32[64,128]{1,0:T(8,128)S(1)}, u32[]{:S(2)}, u32[]{:S(2)}) collective-permute-start(f32[64,128]{1,0:T(8,128)S(1)} %slice_add_fusion.2), channel_id=1, source_target_pairs={{0,4},{1,5},{2,6},{3,7},{4,0},{5,1},{6,2},{7,3},{8,12},{9,13},{10,... | collective-permute-start | bytes 98312 | tf_op jit(solution)/shard_map/ppermute | solution.py:573
  76.8 5.1 %collective-permute-start.10 = (f32[64,128]{1,0:T(8,128)S(1)}, f32[64,128]{1,0:T(8,128)S(1)}, u32[]{:S(2)}, u32[]{:S(2)}) collective-permute-start(f32[64,128]{1,0:T(8,128)S(1)} %add.50), channel_id=1, source_target_pairs={{0,12},{1,13},{2,14},{3,15},{4,8},{5,9},{6,10},{7,11},{8,4},{9,5},... | collective-permute-start | bytes 98312 | tf_op jit(solution)/shard_map/ppermute | solution.py:573
  96.8 6.0 %collective-permute-start.13 = (f32[208,128]{1,0:T(8,128)S(1)}, f32[208,128]{1,0:T(8,128)S(1)}, u32[]{:S(2)}, u32[]{:S(2)}) collective-permute-start(f32[208,128]{1,0:T(8,128)S(1)} %get-tuple-element.63), channel_id=1, source_target_pairs={{0,1},{1,0},{2,3},{3,2},{4,5},{5,4},{6,7},{7,6},{8,9},{9,8},{10,11... | collective-permute-start | bytes 319496 | tf_op jit(solution)/shard_map/ppermute | solution.py:569
  96.9 23.5 %collective-permute-start.17 = (f32[784,128]{1,0:T(8,128)S(1)}, f32[784,128]{1,0:T(8,128)S(1)}, u32[]{:S(2)}, u32[]{:S(2)}) collective-permute-start(f32[784,128]{1,0:T(8,128)S(1)} %get-tuple-element.69), channel_id=1, source_target_pairs={{4,0},{5,1},{6,2},{7,3},{8,4},{9,5},{10,6},{11,7},{12,8},{13,9},{1... | collective-permute-start | bytes 1204232 | tf_op jit(solution)/shard_map/ppermute | solution.py:578
  98.2 22.2 %collective-permute-start.18 = (f32[784,128]{1,0:T(8,128)S(1)}, f32[784,128]{1,0:T(8,128)S(1)}, u32[]{:S(2)}, u32[]{:S(2)}) collective-permute-start(f32[784,128]{1,0:T(8,128)S(1)} %get-tuple-element.70), channel_id=1, source_target_pairs={{0,4},{1,5},{2,6},{3,7},{4,8},{5,9},{6,10},{7,11},{8,12},{9,13},{1... | collective-permute-start | bytes 1204232 | tf_op jit(solution)/shard_map/ppermute | solution.py:577
  102.8 6.0 %collective-permute-start.14 = (f32[208,128]{1,0:T(8,128)S(1)}, f32[208,128]{1,0:T(8,128)S(1)}, u32[]{:S(2)}, u32[]{:S(2)}) collective-permute-start(f32[208,128]{1,0:T(8,128)S(1)} %pad_maximum_fusion.1), channel_id=1, source_target_pairs={{0,3},{1,2},{2,1},{3,0},{4,7},{5,6},{6,5},{7,4},{8,11},{9,10},{10,... | collective-permute-start | bytes 319496 | tf_op jit(solution)/shard_map/ppermute | solution.py:569
  108.8 3.9 %collective-permute-start.15 = (f32[64,128]{1,0:T(8,128)S(1)}, f32[64,128]{1,0:T(8,128)S(1)}, u32[]{:S(2)}, u32[]{:S(2)}) collective-permute-start(f32[64,128]{1,0:T(8,128)S(1)} %slice_add_fusion), channel_id=1, source_target_pairs={{0,4},{1,5},{2,6},{3,7},{4,0},{5,1},{6,2},{7,3},{8,12},{9,13},{10,... | collective-permute-start | bytes 98312 | tf_op jit(solution)/shard_map/ppermute | solution.py:573
  112.7 5.1 %collective-permute-start.16 = (f32[64,128]{1,0:T(8,128)S(1)}, f32[64,128]{1,0:T(8,128)S(1)}, u32[]{:S(2)}, u32[]{:S(2)}) collective-permute-start(f32[64,128]{1,0:T(8,128)S(1)} %add.54), channel_id=1, source_target_pairs={{0,12},{1,13},{2,14},{3,15},{4,8},{5,9},{6,10},{7,11},{8,4},{9,5},... | collective-permute-start | bytes 98312 | tf_op jit(solution)/shard_map/ppermute | solution.py:573
  136.8 4.0 %collective-permute-start.19 = (f32[64,128]{1,0:T(8,128)S(1)}, f32[64,128]{1,0:T(8,128)S(1)}, u32[]{:S(2)}, u32[]{:S(2)}) collective-permute-start(f32[64,128]{1,0:T(8,128)S(1)} %get-tuple-element.73), channel_id=1, source_target_pairs={{0,1},{1,0},{2,3},{3,2},{4,5},{5,4},{6,7},{7,6},{8,9},{9,8},{10,11... | collective-permute-start | bytes 98312 | tf_op jit(solution)/shard_map/ppermute | solution.py:569
  137.6 12.5 %collective-permute-start.27 = (f32[768,128]{1,0:T(8,128)S(1)}, f32[768,128]{1,0:T(8,128)S(1)}, u32[]{:S(2)}, u32[]{:S(2)}) collective-permute-start(f32[768,128]{1,0:T(8,128)S(1)} %get-tuple-element.86), channel_id=1, source_target_pairs={{0,16},{16,32},{32,48},{48,64},{64,80},{80,96},{96,112},{112,128},... | collective-permute-start | bytes 1179656 | tf_op jit(solution)/shard_map/ppermute | solution.py:663
  140.7 5.1 %collective-permute-start.20 = (f32[64,128]{1,0:T(8,128)S(1)}, f32[64,128]{1,0:T(8,128)S(1)}, u32[]{:S(2)}, u32[]{:S(2)}) collective-permute-start(f32[64,128]{1,0:T(8,128)S(1)} %add.56), channel_id=1, source_target_pairs={{0,3},{1,2},{2,1},{3,0},{4,7},{5,6},{6,5},{7,4},{8,11},{9,10},{10,... | collective-permute-start | bytes 98312 | tf_op jit(solution)/shard_map/ppermute | solution.py:569
  145.9 29.1 %collective-permute-start.23 = (f32[768,128]{1,0:T(8,128)S(1)}, f32[768,128]{1,0:T(8,128)S(1)}, u32[]{:S(2)}, u32[]{:S(2)}) collective-permute-start(f32[768,128]{1,0:T(8,128)S(1)} %get-tuple-element.81), channel_id=1, source_target_pairs={{0,1},{1,2},{2,3},{3,0},{4,5},{5,6},{6,7},{7,4},{8,9},{9,10},{10,1... | collective-permute-start | bytes 1179656 | tf_op jit(solution)/shard_map/ppermute | solution.py:565
  145.9 29.1 %collective-permute-start.24 = (f32[768,128]{1,0:T(8,128)S(1)}, f32[768,128]{1,0:T(8,128)S(1)}, u32[]{:S(2)}, u32[]{:S(2)}) collective-permute-start(f32[768,128]{1,0:T(8,128)S(1)} %get-tuple-element.82), channel_id=1, source_target_pairs={{0,2},{1,3},{2,0},{3,1},{4,6},{5,7},{6,4},{7,5},{8,10},{9,11},{10,... | collective-permute-start | bytes 1179656 | tf_op jit(solution)/shard_map/ppermute | solution.py:565
  150.1 24.9 %collective-permute-start.25 = (f32[768,128]{1,0:T(8,128)S(1)}, f32[768,128]{1,0:T(8,128)S(1)}, u32[]{:S(2)}, u32[]{:S(2)}) collective-permute-start(f32[768,128]{1,0:T(8,128)S(1)} %get-tuple-element.83), channel_id=1, source_target_pairs={{0,3},{1,0},{2,1},{3,2},{4,7},{5,4},{6,5},{7,6},{8,11},{9,8},{10,9... | collective-permute-start | bytes 1179656 | tf_op jit(solution)/shard_map/ppermute | solution.py:565
  150.1 3.9 %collective-permute-start.21 = (f32[64,128]{1,0:T(8,128)S(1)}, f32[64,128]{1,0:T(8,128)S(1)}, u32[]{:S(2)}, u32[]{:S(2)}) collective-permute-start(f32[64,128]{1,0:T(8,128)S(1)} %add.57), channel_id=1, source_target_pairs={{0,4},{1,5},{2,6},{3,7},{4,0},{5,1},{6,2},{7,3},{8,12},{9,13},{10,... | collective-permute-start | bytes 98312 | tf_op jit(solution)/shard_map/ppermute | solution.py:573
  150.5 4.2 %collective-permute-start.28 = (f32[64,64]{1,0:T(8,128)S(1)}, f32[64,64]{1,0:T(8,128)S(1)}, u32[]{:S(2)}, u32[]{:S(2)}) collective-permute-start(f32[64,64]{1,0:T(8,128)S(1)} %off.1), channel_id=1, source_target_pairs={{0,4},{1,5},{2,6},{3,7},{4,0},{5,1},{6,2},{7,3},{8,12},{9,13},{10,... | collective-permute-start | bytes 49160 | tf_op jit(solution)/shard_map/ppermute | solution.py:573
  154.0 7.9 %collective-permute-start.22 = (f32[64,128]{1,0:T(8,128)S(1)}, f32[64,128]{1,0:T(8,128)S(1)}, u32[]{:S(2)}, u32[]{:S(2)}) collective-permute-start(f32[64,128]{1,0:T(8,128)S(1)} %add.58), channel_id=1, source_target_pairs={{0,12},{1,13},{2,14},{3,15},{4,8},{5,9},{6,10},{7,11},{8,4},{9,5},... | collective-permute-start | bytes 98312 | tf_op jit(solution)/shard_map/ppermute | solution.py:573
  154.7 5.2 %collective-permute-start.29 = (f32[64,64]{1,0:T(8,128)S(1)}, f32[64,64]{1,0:T(8,128)S(1)}, u32[]{:S(2)}, u32[]{:S(2)}) collective-permute-start(f32[64,64]{1,0:T(8,128)S(1)} %add.60), channel_id=1, source_target_pairs={{0,12},{1,13},{2,14},{3,15},{4,8},{5,9},{6,10},{7,11},{8,4},{9,5},... | collective-permute-start | bytes 49160 | tf_op jit(solution)/shard_map/ppermute | solution.py:573
  159.9 7.1 %collective-permute-start.30 = (f32[64,64]{1,0:T(8,128)S(1)}, f32[64,64]{1,0:T(8,128)S(1)}, u32[]{:S(2)}, u32[]{:S(2)}) collective-permute-start(f32[64,64]{1,0:T(8,128)S(1)} %add.61), channel_id=1, source_target_pairs={{0,1},{1,0},{2,3},{3,2},{4,5},{5,4},{6,7},{7,6},{8,9},{9,8},{10,11... | collective-permute-start | bytes 49160 | tf_op jit(solution)/shard_map/ppermute | solution.py:569
  167.0 5.1 %collective-permute-start.31 = (f32[64,64]{1,0:T(8,128)S(1)}, f32[64,64]{1,0:T(8,128)S(1)}, u32[]{:S(2)}, u32[]{:S(2)}) collective-permute-start(f32[64,64]{1,0:T(8,128)S(1)} %add.62), channel_id=1, source_target_pairs={{0,3},{1,2},{2,1},{3,0},{4,7},{5,6},{6,5},{7,4},{8,11},{9,10},{10,... | collective-permute-start | bytes 49160 | tf_op jit(solution)/shard_map/ppermute | solution.py:569
  167.5 6.4 %collective-permute-start.26 = (f32[64,64]{1,0:T(8,128)S(1)}, f32[64,64]{1,0:T(8,128)S(1)}, u32[]{:S(2)}, u32[]{:S(2)}) collective-permute-start(f32[64,64]{1,0:T(8,128)S(1)} %get-tuple-element.79.factor), channel_id=1, source_target_pairs={{0,16},{16,32},{32,48},{48,64},{64,80},{80,96},{96,112},{112,128},... | collective-permute-start | bytes 49160 | tf_op jit(solution)/shard_map/ppermute | solution.py:670

commit v3 on v2

v3 whole, which is shorter than its diff:
```python
import functools

import jax
import jax.numpy as jnp
from jax import lax
from jax.experimental import pallas as pl
from jax.experimental.pallas import tpu as pltpu
from jax.sharding import PartitionSpec as P


OV = 4
K = 64
NX = 16
LANES = 128
SLABS = 3 * NX
GROUPS = SLABS // 4
FROWS = GROUPS * K
YROWS = FROWS + NX
ZROWS = 3 * K + 2 * NX
F32 = jnp.float32
BF16 = jnp.bfloat16

VM = pl.BlockSpec(memory_space=pltpu.VMEM)
SM = pl.BlockSpec(memory_space=pltpu.SMEM)
PARAMS = pltpu.CompilerParams(vmem_limit_bytes=20 << 20)

FX, FXL, FY, FYL, FZ, FZL, DINV, BW, MASS, UN = range(10)


def f32(*shape):
    return jax.ShapeDtypeStruct(shape, F32)


def lanes(rows):
    return lax.broadcasted_iota(jnp.int32, (rows, LANES), 1)


def roll(x, shift):
    if isinstance(shift, int):
        shift = shift % LANES
        return x if shift == 0 else pltpu.roll(x, shift, 1)
    return pltpu.roll(x, shift, 1)


def unity_of(plane, active):
    value = jnp.minimum(plane + 1, active - plane).astype(F32) / (OV + 1)
    return jnp.clip(value, 0.0, 1.0)


def halves(x):
    high = x.astype(BF16)
    return high, (x - high.astype(F32)).astype(BF16)


def slab(ref, index):
    return ref[pl.ds(pl.multiple_of(index * K, K), K), :]


def put(ref, index, value):
    ref[pl.ds(pl.multiple_of(index * K, K), K), :] = value


def swap_blocks(v):
    block = lanes(v[0].shape[0]) >> 5
    odd, high = (block & 1) == 1, block >= 2
    w0 = jnp.where(odd, roll(v[1], 32), v[0])
    w1 = jnp.where(odd, v[1], roll(v[0], -32))
    w2 = jnp.where(odd, roll(v[3], 32), v[2])
    w3 = jnp.where(odd, v[3], roll(v[2], -32))
    return [
        jnp.where(high, roll(w2, 64), w0),
        jnp.where(high, roll(w3, 64), w1),
        jnp.where(high, w2, roll(w0, -64)),
        jnp.where(high, w3, roll(w1, -64)),
    ]


def turn(items, by):
    items = [jnp.where((by & 1) == 1, items[(i + 1) % 4], items[i]) for i in range(4)]
    return [jnp.where(by >= 2, items[(i + 2) % 4], items[i]) for i in range(4)]


def pack_kernel(scal, v_hbm, fx_hbm, fy_hbm, fz_hbm, m_hbm, p0, p1, p2, p3, v_ref, fx, fy, fz, m, v_sem, f_sem):
    active, px, row = scal[0], scal[1], scal[2]
    whole = K * NX

    def v_copy(c):
        return pltpu.make_async_copy(v_hbm.at[pl.ds(c * whole, whole), :], v_ref.at[pl.ds(c * whole, whole), :], v_sem.at[c])

    for c in range(3):
        v_copy(c).start()
    copies = [
        pltpu.make_async_copy(src, dst, f_sem.at[j])
        for j, (src, dst) in enumerate(((fx_hbm, fx), (fy_hbm, fy), (fz_hbm, fz), (m_hbm, m)))
    ]
    for copy in copies:
        copy.start()
    outs_ref = (p0, p1, p2, p3)

    def body(t, carry):
        c, big = t >> 2, t & 3
        values = []
        for xx in range(4):
            plane = big * 4 + xx
            s = v_ref[pl.ds(c * whole + plane, K, stride=NX), :]
            values.append(jnp.where(plane < active, s, 0.0))
        for d, value in enumerate(turn(swap_blocks(values), px)):
            put(outs_ref[d], t, value)
        return carry

    for c in range(3):
        v_copy(c).wait()
        lax.fori_loop(c * 4, c * 4 + 4, body, 0)
    for copy in copies:
        copy.wait()
    plane = lax.broadcasted_iota(jnp.int32, (NX, LANES), 0)
    depth = lanes(NX)
    inside = plane < active
    fx[...] = jnp.where(plane + 1 < active, fx[...], 0.0)
    fy[...] = jnp.where(inside & (row + 1 < 16), fy[...], 0.0)
    fz[...] = jnp.where(inside & (depth + 1 < LANES), fz[...], 0.0)
    for j, field in enumerate((fx, fy, fz, m)):
        values = [field[pl.ds(xx, 4, stride=4), :] for xx in range(4)]
        for d, value in enumerate(turn(swap_blocks(values), px)):
            outs_ref[d][pl.ds(FROWS + 4 * j, 4), :] = value


def edges(t, values, z_ref, base):
    part = lanes(K) & 31
    ends = None
    for r in range(4):
        moved = roll(values[r], 8 * r)
        here = (part == 8 * r) | (part == (8 * r + 31) % 32)
        ends = jnp.where(here, moved, 0.0 if r == 0 else ends)
    c, big = t >> 2, t & 3
    at = pl.ds(pl.multiple_of(base + c * K, 8), K)
    z_ref[at, :] = jnp.where(big == 0, 0.0, z_ref[at, :]) + roll(ends, big * 2)


def unpack_kernel(scal, r0, r1, r2, r3, b0, b1, b2, b3, z_ref):
    back = (4 - scal[1]) & 3
    refs = (r0, r3, r2, r1)
    outs = (b0, b1, b2, b3)

    def body(t, carry):
        values = turn([slab(r, t) for r in refs], back)
        for r in range(4):
            put(outs[r], t, values[r])
        edges(t, values, z_ref, 0)
        return carry

    lax.fori_loop(0, GROUPS, body, 0)
    values = turn([r[pl.ds(FROWS, NX), :] for r in refs], back)
    for r in range(4):
        outs[r][pl.ds(FROWS, NX), :] = values[r]
        z_ref[pl.ds(3 * K + 4 * r, 4), :] = values[r][8:12, :]
    z_ref[pl.ds(3 * K + NX, NX), :] = jnp.zeros((NX, LANES), F32)


def line(fld, which, r, big):
    return fld[pl.ds(which * NX + 4 * r + big, 1), :]


def join_columns(h_before, h_after, hz):
    before = h_before[pl.ds(h_before.shape[0] - ZROWS, ZROWS), :]
    after = h_after[pl.ds(h_after.shape[0] - ZROWS, ZROWS), :]
    hz[...] = jnp.where((lanes(ZROWS) & 1) == 0, after, roll(before, -62))


def stencils(t, v_refs, fld, h_up, h_dn, hz):
    c, big = t >> 2, t & 3
    lane = lanes(K)
    block, part = lane >> 5, lane & 31
    ends = roll(slab(hz, c), (LANES - 2 * big) & 127)
    vs = [slab(ref, t) for ref in v_refs]
    outs = []
    for r in range(4):
        v = vs[r]
        up = slab(h_up, t) if r == 3 else vs[r + 1]
        dn = slab(h_dn, t) if r == 0 else vs[r - 1]
        lo = roll(jnp.where(block == 3, slab(v_refs[r], jnp.maximum(t - 1, 0)), v), 32)
        hi = roll(jnp.where(block == 0, slab(v_refs[r], jnp.minimum(t + 1, GROUPS - 1)), v), -32)
        side = roll(ends, 31 - 8 * r)
        zp = jnp.where(part == 31, side, roll(v, -1))
        zm = jnp.where(part == 0, side, roll(v, 1))
        out = line(fld, FY, r, big) * (v - up) + line(fld, FYL, r, big) * (v - dn)
        out += line(fld, FX, r, big) * (v - hi) + line(fld, FXL, r, big) * (v - lo)
        out += line(fld, FZ, r, big) * (v - zp) + line(fld, FZL, r, big) * (v - zm)
        outs.append(out)
    return vs, outs


def add_gram(acc, lefts, mids, rights):
    for pair in (0, 2):
        left, right = [], []
        for xx in (pair, pair + 1):
            left.append(jnp.concatenate(halves(mids[xx]) + halves(rights[xx]), axis=0))
            right.append(jnp.concatenate(halves(lefts[xx]), axis=0))
        acc[...] += lax.dot_general(
            jnp.concatenate(left, axis=1),
            jnp.concatenate(right, axis=1),
            (((1,), (1,)), ((), ())),
            preferred_element_type=F32,
        )


def finish_gram(acc, out):
    half = acc[:, 0:K] + acc[:, K : 2 * K]
    out[0:K, 0:K] = half[0:K] + half[K : 2 * K]
    out[0:K, K : 2 * K] = half[2 * K : 3 * K] + half[3 * K : 4 * K]


def first_kernel(
    scal, b0, b1, b2, b3, h_up, h_dn, h_before, h_after, a0, a1, a2, a3, fld, near, hz, acc
):
    join_columns(h_before, h_after, hz)
    active = scal[0]
    v_refs, outs = (b0, b1, b2, b3), (a0, a1, a2, a3)
    lane = lanes(NX)
    row = lax.broadcasted_iota(jnp.int32, (NX, LANES), 0)
    plane = 4 * (row & 3) + (lane >> 5)
    fx, fy, fz, m = (
        jnp.concatenate([ref[FROWS + 4 * j : FROWS + 4 * j + 4, :] for ref in v_refs], axis=0) for j in range(4)
    )
    fxl = roll(jnp.where(lane >= 96, jnp.where((row & 3) == 0, 0.0, pltpu.roll(fx, 1, 0)), fx), 32)
    fyl = jnp.concatenate([h_dn[FROWS + 4 : FROWS + 8, :], fy[0:12, :]], axis=0)
    fzl = jnp.where((lane & 31) == 0, roll(hz[3 * K : 3 * K + NX, :], 31), roll(fz, 1))
    dinv = 1.0 / (fx + fxl + fy + fyl + fz + fzl + m)
    u = unity_of(plane, active)
    weight = m * u * u
    for j, value in enumerate((fx, fxl, fy, fyl, fz, fzl, dinv, weight, m, u)):
        fld[j * NX : (j + 1) * NX, :] = value
    for r in range(4):
        outs[r][pl.ds(FROWS, 4), :] = dinv[4 * r : 4 * r + 4, :]
        outs[r][pl.ds(FROWS + 4, 4), :] = weight[4 * r : 4 * r + 4, :]
        outs[r][pl.ds(FROWS + 8, 8), :] = jnp.zeros((8, LANES), F32)
    near[pl.ds(4 * K, NX), :] = dinv
    near[pl.ds(4 * K + NX, NX), :] = weight
    acc[...] = jnp.zeros_like(acc)

    def body(t, carry):
        vs, avs = stencils(t, v_refs, fld, h_up, h_dn, hz)
        for r in range(4):
            put(outs[r], t, avs[r])
        edges(t, avs, near, K)
        add_gram(acc, vs, [v * line(fld, BW, r, t & 3) for r, v in enumerate(vs)], avs)
        return carry

    lax.fori_loop(0, GROUPS, body, 0)
    finish_gram(acc, near)


def mixed(matrix, v, av, dinv, weight):
    y = v - 0.5 * (av * dinv)
    w = v * (weight * dinv)
    both = lax.dot_general(
        matrix,
        jnp.concatenate(halves(y) + halves(w), axis=0),
        (((1,), (0,)), ((), ())),
        preferred_element_type=F32,
    )
    return both[0:K, :] + both[K : 2 * K, :]


def step_kernel(last, scal, *refs):
    v_refs, a_refs = refs[0:4], refs[4:8]
    fld, mat, hv_up, hv_dn, hv_z, ha_up, ha_dn, ha_before, ha_after = refs[8:17]
    if last:
        rows, img_ref, grams = refs[17:20]
        outs_ref = refs[20:24]
        acc, ha_z, n_up, n_dn, n_z = refs[24:29]
        new_refs, image_refs = refs[29:33], refs[33:37]
    else:
        new_refs, image_refs = refs[17:21], refs[21:25]
        near, n_up, n_dn, n_z, rows, acc, ha_z = refs[25:]
    active, px = scal[0], scal[1]
    join_columns(ha_before, ha_after, ha_z)
    matrix = mat[...]
    one = lanes(1)
    if not last:
        rows[0:8, :] = ha_up[FROWS : FROWS + 8, :]
        rows[8:16, :] = ha_dn[FROWS : FROWS + 8, :]
        for which in range(2):
            out = None
            for e in range(NX):
                at = 3 * K + which * NX + e
                moved = roll(ha_z[at : at + 1, :], 2 * e)
                out = moved if e == 0 else jnp.where((one & 30) == 2 * e, moved, out)
            rows[16 + which : 17 + which, :] = out
    acc[...] = jnp.zeros_like(acc)

    def new_own(t, carry):
        big = t & 3
        for r in range(4):
            value = mixed(
                matrix, slab(v_refs[r], t), slab(a_refs[r], t), line(fld, DINV, r, big), line(fld, BW, r, big)
            )
            if last:
                value = value * line(fld, UN, r, big)
            put(new_refs[r], t, value)
        return carry

    lax.fori_loop(0, GROUPS, new_own, 0, unroll=2)
    block = one >> 5

    def new_side(t, carry):
        big = t & 3
        for start, target, hv, ha in ((0, n_up, hv_up, ha_up), (8, n_dn, hv_dn, ha_dn)):
            value = mixed(
                matrix, slab(hv, t), slab(ha, t), rows[pl.ds(start + big, 1), :], rows[pl.ds(start + 4 + big, 1), :]
            )
            if last:
                value = value * unity_of(big * 4 + block, active)
            put(target, t, value)
        return carry

    lax.fori_loop(0, GROUPS, new_side, 0, unroll=2)
    for c in range(3):
        value = mixed(matrix, slab(hv_z, c), slab(ha_z, c), rows[16:17, :], rows[17:18, :])
        if last:
            xx = jnp.where((one & 1) == 0, block, (block + 1) & 3)
            value = value * unity_of(4 * (((one & 31) >> 1) & 3) + xx, active)
        put(n_z, c, value)

    def body(t, carry):
        vs, avs = stencils(t, new_refs, fld, n_up, n_dn, n_z)
        for r in range(4):
            put(image_refs[r], t, avs[r])
        if last:
            for d, value in enumerate(turn(vs, px)):
                put(outs_ref[d], t, value)
        else:
            edges(t, avs, near, K)
        weight = MASS if last else BW
        add_gram(acc, vs, [v * line(fld, weight, r, t & 3) for r, v in enumerate(vs)], avs)
        return carry

    lax.fori_loop(0, GROUPS, body, 0)
    if last:
        finish_gram(acc, grams)
        start = active - OV
        group, skip = start >> 2, start & 3
        late = (lanes(K) >> 5) < skip
        for c in range(3):
            values = []
            for r in range(4):
                here = slab(image_refs[r], c * 4 + group)
                after = slab(image_refs[r], jnp.minimum(c * 4 + group + 1, GROUPS - 1))
                values.append(roll(jnp.where(late, after, here), ((4 - skip) & 3) * 32))
            for d, value in enumerate(turn(values, px)):
                put(img_ref, d * 3 + c, value)
    else:
        for r in range(4):
            image_refs[r][pl.ds(FROWS, NX), :] = jnp.zeros((NX, LANES), F32)
            new_refs[r][pl.ds(FROWS, NX), :] = jnp.zeros((NX, LANES), F32)
        near[pl.ds(4 * K, 2 * NX), :] = jnp.zeros((2 * NX, LANES), F32)
        finish_gram(acc, near)


def small_dot(a, b, dims=((1,), (0,))):
    return lax.dot_general(a, b, (dims, ((), ())), precision=lax.Precision.HIGHEST, preferred_element_type=F32)


def inverse_factor(gram):
    row = lax.broadcasted_iota(jnp.int32, (8, LANES), 0)
    lane = lanes(8)

    def one_row(x, at):
        return jnp.broadcast_to(x[at : at + 1, :], (8, LANES))

    def one_column(x, at):
        return jnp.broadcast_to(x[:, at : at + 1], (8, LANES))

    parts = []
    for g in range(8):
        left = jnp.concatenate([gram[g * 8 : g * 8 + 8, :], jnp.zeros((8, K), F32)], axis=1)
        parts.append(jnp.where(lane == row + (g * 8 + K), 1.0, left))
    pivots = [None] * 8
    for g0 in range(8):
        top = parts[g0]
        columns = [one_column(top, g0 * 8 + j) for j in range(8)]
        inverse, lines, ahead = [], [], []
        for j in range(8):
            pivot = one_row(columns[j], j)
            line_j = one_row(top, j)
            pivots[g0] = pivot if j == 0 else jnp.where(row == j, pivot, pivots[g0])
            inv = 1.0 / pivot
            factor = jnp.where(row > j, columns[j] * inv, 0.0)
            after = [one_row(columns[k], j) for k in range(j + 1, 8)]
            for k in range(j + 1, 8):
                columns[k] = columns[k] - factor * after[k - j - 1]
            top = top - factor * line_j
            inverse.append(inv)
            lines.append(line_j)
            ahead.append(after)
        parts[g0] = top
        for g in range(g0 + 1, 8):
            part = parts[g]
            columns = [one_column(part, g0 * 8 + j) for j in range(8)]
            for j in range(8):
                factor = columns[j] * inverse[j]
                for k in range(j + 1, 8):
                    columns[k] = columns[k] - factor * ahead[j][k - j - 1]
                part = part - factor * lines[j]
            parts[g] = part
    return jnp.concatenate([(parts[g] * lax.rsqrt(pivots[g]))[:, K:] for g in range(8)], axis=0)


def matrix_kernel(grams, mat):
    both = grams[0:K, :]
    factor = inverse_factor(both[:, 0:K])
    image = small_dot(factor, both[:, K : 2 * K], ((1,), (1,)))
    rayleigh = small_dot(image, factor, ((1,), (1,)))
    other = 0.5 * small_dot(rayleigh, factor, ((0,), (0,)))
    fh, fl = halves(factor)
    oh, ol = halves(other)
    mat[...] = jnp.concatenate(
        [jnp.concatenate([fh, fh, oh, oh], axis=1), jnp.concatenate([fl, fl, ol, ol], axis=1)], axis=0
    )


def factor_kernel(grams, factor_ref, diag_ref):
    both = grams[...]
    factor = inverse_factor(both[:, 0:K])
    factor_ref[...] = factor
    image = small_dot(factor, both[:, K : 2 * K], ((1,), (1,)))
    diag_ref[...] = small_dot(image, factor, ((1,), (1,)))


def cross_kernel(factor, other, raw, out):
    out[...] = small_dot(small_dot(factor[...], raw[:, 0:K]), other[...], ((1,), (1,)))


def off_kernel(w0, w1, w2, w3, img_ref, out):
    acc = jnp.zeros((2 * K, 2 * K), F32)
    for c in range(3):
        for pair in (0, 2):
            left, right = [], []
            for r in (pair, pair + 1):
                left.append(jnp.concatenate(halves(slab((w0, w1, w2, w3)[r], c * 4)), axis=0))
                right.append(jnp.concatenate(halves(slab(img_ref, r * 3 + c)), axis=0))
            acc += lax.dot_general(
                jnp.concatenate(left, axis=1),
                jnp.concatenate(right, axis=1),
                (((1,), (1,)), ((), ())),
                preferred_element_type=F32,
            )
    half = acc[0:K, :] + acc[K : 2 * K, :]
    out[:, 0:K] = half[:, 0:K] + half[:, K : 2 * K]
    out[:, K : 2 * K] = jnp.zeros((K, K), F32)


def out_kernel(scal, factor, r0, r1, r2, r3, out_ref, hold):
    back = (4 - scal[1]) & 3
    refs = (r0, r3, r2, r1)
    fh, fl = halves(factor[...])
    matrix = jnp.concatenate([jnp.concatenate([fh, fh], axis=1), jnp.concatenate([fl, fl], axis=1)], axis=0)

    def body(t, carry):
        c, big = t >> 2, t & 3
        values = swap_blocks(turn([slab(r, t) for r in refs], back))
        for xx in range(4):
            both = lax.dot_general(
                matrix, jnp.concatenate(halves(values[xx]), axis=0), (((1,), (0,)), ((), ())), preferred_element_type=F32
            )
            hold[pl.ds(c * (K * NX) + big * 4 + xx, K, stride=NX), :] = both[0:K, :] + both[K : 2 * K, :]
        return carry

    lax.fori_loop(0, GROUPS, body, 0)

    def cast(i, carry):
        at = pl.ds(pl.multiple_of(i * 128, 128), 128)
        out_ref[at, :] = hold[at, :].astype(BF16)
        return carry

    lax.fori_loop(0, 3 * K * NX // 128, cast, 0)


def call(kernel, n_in, shapes, scratch=(), first=VM, rest=VM, params=PARAMS):
    return pl.pallas_call(
        kernel,
        out_shape=shapes,
        in_specs=[first] + [rest] * (n_in - 1),
        out_specs=jax.tree.map(lambda _: VM, shapes),
        scratch_shapes=list(scratch),
        compiler_params=params,
    )


def shift_x(value, d):
    return lax.ppermute(value, "dom", [(i, (i & 12) + ((i + d) & 3)) for i in range(16)])


def shift_y(value, d):
    return lax.ppermute(value, "dom", [(i, (i + 4 * d) & 15) for i in range(16)])


def halo_y(y_up, y_dn):
    h_dn = lax.ppermute(y_up, "dom", [(i, i + 4) for i in range(12)])
    h_up = lax.ppermute(y_dn, "dom", [(i + 4, i) for i in range(12)])
    return h_up, h_dn


def total(value, shift):
    parts = {}
    for d in (1, 3, 2):
        parts[d] = shift(value, d)
    return (value + parts[2]) + (parts[1] + parts[3])


def to_rows(packed):
    got = [packed[0]]
    for d in (1, 2, 3):
        got.append(shift_x(packed[d], d))
    return got


def exchange(near, images):
    h_before = shift_x(near, 1)
    h_after = shift_x(near, 3)
    own = near[0:K]
    far = shift_x(own, 2)
    h_up, h_dn = halo_y(images[3], images[0])
    grams = (own + far) + (h_before[0:K] + h_after[0:K])
    return total(grams, shift_y), (h_up, h_dn, h_before, h_after)


def blocks(start_vectors, face_x, face_y, face_z, masses, active):
    row = lax.axis_index("dom").astype(jnp.int32)
    scal = jnp.stack([active[0], row & 3, row]).astype(jnp.int32)
    start = start_vectors.reshape(3 * K * NX, LANES)
    fields = [f.reshape(NX, LANES) for f in (face_x, face_y, face_z, masses)]
    msg = f32(YROWS, LANES)
    zmsg = f32(ZROWS, LANES)
    near = f32(K + ZROWS, LANES)
    plane = pltpu.VMEM((NX, LANES), F32)
    columns = pltpu.VMEM((ZROWS, LANES), F32)
    packed = call(
        pack_kernel,
        6,
        (msg,) * 4,
        (pltpu.VMEM((3 * K * NX, LANES), F32),)
        + (plane,) * 4
        + (pltpu.SemaphoreType.DMA((3,)), pltpu.SemaphoreType.DMA((4,))),
        first=SM,
        rest=pl.BlockSpec(memory_space=pl.ANY),
        params=pltpu.CompilerParams(vmem_limit_bytes=67_000_000),
    )(scal, start, *fields)
    got = to_rows(packed)
    *v, z_edge = call(unpack_kernel, 5, (msg,) * 4 + (zmsg,), first=SM)(scal, *got)
    hv = halo_y(v[3], v[0])
    h_before, h_after = shift_x(z_edge, 1), shift_x(z_edge, 3)
    acc = pltpu.VMEM((4 * K, 2 * K), F32)
    *av, fld, near_new, hv_z = call(
        first_kernel, 9, (msg,) * 4 + (f32(10 * NX, LANES), near, zmsg), (acc,), first=SM
    )(scal, *v, *hv, h_before, h_after)
    mat_shape = jax.ShapeDtypeStruct((2 * K, 4 * K), BF16)
    grams, ha = exchange(near_new, av)
    mat = call(matrix_kernel, 1, mat_shape)(grams)
    out = call(
        functools.partial(step_kernel, False),
        18,
        (msg,) * 8 + (near, msg, msg, zmsg, f32(24, LANES)),
        (acc, columns),
        first=SM,
    )(scal, *v, *av, fld, mat, *hv, hv_z, *ha)
    v, av, (near_new, n_up, n_dn, n_z, rows) = out[:4], out[4:8], out[8:]
    grams, ha = exchange(near_new, av)
    mat = call(matrix_kernel, 1, mat_shape)(grams)
    side = pltpu.VMEM((YROWS, LANES), F32)
    part = f32(FROWS, LANES)
    img, grams, *packed = call(
        functools.partial(step_kernel, True),
        19,
        (part, f32(K, LANES)) + (part,) * 4,
        (acc, columns, side, side, columns) + (side,) * 8,
        first=SM,
    )(scal, *v, *av, fld, mat, n_up, n_dn, n_z, *ha, rows)
    behind = [(i, i + 1) for i in range(15)]
    before = lax.ppermute(img, "sub", behind)
    got = to_rows(packed)
    raw_off = call(off_kernel, 5, f32(K, 2 * K))(*packed, before)
    both = jnp.concatenate([grams, raw_off], axis=0)
    both = total(total(both, shift_y), shift_x)
    factor, diag = call(factor_kernel, 1, (f32(K, K), f32(K, K)))(both[0:K])
    other = lax.ppermute(factor, "sub", behind)
    off = call(cross_kernel, 3, f32(K, K))(factor, other, both[K:])
    out = call(
        out_kernel,
        6,
        jax.ShapeDtypeStruct((3 * K * NX, LANES), BF16),
        (pltpu.VMEM((3 * K * NX, LANES), F32),),
        first=SM,
    )(scal, factor, *got)
    return (out.reshape(1, 3, K, 1, NX, LANES), diag[None], off[None])


def solution(mesh):
    placed = (
        P("sub", None, None, "dom", None, None),
        P("sub", "dom", None, None),
        P("sub", "dom", None, None),
        P("sub", "dom", None, None),
        P("sub", "dom", None, None),
        P("sub"),
    )
    return jax.shard_map(
        blocks,
        mesh=mesh,
        in_specs=placed,
        out_specs=(
            P("sub", None, None, "dom", None, None),
            P("sub", None, None),
            P("sub", None, None),
        ),
        check_vma=False,
    )
```

time: 183 us -> 169 us (0.923)
  Pallas kernels: 62.3 us -> 48.1 us
  starting transfers between devices: 59 us -> 63.1 us
  local copies, waits for them, and re-layouts: 4.19 us -> 1.01 us
  waiting for transfers between devices: 54.2 us -> 52.3 us
    ppermute x6 -> x17, starting transfers between devices: 9.97 us -> 28.4 us  [shift_x(): lax.ppermute(value, 'dom', [(i, (i & 12) + (i + d & 3)) for i in range(16)])]
    ppermute x20 -> x11, starting transfers between devices: 31 us -> 16.7 us  [the longest x9 12.8 us: shift_y(): return lax.ppermute(value, 'dom', [(i, i + 4 * d & 15) for i in range(16)])]
    pallas_call x11, Pallas kernels: 62.3 us -> 48.1 us  [the longest x1 9.56 us: blocks(): call(functools.partial(step_kernel, False), 18, (msg,) * 8 + (near, msg,...]
    ppermute x20 -> x11, waiting for transfers between devices: 37.6 us -> 24.3 us  [the longest x9 15.9 us: shift_y(): return lax.ppermute(value, 'dom', [(i, i + 4 * d & 15) for i in range(16)])]
    ppermute x6 -> x17, waiting for transfers between devices: 16.2 us -> 28 us  [shift_x(): lax.ppermute(value, 'dom', [(i, (i & 12) + (i + d & 3)) for i in range(16)])]
    unnamed x10 -> x4, local copies, waits for them, and re-layouts: 4.19 us -> 1 us
  transfers between devices with their start and end apart: 32 -> 34, of which waited for: 18 -> 15; matrix products, arithmetic and copies ran while one was open for 0% -> 0% of each run, Pallas kernels for 5% -> 8%
where the time goes in v3:
time: 169 us; the launch traced here: 167 us
  starting transfers between devices  63.1 us (37%)
  waiting for transfers between devices  52.3 us (31%)
  Pallas kernels  48.1 us (28%)
    ppermute x17, starting transfers between devices, shift_x(): lax.ppermute(value, 'dom', [(i, (i & 12) + (i + d & 3)) for i in range(16)])  28.4 us
    ppermute x17, waiting for transfers between devices, shift_x(): lax.ppermute(value, 'dom', [(i, (i & 12) + (i + d & 3)) for i in range(16)])  28 us
    ppermute x9, waiting for transfers between devices, shift_y(): return lax.ppermute(value, 'dom', [(i, i + 4 * d & 15) for i in range(16)])  15.9 us
    ppermute x3, starting transfers between devices, halo_y(): h_dn = lax.ppermute(y_up, 'dom', [(i, i + 4) for i in range(12)])  14.2 us
    ppermute x9, starting transfers between devices, shift_y(): return lax.ppermute(value, 'dom', [(i, i + 4 * d & 15) for i in range(16)])  12.8 us
    pallas_call x1, Pallas kernels, blocks(): call(functools.partial(step_kernel, False), 18, (msg,) * 8 + (near, msg,...  9.56 us
    pallas_call x1, Pallas kernels, blocks(): call(functools.partial(step_kernel, True), 19, (part, f32(K, LANES)) + (p...  9.47 us
    ppermute x1, waiting for transfers between devices, blocks(): before = lax.ppermute(img, 'sub', behind)  8.38 us
  transfers between devices with their start and end apart: 34, of which 15 were waited for; matrix products, arithmetic and copies ran while one was open for 0% of the time, Pallas kernels for 8%

profile of v3, /device:TPU:128, one launch (start us, length us, event | category | flops | bytes accessed | tf_op | source)
XLA Modules:
  0.0 166.8 jit_solution(8790812853033355551)
XLA Ops:
  1.9 5.6 %shard_map.85 = (f32[784,128]{1,0:T(8,128)}, f32[784,128]{1,0:T(8,128)}, f32[784,128]{1,0:T(8,128)}, f32[784,128]{1,0:T(8,128)}) custom-call(s32[3]{0:T(128)} %pad_add_fusion.scal, f32[3072,128]{1,0:T(8,128)} %bitcast.12, f32[16,128]{1,0:T(8,128)} %bitcast.15, f32[16,128]{1,0:T(8,128)} %bitcast.16, f32[16,128]{1,0:T(8,128)} %bitcast.17, f32[16,128]{1,0:T(8,128)} %bitcast.18), custom_call_target="tpu_custom_call" | custom-call | tf_op jit(solution)/shard_map/pallas_call | solution.py:538
  7.5 1.6 collective-permute-start
  9.1 2.7 %collective-permute-start.1 = (f32[784,128]{1,0:T(8,128)}, f32[784,128]{1,0:T(8,128)S(1)}, u32[]{:S(2)}, u32[]{:S(2)}) collective-permute-start(f32[784,128]{1,0:T(8,128)} %get-tuple-element.42), channel_id=1, source_target_pairs={{0,2},{1,3},{2,0},{3,1},{4,6},{5,7},{6,4},{7,5},{8,10},{9,11},{10,... | collective-permute-start | bytes 1204232 | tf_op jit(solution)/shard_map/ppermute | solution.py:491
  11.8 1.4 collective-permute-start.2
  13.2 6.9 %collective-permute-done.r1 = f32[784,128]{1,0:T(8,128)S(1)} collective-permute-done((f32[784,128]{1,0:T(8,128)}, f32[784,128]{1,0:T(8,128)S(1)}, u32[]{:S(2)}, u32[]{:S(2)}) %collective-permute-start) | collective-permute-done | bytes 401440 | tf_op jit(solution)/shard_map/ppermute | solution.py:491
  20.2 9.4 %collective-permute-done.1.r2 = f32[784,128]{1,0:T(8,128)S(1)} collective-permute-done((f32[784,128]{1,0:T(8,128)}, f32[784,128]{1,0:T(8,128)S(1)}, u32[]{:S(2)}, u32[]{:S(2)}) %collective-permute-start.1) | collective-permute-done | bytes 401440 | tf_op jit(solution)/shard_map/ppermute | solution.py:491
  30.6 2.5 %shard_map.86 = (f32[784,128]{1,0:T(8,128)S(1)}, f32[784,128]{1,0:T(8,128)S(1)}, f32[784,128]{1,0:T(8,128)S(1)}, f32[784,128]{1,0:T(8,128)S(1)}, f32[224,128]{1,0:T(8,128)S(1)}) custom-call(s32[3]{0:T(128)S(1)} %copy-done.1, f32[784,128]{1,0:T(8,128)S(1)} %copy-done, f32[784,128]{1,0:T(8,128)S(1)} %collective-permute-done.r1, ...), custom_call_target="tpu_custom_call" | custom-call | tf_op jit(solution)/shard_map/pallas_call | solution.py:550
  33.1 1.3 collective-permute-start.3
  34.4 4.6 %collective-permute-start.4 = (f32[784,128]{1,0:T(8,128)S(1)}, f32[784,128]{1,0:T(8,128)S(1)}, u32[]{:S(2)}, u32[]{:S(2)}) collective-permute-start(f32[784,128]{1,0:T(8,128)S(1)} %get-tuple-element.47.b3.refs_3_), channel_id=1, source_target_pairs={{0,4},{1,5},{2,6},{3,7},{4,8},{5,9},{6,10},{7,11},{8,12},{9,13},{1... | collective-permute-start | bytes 1204232 | tf_op jit(solution)/shard_map/ppermute | solution.py:499
  39.0 2.3 %collective-permute-start.6 = (f32[224,128]{1,0:T(8,128)S(1)}, f32[224,128]{1,0:T(8,128)S(1)}, u32[]{:S(2)}, u32[]{:S(2)}) collective-permute-start(f32[224,128]{1,0:T(8,128)S(1)} %get-tuple-element.48), channel_id=1, source_target_pairs={{0,3},{1,0},{2,1},{3,2},{4,7},{5,4},{6,5},{7,6},{8,11},{9,8},{10,9... | collective-permute-start | bytes 344072 | tf_op jit(solution)/shard_map/ppermute | solution.py:491
  41.4 2.5 %collective-permute-done.6.h_after = f32[224,128]{1,0:T(8,128)S(1)} collective-permute-done((f32[224,128]{1,0:T(8,128)S(1)}, f32[224,128]{1,0:T(8,128)S(1)}, u32[]{:S(2)}, u32[]{:S(2)}) %collective-permute-start.6) | collective-permute-done | bytes 114720 | tf_op jit(solution)/shard_map/ppermute | solution.py:491
  43.9 3.5 %collective-permute-done.5.h_before = f32[224,128]{1,0:T(8,128)S(1)} collective-permute-done((f32[224,128]{1,0:T(8,128)S(1)}, f32[224,128]{1,0:T(8,128)S(1)}, u32[]{:S(2)}, u32[]{:S(2)}) %collective-permute-start.5) | collective-permute-done | bytes 114720 | tf_op jit(solution)/shard_map/ppermute | solution.py:491
  47.4 6.0 %shard_map.87 = (f32[784,128]{1,0:T(8,128)S(1)}, f32[784,128]{1,0:T(8,128)S(1)}, f32[784,128]{1,0:T(8,128)S(1)}, f32[784,128]{1,0:T(8,128)S(1)}, f32[160,128]{1,...) custom-call(s32[3]{0:T(128)S(1)} %copy-done.1, f32[784,128]{1,0:T(8,128)S(1)} %get-tuple-element.44.b0.refs_0_, ...), custom_call_target="tpu_custom_call" | custom-call | tf_op jit(solution)/shard_map/pallas_call | solution.py:554
  53.4 2.4 %collective-permute-start.9 = (f32[288,128]{1,0:T(8,128)S(1)}, f32[288,128]{1,0:T(8,128)S(1)}, u32[]{:S(2)}, u32[]{:S(2)}) collective-permute-start(f32[288,128]{1,0:T(8,128)S(1)} %get-tuple-element.54), channel_id=1, source_target_pairs={{0,3},{1,0},{2,1},{3,2},{4,7},{5,4},{6,5},{7,6},{8,11},{9,8},{10,9... | collective-permute-start | bytes 442376 | tf_op jit(solution)/shard_map/ppermute | solution.py:491
  55.7 1.6 collective-permute-start.7
  57.3 1.3 collective-permute-start.13
  58.6 5.0 %collective-permute-start.14 = (f32[784,128]{1,0:T(8,128)S(1)}, f32[784,128]{1,0:T(8,128)S(1)}, u32[]{:S(2)}, u32[]{:S(2)}) collective-permute-start(f32[784,128]{1,0:T(8,128)S(1)} %get-tuple-element.52.refs_7_), channel_id=1, source_target_pairs={{0,4},{1,5},{2,6},{3,7},{4,8},{5,9},{6,10},{7,11},{8,12},{9,13},{1... | collective-permute-start | bytes 1204232 | tf_op jit(solution)/shard_map/ppermute | solution.py:499
  63.7 3.1 %collective-permute-start.12 = (f32[64,128]{1,0:T(8,128)S(1)}, f32[64,128]{1,0:T(8,128)S(1)}, u32[]{:S(2)}, u32[]{:S(2)}) collective-permute-start(f32[64,128]{1,0:T(8,128)S(1)} %fusion.1), channel_id=1, source_target_pairs={{0,12},{1,13},{2,14},{3,15},{4,0},{5,1},{6,2},{7,3},{8,4},{9,5},{1... | collective-permute-start | bytes 98312 | tf_op jit(solution)/shard_map/ppermute | solution.py:495
  66.8 2.6 %collective-permute-start.10 = (f32[64,128]{1,0:T(8,128)S(1)}, f32[64,128]{1,0:T(8,128)S(1)}, u32[]{:S(2)}, u32[]{:S(2)}) collective-permute-start(f32[64,128]{1,0:T(8,128)S(1)} %fusion.1), channel_id=1, source_target_pairs={{0,8},{1,9},{2,10},{3,11},{4,12},{5,13},{6,14},{7,15},{8,0},{9,1},... | collective-permute-start | bytes 98312 | tf_op jit(solution)/shard_map/ppermute | solution.py:495
  70.5 1.4 collective-permute-done.11
  71.9 4.0 %collective-permute-done.10 = f32[64,128]{1,0:T(8,128)S(1)} collective-permute-done((f32[64,128]{1,0:T(8,128)S(1)}, f32[64,128]{1,0:T(8,128)S(1)}, u32[]{:S(2)}, u32[]{:S(2)}) %collective-permute-start.10) | collective-permute-done | bytes 32800 | tf_op jit(solution)/shard_map/ppermute | solution.py:495
  75.8 2.5 %shard_map.88.refs_9_ = bf16[128,256]{1,0:T(8,128)(2,1)S(1)} custom-call(f32[64,128]{1,0:T(8,128)S(1)} %add_add_fusion.3.grams), custom_call_target="tpu_custom_call" | custom-call | tf_op jit(solution)/shard_map/pallas_call | solution.py:559
  78.4 9.6 %shard_map.89 = (f32[784,128]{1,0:T(8,128)S(1)}, f32[784,128]{1,0:T(8,128)S(1)}, f32[784,128]{1,0:T(8,128)S(1)}, f32[784,128]{1,0:T(8,128)S(1)}, f32[784,128]{1,...) custom-call(s32[3]{0:T(128)S(1)} %copy-done.1, ...), custom_call_target="tpu_custom_call" | custom-call | tf_op jit(solution)/shard_map/pallas_call | solution.py:560
  87.9 1.9 %collective-permute-start.17 = (f32[288,128]{1,0:T(8,128)S(1)}, f32[288,128]{1,0:T(8,128)S(1)}, u32[]{:S(2)}, u32[]{:S(2)}) collective-permute-start(f32[288,128]{1,0:T(8,128)S(1)} %get-tuple-element.64), channel_id=1, source_target_pairs={{0,3},{1,0},{2,1},{3,2},{4,7},{5,4},{6,5},{7,6},{8,11},{9,8},{10,9... | collective-permute-start | bytes 442376 | tf_op jit(solution)/shard_map/ppermute | solution.py:491
  90.5 2.0 %collective-permute-start.15 = (f32[64,128]{1,0:T(8,128)S(1)}, f32[64,128]{1,0:T(8,128)S(1)}, u32[]{:S(2)}, u32[]{:S(2)}) collective-permute-start(f32[64,128]{1,0:T(8,128)S(1)} %slice.27), channel_id=1, source_target_pairs={{0,2},{1,3},{2,0},{3,1},{4,6},{5,7},{6,4},{7,5},{8,10},{9,11},{10,... | collective-permute-start | bytes 98312 | tf_op jit(solution)/shard_map/ppermute | solution.py:491
  92.5 1.3 collective-permute-start.21
  93.8 4.6 %collective-permute-start.22 = (f32[784,128]{1,0:T(8,128)S(1)}, f32[784,128]{1,0:T(8,128)S(1)}, u32[]{:S(2)}, u32[]{:S(2)}) collective-permute-start(f32[784,128]{1,0:T(8,128)S(1)} %get-tuple-element.63.refs_7_), channel_id=1, source_target_pairs={{0,4},{1,5},{2,6},{3,7},{4,8},{5,9},{6,10},{7,11},{8,12},{9,13},{1... | collective-permute-start | bytes 1204232 | tf_op jit(solution)/shard_map/ppermute | solution.py:499
  98.5 2.0 %collective-permute-start.19 = (f32[64,128]{1,0:T(8,128)S(1)}, f32[64,128]{1,0:T(8,128)S(1)}, u32[]{:S(2)}, u32[]{:S(2)}) collective-permute-start(f32[64,128]{1,0:T(8,128)S(1)} %fusion), channel_id=1, source_target_pairs={{0,4},{1,5},{2,6},{3,7},{4,8},{5,9},{6,10},{7,11},{8,12},{9,13},{1... | collective-permute-start | bytes 98312 | tf_op jit(solution)/shard_map/ppermute | solution.py:495
  101.0 2.0 %collective-permute-done.20 = f32[64,128]{1,0:T(8,128)S(1)} collective-permute-done((f32[64,128]{1,0:T(8,128)S(1)}, f32[64,128]{1,0:T(8,128)S(1)}, u32[]{:S(2)}, u32[]{:S(2)}) %collective-permute-start.20) | collective-permute-done | bytes 32800 | tf_op jit(solution)/shard_map/ppermute | solution.py:495
  102.9 1.1 collective-permute-done.19
  104.1 1.9 %collective-permute-done.18 = f32[64,128]{1,0:T(8,128)S(1)} collective-permute-done((f32[64,128]{1,0:T(8,128)S(1)}, f32[64,128]{1,0:T(8,128)S(1)}, u32[]{:S(2)}, u32[]{:S(2)}) %collective-permute-start.18) | collective-permute-done | bytes 32800 | tf_op jit(solution)/shard_map/ppermute | solution.py:495
  106.0 2.5 %shard_map.90.refs_9_ = bf16[128,256]{1,0:T(8,128)(2,1)S(1)} custom-call(f32[64,128]{1,0:T(8,128)S(1)} %add_add_fusion.2.grams), custom_call_target="tpu_custom_call" | custom-call | tf_op jit(solution)/shard_map/pallas_call | solution.py:569
  108.5 9.5 %shard_map.91 = (f32[768,128]{1,0:T(8,128)S(1)}, f32[64,128]{1,0:T(8,128)S(1)}, f32[768,128]{1,0:T(8,128)S(1)}, f32[768,128]{1,0:T(8,128)S(1)}, f32[768,128]{1,0:T(8,128)S(1)}, /*index=5*/f32[768,128]{1,0:T(8,128)S(1)}) custom-call(s32[3]{0:T(128)S(1)} %copy-done.1, f32[784,128]{1,0:T(8,128)S(1)} %get-tuple-element.56.refs_0_, ...), custom_call_target="tpu_custom_call" | custom-call | tf_op jit(solution)/shard_map/pallas_call | solution.py:572
  118.0 1.9 %collective-permute-start.23 = (f32[768,128]{1,0:T(8,128)S(1)}, f32[768,128]{1,0:T(8,128)S(1)}, u32[]{:S(2)}, u32[]{:S(2)}) collective-permute-start(f32[768,128]{1,0:T(8,128)S(1)} %get-tuple-element.74), channel_id=1, source_target_pairs={{0,16},{16,32},{32,48},{48,64},{64,80},{80,96},{96,112},{112,128},... | collective-permute-start | bytes 1179656 | tf_op jit(solution)/shard_map/ppermute | solution.py:580
  119.9 8.4 %collective-permute-done.23.img_ref = f32[768,128]{1,0:T(8,128)S(1)} collective-permute-done((f32[768,128]{1,0:T(8,128)S(1)}, f32[768,128]{1,0:T(8,128)S(1)}, u32[]{:S(2)}, u32[]{:S(2)}) %collective-permute-start.23) | collective-permute-done | bytes 393248 | tf_op jit(solution)/shard_map/ppermute | solution.py:580
  129.3 2.6 %collective-permute-start.26 = (f32[128,128]{1,0:T(8,128)S(1)}, f32[128,128]{1,0:T(8,128)S(1)}, u32[]{:S(2)}, u32[]{:S(2)}) collective-permute-start(f32[128,128]{1,0:T(8,128)S(1)} %pad_maximum_fusion), channel_id=1, source_target_pairs={{0,12},{1,13},{2,14},{3,15},{4,0},{5,1},{6,2},{7,3},{8,4},{9,5},{1... | collective-permute-start | bytes 196616 | tf_op jit(solution)/shard_map/ppermute | solution.py:495
  131.9 1.2 collective-permute-start.24
  133.2 1.4 collective-permute-done.25
  134.6 3.2 %collective-permute-done.24 = f32[128,128]{1,0:T(8,128)S(1)} collective-permute-done((f32[128,128]{1,0:T(8,128)S(1)}, f32[128,128]{1,0:T(8,128)S(1)}, u32[]{:S(2)}, u32[]{:S(2)}) %collective-permute-start.24) | collective-permute-done | bytes 65568 | tf_op jit(solution)/shard_map/ppermute | solution.py:495
  137.7 2.7 %collective-permute-start.29 = (f32[128,128]{1,0:T(8,128)S(1)}, f32[128,128]{1,0:T(8,128)S(1)}, u32[]{:S(2)}, u32[]{:S(2)}) collective-permute-start(f32[128,128]{1,0:T(8,128)S(1)} %add_add_fusion.1), channel_id=1, source_target_pairs={{0,3},{1,0},{2,1},{3,2},{4,7},{5,4},{6,5},{7,6},{8,11},{9,8},{10,9... | collective-permute-start | bytes 196616 | tf_op jit(solution)/shard_map/ppermute | solution.py:491
  140.4 1.6 collective-permute-start.27
  142.0 2.5 %collective-permute-start.30 = (f32[768,128]{1,0:T(8,128)S(1)}, f32[768,128]{1,0:T(8,128)S(1)}, u32[]{:S(2)}, u32[]{:S(2)}) collective-permute-start(f32[768,128]{1,0:T(8,128)S(1)} %get-tuple-element.71.w1), channel_id=1, source_target_pairs={{0,1},{1,2},{2,3},{3,0},{4,5},{5,6},{6,7},{7,4},{8,9},{9,10},{10,1... | collective-permute-start | bytes 1179656 | tf_op jit(solution)/shard_map/ppermute | solution.py:491
  145.4 2.4 %collective-permute-done.29 = f32[128,128]{1,0:T(8,128)S(1)} collective-permute-done((f32[128,128]{1,0:T(8,128)S(1)}, f32[128,128]{1,0:T(8,128)S(1)}, u32[]{:S(2)}, u32[]{:S(2)}) %collective-permute-start.29) | collective-permute-done | bytes 65568 | tf_op jit(solution)/shard_map/ppermute | solution.py:491
  147.9 4.2 %collective-permute-start.32 = (f32[768,128]{1,0:T(8,128)S(1)}, f32[768,128]{1,0:T(8,128)S(1)}, u32[]{:S(2)}, u32[]{:S(2)}) collective-permute-start(f32[768,128]{1,0:T(8,128)S(1)} %get-tuple-element.73.w3), channel_id=1, source_target_pairs={{0,3},{1,0},{2,1},{3,2},{4,7},{5,4},{6,5},{7,6},{8,11},{9,8},{10,9... | collective-permute-start | bytes 1179656 | tf_op jit(solution)/shard_map/ppermute | solution.py:491
  152.1 2.8 %shard_map.93 = (f32[64,64]{1,0:T(8,128)S(1)}, f32[64,64]{1,0:T(8,128)}) custom-call(f32[64,128]{1,0:T(8,128)S(1)} %get-tuple-element.81.grams), custom_call_target="tpu_custom_call" | custom-call | tf_op jit(solution)/shard_map/pallas_call | solution.py:585
  154.9 1.9 %collective-permute-start.33 = (f32[64,64]{1,0:T(8,128)S(1)}, f32[64,64]{1,0:T(8,128)S(1)}, u32[]{:S(2)}, u32[]{:S(2)}) collective-permute-start(f32[64,64]{1,0:T(8,128)S(1)} %get-tuple-element.75.factor), channel_id=1, source_target_pairs={{0,16},{16,32},{32,48},{48,64},{64,80},{80,96},{96,112},{112,128},... | collective-permute-start | bytes 49160 | tf_op jit(solution)/shard_map/ppermute | solution.py:586
  156.8 3.1 %collective-permute-done.30.r1 = f32[768,128]{1,0:T(8,128)S(1)} collective-permute-done((f32[768,128]{1,0:T(8,128)S(1)}, f32[768,128]{1,0:T(8,128)S(1)}, u32[]{:S(2)}, u32[]{:S(2)}) %collective-permute-start.30) | collective-permute-done | bytes 393248 | tf_op jit(solution)/shard_map/ppermute | solution.py:491
  160.0 5.8 %shard_map.94 = bf16[3072,128]{1,0:T(8,128)(2,1)} custom-call(s32[3]{0:T(128)S(1)} %copy-done.1, f32[64,64]{1,0:T(8,128)S(1)} %get-tuple-element.75.factor, f32[768,128]{1,0:T(8,128)S(1)} %get-tuple-element.70.w0.r0, f32[768,128]{1,0:T(8,128)S(1)} %collective-permute-done.30.r1, f32[768,128]{1,0:T(8,128)S(1)} %collective-permute-done.31.r2, ...), custom_call_target="tpu_custom_call" | custom-call | tf_op jit(solution)/shard_map/pallas_call | solution.py:588
  (46 shorter events, 6.9 us)
Async XLA Ops:
  1.9 27.7 %copy-start.1 = (s32[3]{0:T(128)S(1)}, s32[3]{0:T(128)}, u32[]{:S(2)}) copy-start(s32[3]{0:T(128)} %pad_add_fusion.scal) | copy-start | bytes 40
  7.5 12.7 %collective-permute-start = (f32[784,128]{1,0:T(8,128)}, f32[784,128]{1,0:T(8,128)S(1)}, u32[]{:S(2)}, u32[]{:S(2)}) collective-permute-start(f32[784,128]{1,0:T(8,128)} %get-tuple-element.41), channel_id=1, source_target_pairs={{0,1},{1,2},{2,3},{3,0},{4,5},{5,6},{6,7},{7,4},{8,9},{9,10},{10,1... | collective-permute-start | bytes 1204232 | tf_op jit(solution)/shard_map/ppermute | solution.py:491
  9.1 20.5 %collective-permute-start.1 = (f32[784,128]{1,0:T(8,128)}, f32[784,128]{1,0:T(8,128)S(1)}, u32[]{:S(2)}, u32[]{:S(2)}) collective-permute-start(f32[784,128]{1,0:T(8,128)} %get-tuple-element.42), channel_id=1, source_target_pairs={{0,2},{1,3},{2,0},{3,1},{4,6},{5,7},{6,4},{7,5},{8,10},{9,11},{10,... | collective-permute-start | bytes 1204232 | tf_op jit(solution)/shard_map/ppermute | solution.py:491
  11.8 17.8 %collective-permute-start.2 = (f32[784,128]{1,0:T(8,128)}, f32[784,128]{1,0:T(8,128)S(1)}, u32[]{:S(2)}, u32[]{:S(2)}) collective-permute-start(f32[784,128]{1,0:T(8,128)} %get-tuple-element.43), channel_id=1, source_target_pairs={{0,3},{1,0},{2,1},{3,2},{4,7},{5,4},{6,5},{7,6},{8,11},{9,8},{10,9... | collective-permute-start | bytes 1204232 | tf_op jit(solution)/shard_map/ppermute | solution.py:491
  29.6 1.0 copy-start
  33.1 14.2 %collective-permute-start.3 = (f32[784,128]{1,0:T(8,128)S(1)}, f32[784,128]{1,0:T(8,128)S(1)}, u32[]{:S(2)}, u32[]{:S(2)}) collective-permute-start(f32[784,128]{1,0:T(8,128)S(1)} %get-tuple-element.44.b0.refs_0_), channel_id=1, source_target_pairs={{4,0},{5,1},{6,2},{7,3},{8,4},{9,5},{10,6},{11,7},{12,8},{13,9},{1... | collective-permute-start | bytes 1204232 | tf_op jit(solution)/shard_map/ppermute | solution.py:500
  34.4 12.9 %collective-permute-start.4 = (f32[784,128]{1,0:T(8,128)S(1)}, f32[784,128]{1,0:T(8,128)S(1)}, u32[]{:S(2)}, u32[]{:S(2)}) collective-permute-start(f32[784,128]{1,0:T(8,128)S(1)} %get-tuple-element.47.b3.refs_3_), channel_id=1, source_target_pairs={{0,4},{1,5},{2,6},{3,7},{4,8},{5,9},{6,10},{7,11},{8,12},{9,13},{1... | collective-permute-start | bytes 1204232 | tf_op jit(solution)/shard_map/ppermute | solution.py:499
  39.0 4.9 %collective-permute-start.6 = (f32[224,128]{1,0:T(8,128)S(1)}, f32[224,128]{1,0:T(8,128)S(1)}, u32[]{:S(2)}, u32[]{:S(2)}) collective-permute-start(f32[224,128]{1,0:T(8,128)S(1)} %get-tuple-element.48), channel_id=1, source_target_pairs={{0,3},{1,0},{2,1},{3,2},{4,7},{5,4},{6,5},{7,6},{8,11},{9,8},{10,9... | collective-permute-start | bytes 344072 | tf_op jit(solution)/shard_map/ppermute | solution.py:491
  41.4 6.0 %collective-permute-start.5 = (f32[224,128]{1,0:T(8,128)S(1)}, f32[224,128]{1,0:T(8,128)S(1)}, u32[]{:S(2)}, u32[]{:S(2)}) collective-permute-start(f32[224,128]{1,0:T(8,128)S(1)} %get-tuple-element.48), channel_id=1, source_target_pairs={{0,1},{1,2},{2,3},{3,0},{4,5},{5,6},{6,7},{7,4},{8,9},{9,10},{10,1... | collective-permute-start | bytes 344072 | tf_op jit(solution)/shard_map/ppermute | solution.py:491
  53.4 10.3 %collective-permute-start.9 = (f32[288,128]{1,0:T(8,128)S(1)}, f32[288,128]{1,0:T(8,128)S(1)}, u32[]{:S(2)}, u32[]{:S(2)}) collective-permute-start(f32[288,128]{1,0:T(8,128)S(1)} %get-tuple-element.54), channel_id=1, source_target_pairs={{0,3},{1,0},{2,1},{3,2},{4,7},{5,4},{6,5},{7,6},{8,11},{9,8},{10,9... | collective-permute-start | bytes 442376 | tf_op jit(solution)/shard_map/ppermute | solution.py:491
  55.7 7.9 %collective-permute-start.8 = (f32[288,128]{1,0:T(8,128)S(1)}, f32[288,128]{1,0:T(8,128)S(1)}, u32[]{:S(2)}, u32[]{:S(2)}) collective-permute-start(f32[288,128]{1,0:T(8,128)S(1)} %get-tuple-element.54), channel_id=1, source_target_pairs={{0,1},{1,2},{2,3},{3,0},{4,5},{5,6},{6,7},{7,4},{8,9},{9,10},{10,1... | collective-permute-start | bytes 442376 | tf_op jit(solution)/shard_map/ppermute | solution.py:491
  55.7 7.9 %collective-permute-start.7 = (f32[64,128]{1,0:T(8,128)S(1)}, f32[64,128]{1,0:T(8,128)S(1)}, u32[]{:S(2)}, u32[]{:S(2)}) collective-permute-start(f32[64,128]{1,0:T(8,128)S(1)} %slice.24), channel_id=1, source_target_pairs={{0,2},{1,3},{2,0},{3,1},{4,6},{5,7},{6,4},{7,5},{8,10},{9,11},{10,... | collective-permute-start | bytes 98312 | tf_op jit(solution)/shard_map/ppermute | solution.py:491
  57.3 21.1 %collective-permute-start.13 = (f32[784,128]{1,0:T(8,128)S(1)}, f32[784,128]{1,0:T(8,128)S(1)}, u32[]{:S(2)}, u32[]{:S(2)}) collective-permute-start(f32[784,128]{1,0:T(8,128)S(1)} %get-tuple-element.49.refs_4_), channel_id=1, source_target_pairs={{4,0},{5,1},{6,2},{7,3},{8,4},{9,5},{10,6},{11,7},{12,8},{13,9},{1... | collective-permute-start | bytes 1204232 | tf_op jit(solution)/shard_map/ppermute | solution.py:500
  58.6 19.8 %collective-permute-start.14 = (f32[784,128]{1,0:T(8,128)S(1)}, f32[784,128]{1,0:T(8,128)S(1)}, u32[]{:S(2)}, u32[]{:S(2)}) collective-permute-start(f32[784,128]{1,0:T(8,128)S(1)} %get-tuple-element.52.refs_7_), channel_id=1, source_target_pairs={{0,4},{1,5},{2,6},{3,7},{4,8},{5,9},{6,10},{7,11},{8,12},{9,13},{1... | collective-permute-start | bytes 1204232 | tf_op jit(solution)/shard_map/ppermute | solution.py:499
  63.7 6.8 %collective-permute-start.12 = (f32[64,128]{1,0:T(8,128)S(1)}, f32[64,128]{1,0:T(8,128)S(1)}, u32[]{:S(2)}, u32[]{:S(2)}) collective-permute-start(f32[64,128]{1,0:T(8,128)S(1)} %fusion.1), channel_id=1, source_target_pairs={{0,12},{1,13},{2,14},{3,15},{4,0},{5,1},{6,2},{7,3},{8,4},{9,5},{1... | collective-permute-start | bytes 98312 | tf_op jit(solution)/shard_map/ppermute | solution.py:495
  66.8 5.1 %collective-permute-start.11 = (f32[64,128]{1,0:T(8,128)S(1)}, f32[64,128]{1,0:T(8,128)S(1)}, u32[]{:S(2)}, u32[]{:S(2)}) collective-permute-start(f32[64,128]{1,0:T(8,128)S(1)} %fusion.1), channel_id=1, source_target_pairs={{0,4},{1,5},{2,6},{3,7},{4,8},{5,9},{6,10},{7,11},{8,12},{9,13},{1... | collective-permute-start | bytes 98312 | tf_op jit(solution)/shard_map/ppermute | solution.py:495
  66.8 9.1 %collective-permute-start.10 = (f32[64,128]{1,0:T(8,128)S(1)}, f32[64,128]{1,0:T(8,128)S(1)}, u32[]{:S(2)}, u32[]{:S(2)}) collective-permute-start(f32[64,128]{1,0:T(8,128)S(1)} %fusion.1), channel_id=1, source_target_pairs={{0,8},{1,9},{2,10},{3,11},{4,12},{5,13},{6,14},{7,15},{8,0},{9,1},... | collective-permute-start | bytes 98312 | tf_op jit(solution)/shard_map/ppermute | solution.py:495
  87.9 10.4 %collective-permute-start.17 = (f32[288,128]{1,0:T(8,128)S(1)}, f32[288,128]{1,0:T(8,128)S(1)}, u32[]{:S(2)}, u32[]{:S(2)}) collective-permute-start(f32[288,128]{1,0:T(8,128)S(1)} %get-tuple-element.64), channel_id=1, source_target_pairs={{0,3},{1,0},{2,1},{3,2},{4,7},{5,4},{6,5},{7,6},{8,11},{9,8},{10,9... | collective-permute-start | bytes 442376 | tf_op jit(solution)/shard_map/ppermute | solution.py:491
  89.8 8.5 %collective-permute-start.16 = (f32[288,128]{1,0:T(8,128)S(1)}, f32[288,128]{1,0:T(8,128)S(1)}, u32[]{:S(2)}, u32[]{:S(2)}) collective-permute-start(f32[288,128]{1,0:T(8,128)S(1)} %get-tuple-element.64), channel_id=1, source_target_pairs={{0,1},{1,2},{2,3},{3,0},{4,5},{5,6},{6,7},{7,4},{8,9},{9,10},{10,1... | collective-permute-start | bytes 442376 | tf_op jit(solution)/shard_map/ppermute | solution.py:491
  90.5 7.8 %collective-permute-start.15 = (f32[64,128]{1,0:T(8,128)S(1)}, f32[64,128]{1,0:T(8,128)S(1)}, u32[]{:S(2)}, u32[]{:S(2)}) collective-permute-start(f32[64,128]{1,0:T(8,128)S(1)} %slice.27), channel_id=1, source_target_pairs={{0,2},{1,3},{2,0},{3,1},{4,6},{5,7},{6,4},{7,5},{8,10},{9,11},{10,... | collective-permute-start | bytes 98312 | tf_op jit(solution)/shard_map/ppermute | solution.py:491
  92.5 16.0 %collective-permute-start.21 = (f32[784,128]{1,0:T(8,128)S(1)}, f32[784,128]{1,0:T(8,128)S(1)}, u32[]{:S(2)}, u32[]{:S(2)}) collective-permute-start(f32[784,128]{1,0:T(8,128)S(1)} %get-tuple-element.60.refs_4_), channel_id=1, source_target_pairs={{4,0},{5,1},{6,2},{7,3},{8,4},{9,5},{10,6},{11,7},{12,8},{13,9},{1... | collective-permute-start | bytes 1204232 | tf_op jit(solution)/shard_map/ppermute | solution.py:500
  93.8 14.7 %collective-permute-start.22 = (f32[784,128]{1,0:T(8,128)S(1)}, f32[784,128]{1,0:T(8,128)S(1)}, u32[]{:S(2)}, u32[]{:S(2)}) collective-permute-start(f32[784,128]{1,0:T(8,128)S(1)} %get-tuple-element.63.refs_7_), channel_id=1, source_target_pairs={{0,4},{1,5},{2,6},{3,7},{4,8},{5,9},{6,10},{7,11},{8,12},{9,13},{1... | collective-permute-start | bytes 1204232 | tf_op jit(solution)/shard_map/ppermute | solution.py:499
  98.4 4.5 %collective-permute-start.20 = (f32[64,128]{1,0:T(8,128)S(1)}, f32[64,128]{1,0:T(8,128)S(1)}, u32[]{:S(2)}, u32[]{:S(2)}) collective-permute-start(f32[64,128]{1,0:T(8,128)S(1)} %fusion), channel_id=1, source_target_pairs={{0,12},{1,13},{2,14},{3,15},{4,0},{5,1},{6,2},{7,3},{8,4},{9,5},{1... | collective-permute-start | bytes 98312 | tf_op jit(solution)/shard_map/ppermute | solution.py:495
  98.5 5.5 %collective-permute-start.19 = (f32[64,128]{1,0:T(8,128)S(1)}, f32[64,128]{1,0:T(8,128)S(1)}, u32[]{:S(2)}, u32[]{:S(2)}) collective-permute-start(f32[64,128]{1,0:T(8,128)S(1)} %fusion), channel_id=1, source_target_pairs={{0,4},{1,5},{2,6},{3,7},{4,8},{5,9},{6,10},{7,11},{8,12},{9,13},{1... | collective-permute-start | bytes 98312 | tf_op jit(solution)/shard_map/ppermute | solution.py:495
  100.5 5.4 %collective-permute-start.18 = (f32[64,128]{1,0:T(8,128)S(1)}, f32[64,128]{1,0:T(8,128)S(1)}, u32[]{:S(2)}, u32[]{:S(2)}) collective-permute-start(f32[64,128]{1,0:T(8,128)S(1)} %fusion), channel_id=1, source_target_pairs={{0,8},{1,9},{2,10},{3,11},{4,12},{5,13},{6,14},{7,15},{8,0},{9,1},... | collective-permute-start | bytes 98312 | tf_op jit(solution)/shard_map/ppermute | solution.py:495
  118.0 10.3 %collective-permute-start.23 = (f32[768,128]{1,0:T(8,128)S(1)}, f32[768,128]{1,0:T(8,128)S(1)}, u32[]{:S(2)}, u32[]{:S(2)}) collective-permute-start(f32[768,128]{1,0:T(8,128)S(1)} %get-tuple-element.74), channel_id=1, source_target_pairs={{0,16},{16,32},{32,48},{48,64},{64,80},{80,96},{96,112},{112,128},... | collective-permute-start | bytes 1179656 | tf_op jit(solution)/shard_map/ppermute | solution.py:580
  128.6 5.9 %collective-permute-start.25 = (f32[128,128]{1,0:T(8,128)S(1)}, f32[128,128]{1,0:T(8,128)S(1)}, u32[]{:S(2)}, u32[]{:S(2)}) collective-permute-start(f32[128,128]{1,0:T(8,128)S(1)} %pad_maximum_fusion), channel_id=1, source_target_pairs={{0,4},{1,5},{2,6},{3,7},{4,8},{5,9},{6,10},{7,11},{8,12},{9,13},{1... | collective-permute-start | bytes 196616 | tf_op jit(solution)/shard_map/ppermute | solution.py:495
  129.3 5.3 %collective-permute-start.26 = (f32[128,128]{1,0:T(8,128)S(1)}, f32[128,128]{1,0:T(8,128)S(1)}, u32[]{:S(2)}, u32[]{:S(2)}) collective-permute-start(f32[128,128]{1,0:T(8,128)S(1)} %pad_maximum_fusion), channel_id=1, source_target_pairs={{0,12},{1,13},{2,14},{3,15},{4,0},{5,1},{6,2},{7,3},{8,4},{9,5},{1... | collective-permute-start | bytes 196616 | tf_op jit(solution)/shard_map/ppermute | solution.py:495
  131.9 5.8 %collective-permute-start.24 = (f32[128,128]{1,0:T(8,128)S(1)}, f32[128,128]{1,0:T(8,128)S(1)}, u32[]{:S(2)}, u32[]{:S(2)}) collective-permute-start(f32[128,128]{1,0:T(8,128)S(1)} %pad_maximum_fusion), channel_id=1, source_target_pairs={{0,8},{1,9},{2,10},{3,11},{4,12},{5,13},{6,14},{7,15},{8,0},{9,1},... | collective-permute-start | bytes 196616 | tf_op jit(solution)/shard_map/ppermute | solution.py:495
  137.7 10.1 %collective-permute-start.29 = (f32[128,128]{1,0:T(8,128)S(1)}, f32[128,128]{1,0:T(8,128)S(1)}, u32[]{:S(2)}, u32[]{:S(2)}) collective-permute-start(f32[128,128]{1,0:T(8,128)S(1)} %add_add_fusion.1), channel_id=1, source_target_pairs={{0,3},{1,0},{2,1},{3,2},{4,7},{5,4},{6,5},{7,6},{8,11},{9,8},{10,9... | collective-permute-start | bytes 196616 | tf_op jit(solution)/shard_map/ppermute | solution.py:491
  140.4 11.6 %collective-permute-start.28 = (f32[128,128]{1,0:T(8,128)S(1)}, f32[128,128]{1,0:T(8,128)S(1)}, u32[]{:S(2)}, u32[]{:S(2)}) collective-permute-start(f32[128,128]{1,0:T(8,128)S(1)} %add_add_fusion.1), channel_id=1, source_target_pairs={{0,1},{1,2},{2,3},{3,0},{4,5},{5,6},{6,7},{7,4},{8,9},{9,10},{10,1... | collective-permute-start | bytes 196616 | tf_op jit(solution)/shard_map/ppermute | solution.py:491
  140.4 11.6 %collective-permute-start.27 = (f32[128,128]{1,0:T(8,128)S(1)}, f32[128,128]{1,0:T(8,128)S(1)}, u32[]{:S(2)}, u32[]{:S(2)}) collective-permute-start(f32[128,128]{1,0:T(8,128)S(1)} %add_add_fusion.1), channel_id=1, source_target_pairs={{0,2},{1,3},{2,0},{3,1},{4,6},{5,7},{6,4},{7,5},{8,10},{9,11},{10,... | collective-permute-start | bytes 196616 | tf_op jit(solution)/shard_map/ppermute | solution.py:491
  142.0 18.0 %collective-permute-start.30 = (f32[768,128]{1,0:T(8,128)S(1)}, f32[768,128]{1,0:T(8,128)S(1)}, u32[]{:S(2)}, u32[]{:S(2)}) collective-permute-start(f32[768,128]{1,0:T(8,128)S(1)} %get-tuple-element.71.w1), channel_id=1, source_target_pairs={{0,1},{1,2},{2,3},{3,0},{4,5},{5,6},{6,7},{7,4},{8,9},{9,10},{10,1... | collective-permute-start | bytes 1179656 | tf_op jit(solution)/shard_map/ppermute | solution.py:491
  144.5 15.4 %collective-permute-start.31 = (f32[768,128]{1,0:T(8,128)S(1)}, f32[768,128]{1,0:T(8,128)S(1)}, u32[]{:S(2)}, u32[]{:S(2)}) collective-permute-start(f32[768,128]{1,0:T(8,128)S(1)} %get-tuple-element.72.w2), channel_id=1, source_target_pairs={{0,2},{1,3},{2,0},{3,1},{4,6},{5,7},{6,4},{7,5},{8,10},{9,11},{10,... | collective-permute-start | bytes 1179656 | tf_op jit(solution)/shard_map/ppermute | solution.py:491
  147.9 12.1 %collective-permute-start.32 = (f32[768,128]{1,0:T(8,128)S(1)}, f32[768,128]{1,0:T(8,128)S(1)}, u32[]{:S(2)}, u32[]{:S(2)}) collective-permute-start(f32[768,128]{1,0:T(8,128)S(1)} %get-tuple-element.73.w3), channel_id=1, source_target_pairs={{0,3},{1,0},{2,1},{3,2},{4,7},{5,4},{6,5},{7,6},{8,11},{9,8},{10,9... | collective-permute-start | bytes 1179656 | tf_op jit(solution)/shard_map/ppermute | solution.py:491
  154.9 10.9 %collective-permute-start.33 = (f32[64,64]{1,0:T(8,128)S(1)}, f32[64,64]{1,0:T(8,128)S(1)}, u32[]{:S(2)}, u32[]{:S(2)}) collective-permute-start(f32[64,64]{1,0:T(8,128)S(1)} %get-tuple-element.75.factor), channel_id=1, source_target_pairs={{0,16},{16,32},{32,48},{48,64},{64,80},{80,96},{96,112},{112,128},... | collective-permute-start | bytes 49160 | tf_op jit(solution)/shard_map/ppermute | solution.py:586

commit v4 on v3

--- a/solution.py
+++ b/solution.py
@@ -338,6 +338,7 @@
     lax.fori_loop(0, GROUPS, body, 0)
     if last:
         finish_gram(acc, grams)
+        img_ref[pl.ds(FROWS, K), :] = grams[...]
         start = active - OV
         group, skip = start >> 2, start & 3
         late = (lanes(K) >> 5) < skip
@@ -419,18 +420,6 @@
     )
 
 
-def factor_kernel(grams, factor_ref, diag_ref):
-    both = grams[...]
-    factor = inverse_factor(both[:, 0:K])
-    factor_ref[...] = factor
-    image = small_dot(factor, both[:, K : 2 * K], ((1,), (1,)))
-    diag_ref[...] = small_dot(image, factor, ((1,), (1,)))
-
-
-def cross_kernel(factor, other, raw, out):
-    out[...] = small_dot(small_dot(factor[...], raw[:, 0:K]), other[...], ((1,), (1,)))
-
-
 def off_kernel(w0, w1, w2, w3, img_ref, out):
     acc = jnp.zeros((2 * K, 2 * K), F32)
     for c in range(3):
@@ -447,33 +436,52 @@
             )
     half = acc[0:K, :] + acc[K : 2 * K, :]
     out[:, 0:K] = half[:, 0:K] + half[:, K : 2 * K]
-    out[:, K : 2 * K] = jnp.zeros((K, K), F32)
-
-
-def out_kernel(scal, factor, r0, r1, r2, r3, out_ref, hold):
+    before = pltpu.roll(img_ref[pl.ds(FROWS, K), :], K, 1)
+    out[:, K : 2 * K] = before[:, K : 2 * K]
+
+
+def out_kernel(scal, both, r0, r1, r2, r3, out_hbm, diag_ref, off_ref, hold, cast, sem):
     back = (4 - scal[1]) & 3
     refs = (r0, r3, r2, r1)
-    fh, fl = halves(factor[...])
+    gram = both[0:K, :]
+    raw = both[K : 2 * K, :]
+    row = lax.broadcasted_iota(jnp.int32, (K, K), 0)
+    column = lax.broadcasted_iota(jnp.int32, (K, K), 1)
+    before = jnp.where(scal[3] == 0, (row == column).astype(F32), raw[:, K : 2 * K])
+    factor = inverse_factor(gram[:, 0:K])
+    other = inverse_factor(before)
+    image = small_dot(factor, gram[:, K : 2 * K], ((1,), (1,)))
+    diag_ref[...] = small_dot(image, factor, ((1,), (1,)))
+    off_ref[...] = small_dot(small_dot(factor, raw[:, 0:K]), other, ((1,), (1,)))
+    fh, fl = halves(factor)
     matrix = jnp.concatenate([jnp.concatenate([fh, fh], axis=1), jnp.concatenate([fl, fl], axis=1)], axis=0)
+    whole = K * NX
 
     def body(t, carry):
         c, big = t >> 2, t & 3
         values = swap_blocks(turn([slab(r, t) for r in refs], back))
         for xx in range(4):
-            both = lax.dot_general(
+            mix = lax.dot_general(
                 matrix, jnp.concatenate(halves(values[xx]), axis=0), (((1,), (0,)), ((), ())), preferred_element_type=F32
             )
-            hold[pl.ds(c * (K * NX) + big * 4 + xx, K, stride=NX), :] = both[0:K, :] + both[K : 2 * K, :]
-        return carry
-
-    lax.fori_loop(0, GROUPS, body, 0)
-
-    def cast(i, carry):
+            hold[pl.ds(c * whole + big * 4 + xx, K, stride=NX), :] = mix[0:K, :] + mix[K : 2 * K, :]
+        return carry
+
+    def to_bf16(i, carry):
         at = pl.ds(pl.multiple_of(i * 128, 128), 128)
-        out_ref[at, :] = hold[at, :].astype(BF16)
-        return carry
-
-    lax.fori_loop(0, 3 * K * NX // 128, cast, 0)
+        cast[at, :] = hold[at, :].astype(BF16)
+        return carry
+
+    def copy(c):
+        at = pl.ds(c * whole, whole)
+        return pltpu.make_async_copy(cast.at[at, :], out_hbm.at[at, :], sem.at[c])
+
+    for c in range(3):
+        lax.fori_loop(4 * c, 4 * c + 4, body, 0)
+        lax.fori_loop(c * (whole // 128), (c + 1) * (whole // 128), to_bf16, 0)
+        copy(c).start()
+    for c in range(3):
+        copy(c).wait()
 
 
 def call(kernel, n_in, shapes, scratch=(), first=VM, rest=VM, params=PARAMS):
@@ -516,18 +524,19 @@
 
 
 def exchange(near, images):
+    own = total(near[0:K], shift_y)
+    h_up, h_dn = halo_y(images[3], images[0])
+    near = jnp.concatenate([own, near[K:]], axis=0)
     h_before = shift_x(near, 1)
     h_after = shift_x(near, 3)
-    own = near[0:K]
     far = shift_x(own, 2)
-    h_up, h_dn = halo_y(images[3], images[0])
     grams = (own + far) + (h_before[0:K] + h_after[0:K])
-    return total(grams, shift_y), (h_up, h_dn, h_before, h_after)
+    return grams, (h_up, h_dn, h_before, h_after)
 
 
 def blocks(start_vectors, face_x, face_y, face_z, masses, active):
     row = lax.axis_index("dom").astype(jnp.int32)
-    scal = jnp.stack([active[0], row & 3, row]).astype(jnp.int32)
+    scal = jnp.stack([active[0], row & 3, row, lax.axis_index("sub").astype(jnp.int32)]).astype(jnp.int32)
     start = start_vectors.reshape(3 * K * NX, LANES)
     fields = [f.reshape(NX, LANES) for f in (face_x, face_y, face_z, masses)]
     msg = f32(YROWS, LANES)
@@ -572,7 +581,7 @@
     img, grams, *packed = call(
         functools.partial(step_kernel, True),
         19,
-        (part, f32(K, LANES)) + (part,) * 4,
+        (f32(FROWS + K, LANES), f32(K, LANES)) + (part,) * 4,
         (acc, columns, side, side, columns) + (side,) * 8,
         first=SM,
     )(scal, *v, *av, fld, mat, n_up, n_dn, n_z, *ha, rows)
@@ -582,16 +591,20 @@
     raw_off = call(off_kernel, 5, f32(K, 2 * K))(*packed, before)
     both = jnp.concatenate([grams, raw_off], axis=0)
     both = total(total(both, shift_y), shift_x)
-    factor, diag = call(factor_kernel, 1, (f32(K, K), f32(K, K)))(both[0:K])
-    other = lax.ppermute(factor, "sub", behind)
-    off = call(cross_kernel, 3, f32(K, K))(factor, other, both[K:])
-    out = call(
+    hbm = pl.BlockSpec(memory_space=pl.ANY)
+    out, diag, off = pl.pallas_call(
         out_kernel,
-        6,
-        jax.ShapeDtypeStruct((3 * K * NX, LANES), BF16),
-        (pltpu.VMEM((3 * K * NX, LANES), F32),),
-        first=SM,
-    )(scal, factor, *got)
+        out_shape=(jax.ShapeDtypeStruct((3 * K * NX, LANES), BF16), f32(K, K), f32(K, K)),
+        in_specs=[SM] + [VM] * 5,
+        out_specs=(hbm, VM, VM),
+        scratch_shapes=[
+            pltpu.VMEM((3 * K * NX, LANES), F32),
+            pltpu.VMEM((3 * K * NX, LANES), BF16),
+            pltpu.SemaphoreType.DMA((3,)),
+        ],
+        compiler_params=PARAMS,
+        name="rows",
+    )(scal, both, *got)
     return (out.reshape(1, 3, K, 1, NX, LANES), diag[None], off[None])
 
 

time: 169 us -> 171 us (1.012)
  waiting for transfers between devices: 52.3 us -> 60 us
  starting transfers between devices: 63.1 us -> 56.9 us
    ppermute x17, waiting for transfers between devices: 28 us -> 50.8 us  [shift_x(): lax.ppermute(value, 'dom', [(i, (i & 12) + (i + d & 3)) for i in range(16)])]
    ppermute x9, waiting for transfers between devices: 15.9 us -> 0.55 us  [shift_y(): return lax.ppermute(value, 'dom', [(i, i + 4 * d & 15) for i in range(16)])]
    ppermute x17, starting transfers between devices: 28.4 us -> 22.9 us  [shift_x(): lax.ppermute(value, 'dom', [(i, (i & 12) + (i + d & 3)) for i in range(16)])]
    ppermute x1 -> x0, starting transfers between devices: 1.91 us -> none  [blocks(): other = lax.ppermute(factor, 'sub', behind)]
    pallas_call x4 -> x2, Pallas kernels: 19.1 us -> 19.3 us  [the longest x1 9.87 us: blocks(): pl.pallas_call(out_kernel, out_shape=(jax.ShapeDtypeStruct((3 * K * NX, L...]
  transfers between devices with their start and end apart: 34 -> 33, of which waited for: 15 -> 12; matrix products, arithmetic and copies ran while one was open for 0% -> 0% of each run, Pallas kernels for 8% -> 3%
where the time goes in v4:
time: 171 us; the launch traced here: 169 us
  waiting for transfers between devices  60 us (35%)
  starting transfers between devices  56.9 us (33%)
  Pallas kernels  48.4 us (28%)
  between operations  1.76 us (1%)
    ppermute x17, waiting for transfers between devices, shift_x(): lax.ppermute(value, 'dom', [(i, (i & 12) + (i + d & 3)) for i in range(16)])  50.8 us
    ppermute x17, starting transfers between devices, shift_x(): lax.ppermute(value, 'dom', [(i, (i & 12) + (i + d & 3)) for i in range(16)])  22.9 us
    ppermute x9, starting transfers between devices, shift_y(): return lax.ppermute(value, 'dom', [(i, i + 4 * d & 15) for i in range(16)])  14.4 us
    ppermute x3, starting transfers between devices, halo_y(): h_dn = lax.ppermute(y_up, 'dom', [(i, i + 4) for i in range(12)])  13.7 us
    pallas_call x1, Pallas kernels, blocks(): pl.pallas_call(out_kernel, out_shape=(jax.ShapeDtypeStruct((3 * K * NX, L...  9.87 us
    pallas_call x1, Pallas kernels, blocks(): call(functools.partial(step_kernel, False), 18, (msg,) * 8 + (near, msg,...  9.56 us
    pallas_call x1, Pallas kernels, blocks(): call(functools.partial(step_kernel, True), 19, (f32(FROWS + K, LANES), f3...  9.47 us
    ppermute x1, waiting for transfers between devices, blocks(): before = lax.ppermute(img, 'sub', behind)  8.73 us
  transfers between devices with their start and end apart: 33, of which 12 were waited for; matrix products, arithmetic and copies ran while one was open for 0% of the time, Pallas kernels for 3%

profile of v4, /device:TPU:128, one launch (start us, length us, event | category | flops | bytes accessed | tf_op | source)
XLA Modules:
  0.0 168.8 jit_solution(4676764399729143732)
XLA Ops:
  1.3 0.7 pad_add_fusion.scal
  1.9 5.6 %shard_map.85 = (f32[784,128]{1,0:T(8,128)}, f32[784,128]{1,0:T(8,128)}, f32[784,128]{1,0:T(8,128)}, f32[784,128]{1,0:T(8,128)}) custom-call(s32[4]{0:T(128)} %pad_add_fusion.scal, f32[3072,128]{1,0:T(8,128)} %bitcast.13, f32[16,128]{1,0:T(8,128)} %bitcast.14, f32[16,128]{1,0:T(8,128)} %bitcast.15, f32[16,128]{1,0:T(8,128)} %bitcast.16, f32[16,128]{1,0:T(8,128)} %bitcast.17), custom_call_target="tpu_custom_call" | custom-call | tf_op jit(solution)/shard_map/pallas_call | solution.py:547
  7.6 1.6 collective-permute-start
  9.1 2.7 %collective-permute-start.1 = (f32[784,128]{1,0:T(8,128)}, f32[784,128]{1,0:T(8,128)S(1)}, u32[]{:S(2)}, u32[]{:S(2)}) collective-permute-start(f32[784,128]{1,0:T(8,128)} %get-tuple-element.43), channel_id=1, source_target_pairs={{0,2},{1,3},{2,0},{3,1},{4,6},{5,7},{6,4},{7,5},{8,10},{9,11},{10,... | collective-permute-start | bytes 1204232 | tf_op jit(solution)/shard_map/ppermute | solution.py:499
  11.9 1.4 collective-permute-start.2
  13.3 6.9 %collective-permute-done.r1 = f32[784,128]{1,0:T(8,128)S(1)} collective-permute-done((f32[784,128]{1,0:T(8,128)}, f32[784,128]{1,0:T(8,128)S(1)}, u32[]{:S(2)}, u32[]{:S(2)}) %collective-permute-start) | collective-permute-done | bytes 401440 | tf_op jit(solution)/shard_map/ppermute | solution.py:499
  20.2 9.4 %collective-permute-done.1.r2 = f32[784,128]{1,0:T(8,128)S(1)} collective-permute-done((f32[784,128]{1,0:T(8,128)}, f32[784,128]{1,0:T(8,128)S(1)}, u32[]{:S(2)}, u32[]{:S(2)}) %collective-permute-start.1) | collective-permute-done | bytes 401440 | tf_op jit(solution)/shard_map/ppermute | solution.py:499
  29.7 1.0 copy-done
  30.7 2.5 %shard_map.86 = (f32[784,128]{1,0:T(8,128)S(1)}, f32[784,128]{1,0:T(8,128)S(1)}, f32[784,128]{1,0:T(8,128)S(1)}, f32[784,128]{1,0:T(8,128)S(1)}, f32[224,128]{1,0:T(8,128)S(1)}) custom-call(s32[4]{0:T(128)S(1)} %copy-done.1, f32[784,128]{1,0:T(8,128)S(1)} %copy-done, f32[784,128]{1,0:T(8,128)S(1)} %collective-permute-done.r1, ...), custom_call_target="tpu_custom_call" | custom-call | tf_op jit(solution)/shard_map/pallas_call | solution.py:559
  33.2 1.3 collective-permute-start.3
  34.5 4.6 %collective-permute-start.4 = (f32[784,128]{1,0:T(8,128)S(1)}, f32[784,128]{1,0:T(8,128)S(1)}, u32[]{:S(2)}, u32[]{:S(2)}) collective-permute-start(f32[784,128]{1,0:T(8,128)S(1)} %get-tuple-element.48.b3.refs_3_), channel_id=1, source_target_pairs={{0,4},{1,5},{2,6},{3,7},{4,8},{5,9},{6,10},{7,11},{8,12},{9,13},{1... | collective-permute-start | bytes 1204232 | tf_op jit(solution)/shard_map/ppermute | solution.py:507
  39.1 2.3 %collective-permute-start.6 = (f32[224,128]{1,0:T(8,128)S(1)}, f32[224,128]{1,0:T(8,128)S(1)}, u32[]{:S(2)}, u32[]{:S(2)}) collective-permute-start(f32[224,128]{1,0:T(8,128)S(1)} %get-tuple-element.49), channel_id=1, source_target_pairs={{0,3},{1,0},{2,1},{3,2},{4,7},{5,4},{6,5},{7,6},{8,11},{9,8},{10,9... | collective-permute-start | bytes 344072 | tf_op jit(solution)/shard_map/ppermute | solution.py:499
  41.4 2.5 %collective-permute-done.6.h_after = f32[224,128]{1,0:T(8,128)S(1)} collective-permute-done((f32[224,128]{1,0:T(8,128)S(1)}, f32[224,128]{1,0:T(8,128)S(1)}, u32[]{:S(2)}, u32[]{:S(2)}) %collective-permute-start.6) | collective-permute-done | bytes 114720 | tf_op jit(solution)/shard_map/ppermute | solution.py:499
  44.0 3.5 %collective-permute-done.5.h_before = f32[224,128]{1,0:T(8,128)S(1)} collective-permute-done((f32[224,128]{1,0:T(8,128)S(1)}, f32[224,128]{1,0:T(8,128)S(1)}, u32[]{:S(2)}, u32[]{:S(2)}) %collective-permute-start.5) | collective-permute-done | bytes 114720 | tf_op jit(solution)/shard_map/ppermute | solution.py:499
  47.4 6.0 %shard_map.87 = (f32[784,128]{1,0:T(8,128)S(1)}, f32[784,128]{1,0:T(8,128)S(1)}, f32[784,128]{1,0:T(8,128)S(1)}, f32[784,128]{1,0:T(8,128)S(1)}, f32[160,128]{1,...) custom-call(s32[4]{0:T(128)S(1)} %copy-done.1, f32[784,128]{1,0:T(8,128)S(1)} %get-tuple-element.45.b0.refs_0_, ...), custom_call_target="tpu_custom_call" | custom-call | tf_op jit(solution)/shard_map/pallas_call | solution.py:563
  53.4 1.6 collective-permute-start.8
  55.1 1.8 %collective-permute-start.9 = (f32[64,128]{1,0:T(8,128)S(1)}, f32[64,128]{1,0:T(8,128)S(1)}, u32[]{:S(2)}, u32[]{:S(2)}) collective-permute-start(f32[64,128]{1,0:T(8,128)S(1)} %slice.24), channel_id=1, source_target_pairs={{0,12},{1,13},{2,14},{3,15},{4,0},{5,1},{6,2},{7,3},{8,4},{9,5},{1... | collective-permute-start | bytes 98312 | tf_op jit(solution)/shard_map/ppermute | solution.py:503
  56.9 1.9 %collective-permute-start.7 = (f32[64,128]{1,0:T(8,128)S(1)}, f32[64,128]{1,0:T(8,128)S(1)}, u32[]{:S(2)}, u32[]{:S(2)}) collective-permute-start(f32[64,128]{1,0:T(8,128)S(1)} %slice.24), channel_id=1, source_target_pairs={{0,8},{1,9},{2,10},{3,11},{4,12},{5,13},{6,14},{7,15},{8,0},{9,1},... | collective-permute-start | bytes 98312 | tf_op jit(solution)/shard_map/ppermute | solution.py:503
  58.8 1.3 collective-permute-start.13
  60.1 4.6 %collective-permute-start.14 = (f32[784,128]{1,0:T(8,128)S(1)}, f32[784,128]{1,0:T(8,128)S(1)}, u32[]{:S(2)}, u32[]{:S(2)}) collective-permute-start(f32[784,128]{1,0:T(8,128)S(1)} %get-tuple-element.53.refs_7_), channel_id=1, source_target_pairs={{0,4},{1,5},{2,6},{3,7},{4,8},{5,9},{6,10},{7,11},{8,12},{9,13},{1... | collective-permute-start | bytes 1204232 | tf_op jit(solution)/shard_map/ppermute | solution.py:507
  64.7 3.3 %collective-permute-start.12 = (f32[288,128]{1,0:T(8,128)S(1)}, f32[288,128]{1,0:T(8,128)S(1)}, u32[]{:S(2)}, u32[]{:S(2)}) collective-permute-start(f32[288,128]{1,0:T(8,128)S(1)} %pad_maximum_fusion), channel_id=1, source_target_pairs={{0,3},{1,0},{2,1},{3,2},{4,7},{5,4},{6,5},{7,6},{8,11},{9,8},{10,9... | collective-permute-start | bytes 442376 | tf_op jit(solution)/shard_map/ppermute | solution.py:499
  68.0 1.6 collective-permute-start.10
  69.6 4.0 %collective-permute-done.10 = f32[64,128]{1,0:T(8,128)S(1)} collective-permute-done((f32[64,128]{1,0:T(8,128)S(1)}, f32[64,128]{1,0:T(8,128)S(1)}, u32[]{:S(2)}, u32[]{:S(2)}) %collective-permute-start.10) | collective-permute-done | bytes 32800 | tf_op jit(solution)/shard_map/ppermute | solution.py:499
  73.5 1.2 collective-permute-done.11.refs_15_
  74.7 2.5 %shard_map.88.refs_9_ = bf16[128,256]{1,0:T(8,128)(2,1)S(1)} custom-call(f32[64,128]{1,0:T(8,128)S(1)} %fusion.1.grams), custom_call_target="tpu_custom_call" | custom-call | tf_op jit(solution)/shard_map/pallas_call | solution.py:568
  77.2 9.6 %shard_map.89 = (f32[784,128]{1,0:T(8,128)S(1)}, f32[784,128]{1,0:T(8,128)S(1)}, f32[784,128]{1,0:T(8,128)S(1)}, f32[784,128]{1,0:T(8,128)S(1)}, f32[784,128]{1,...) custom-call(s32[4]{0:T(128)S(1)} %copy-done.1, ...), custom_call_target="tpu_custom_call" | custom-call | tf_op jit(solution)/shard_map/pallas_call | solution.py:569
  86.8 1.2 collective-permute-start.16
  88.0 2.3 %collective-permute-start.17 = (f32[64,128]{1,0:T(8,128)S(1)}, f32[64,128]{1,0:T(8,128)S(1)}, u32[]{:S(2)}, u32[]{:S(2)}) collective-permute-start(f32[64,128]{1,0:T(8,128)S(1)} %slice.28), channel_id=1, source_target_pairs={{0,12},{1,13},{2,14},{3,15},{4,0},{5,1},{6,2},{7,3},{8,4},{9,5},{1... | collective-permute-start | bytes 98312 | tf_op jit(solution)/shard_map/ppermute | solution.py:503
  90.8 1.3 collective-permute-start.21
  92.1 4.6 %collective-permute-start.22 = (f32[784,128]{1,0:T(8,128)S(1)}, f32[784,128]{1,0:T(8,128)S(1)}, u32[]{:S(2)}, u32[]{:S(2)}) collective-permute-start(f32[784,128]{1,0:T(8,128)S(1)} %get-tuple-element.64.refs_7_), channel_id=1, source_target_pairs={{0,4},{1,5},{2,6},{3,7},{4,8},{5,9},{6,10},{7,11},{8,12},{9,13},{1... | collective-permute-start | bytes 1204232 | tf_op jit(solution)/shard_map/ppermute | solution.py:507
  96.8 2.0 %collective-permute-start.20 = (f32[288,128]{1,0:T(8,128)S(1)}, f32[288,128]{1,0:T(8,128)S(1)}, u32[]{:S(2)}, u32[]{:S(2)}) collective-permute-start(f32[288,128]{1,0:T(8,128)S(1)} %pad_maximum_fusion.1), channel_id=1, source_target_pairs={{0,3},{1,0},{2,1},{3,2},{4,7},{5,4},{6,5},{7,6},{8,11},{9,8},{10,9... | collective-permute-start | bytes 442376 | tf_op jit(solution)/shard_map/ppermute | solution.py:499
  98.9 1.5 collective-permute-start.18
  100.4 4.0 %collective-permute-done.18 = f32[64,128]{1,0:T(8,128)S(1)} collective-permute-done((f32[64,128]{1,0:T(8,128)S(1)}, f32[64,128]{1,0:T(8,128)S(1)}, u32[]{:S(2)}, u32[]{:S(2)}) %collective-permute-start.18) | collective-permute-done | bytes 32800 | tf_op jit(solution)/shard_map/ppermute | solution.py:499
  104.4 1.1 collective-permute-done.19.refs_15_
  105.5 2.5 %shard_map.90.refs_9_ = bf16[128,256]{1,0:T(8,128)(2,1)S(1)} custom-call(f32[64,128]{1,0:T(8,128)S(1)} %fusion.grams), custom_call_target="tpu_custom_call" | custom-call | tf_op jit(solution)/shard_map/pallas_call | solution.py:578
  108.1 9.5 %shard_map.91 = (f32[832,128]{1,0:T(8,128)S(1)}, f32[64,128]{1,0:T(8,128)S(1)}, f32[768,128]{1,0:T(8,128)S(1)}, f32[768,128]{1,0:T(8,128)S(1)}, f32[768,128]{1,0:T(8,128)S(1)}, /*index=5*/f32[768,128]{1,0:T(8,128)S(1)}) custom-call(s32[4]{0:T(128)S(1)} %copy-done.1, f32[784,128]{1,0:T(8,128)S(1)} %get-tuple-element.57.refs_0_, ...), custom_call_target="tpu_custom_call" | custom-call | tf_op jit(solution)/shard_map/pallas_call | solution.py:581
  117.5 1.9 %collective-permute-start.23 = (f32[832,128]{1,0:T(8,128)S(1)}, f32[832,128]{1,0:T(8,128)S(1)}, u32[]{:S(2)}, u32[]{:S(2)}) collective-permute-start(f32[832,128]{1,0:T(8,128)S(1)} %get-tuple-element.75), channel_id=1, source_target_pairs={{0,16},{16,32},{32,48},{48,64},{64,80},{80,96},{96,112},{112,128},... | collective-permute-start | bytes 1277960 | tf_op jit(solution)/shard_map/ppermute | solution.py:589
  119.5 8.7 %collective-permute-done.23.img_ref = f32[832,128]{1,0:T(8,128)S(1)} collective-permute-done((f32[832,128]{1,0:T(8,128)S(1)}, f32[832,128]{1,0:T(8,128)S(1)}, u32[]{:S(2)}, u32[]{:S(2)}) %collective-permute-start.23) | collective-permute-done | bytes 426016 | tf_op jit(solution)/shard_map/ppermute | solution.py:589
  128.6 1.0 collective-permute-start.25
  129.6 2.3 %collective-permute-start.26 = (f32[128,128]{1,0:T(8,128)S(1)}, f32[128,128]{1,0:T(8,128)S(1)}, u32[]{:S(2)}, u32[]{:S(2)}) collective-permute-start(f32[128,128]{1,0:T(8,128)S(1)} %pad_maximum_fusion.2), channel_id=1, source_target_pairs={{0,12},{1,13},{2,14},{3,15},{4,0},{5,1},{6,2},{7,3},{8,4},{9,5},{1... | collective-permute-start | bytes 196616 | tf_op jit(solution)/shard_map/ppermute | solution.py:503
  131.9 1.8 %collective-permute-start.24 = (f32[128,128]{1,0:T(8,128)S(1)}, f32[128,128]{1,0:T(8,128)S(1)}, u32[]{:S(2)}, u32[]{:S(2)}) collective-permute-start(f32[128,128]{1,0:T(8,128)S(1)} %pad_maximum_fusion.2), channel_id=1, source_target_pairs={{0,8},{1,9},{2,10},{3,11},{4,12},{5,13},{6,14},{7,15},{8,0},{9,1},... | collective-permute-start | bytes 196616 | tf_op jit(solution)/shard_map/ppermute | solution.py:503
  133.7 3.4 %collective-permute-start.31 = (f32[768,128]{1,0:T(8,128)S(1)}, f32[768,128]{1,0:T(8,128)S(1)}, u32[]{:S(2)}, u32[]{:S(2)}) collective-permute-start(f32[768,128]{1,0:T(8,128)S(1)} %get-tuple-element.73.w2), channel_id=1, source_target_pairs={{0,2},{1,3},{2,0},{3,1},{4,6},{5,7},{6,4},{7,5},{8,10},{9,11},{10,... | collective-permute-start | bytes 1179656 | tf_op jit(solution)/shard_map/ppermute | solution.py:499
  137.1 0.5 collective-permute-done.24
  137.7 2.0 %collective-permute-start.29 = (f32[128,128]{1,0:T(8,128)S(1)}, f32[128,128]{1,0:T(8,128)S(1)}, u32[]{:S(2)}, u32[]{:S(2)}) collective-permute-start(f32[128,128]{1,0:T(8,128)S(1)} %add_add_fusion.1), channel_id=1, source_target_pairs={{0,3},{1,0},{2,1},{3,2},{4,7},{5,4},{6,5},{7,6},{8,11},{9,8},{10,9... | collective-permute-start | bytes 196616 | tf_op jit(solution)/shard_map/ppermute | solution.py:499
  139.8 13.2 %collective-permute-done.29 = f32[128,128]{1,0:T(8,128)S(1)} collective-permute-done((f32[128,128]{1,0:T(8,128)S(1)}, f32[128,128]{1,0:T(8,128)S(1)}, u32[]{:S(2)}, u32[]{:S(2)}) %collective-permute-start.29) | collective-permute-done | bytes 65568 | tf_op jit(solution)/shard_map/ppermute | solution.py:499
  153.0 0.9 collective-permute-start.27
  153.9 4.9 %collective-permute-done.27 = f32[128,128]{1,0:T(8,128)S(1)} collective-permute-done((f32[128,128]{1,0:T(8,128)S(1)}, f32[128,128]{1,0:T(8,128)S(1)}, u32[]{:S(2)}, u32[]{:S(2)}) %collective-permute-start.27) | collective-permute-done | bytes 65568 | tf_op jit(solution)/shard_map/ppermute | solution.py:499
  158.8 9.9 %rows.1 = (bf16[3072,128]{1,0:T(8,128)(2,1)}, f32[64,64]{1,0:T(8,128)}, f32[64,64]{1,0:T(8,128)}) custom-call(s32[4]{0:T(128)S(1)} %copy-done.1, f32[128,128]{1,0:T(8,128)S(1)} %add_add_fusion.both, f32[768,128]{1,0:T(8,128)S(1)} %get-tuple-element.71.w0.r0, f32[768,128]{1,0:T(8,128)S(1)} %collective-permute-done.30.r1, ...), custom_call_target="tpu_custom_call" | custom-call | tf_op jit(solution)/shard_map/rows/pallas_call | solution.py:595
  (45 shorter events, 1.2 us)
Async XLA Ops:
  1.9 27.7 %copy-start.1 = (s32[4]{0:T(128)S(1)}, s32[4]{0:T(128)}, u32[]{:S(2)}) copy-start(s32[4]{0:T(128)} %pad_add_fusion.scal) | copy-start | bytes 52
  7.6 12.7 %collective-permute-start = (f32[784,128]{1,0:T(8,128)}, f32[784,128]{1,0:T(8,128)S(1)}, u32[]{:S(2)}, u32[]{:S(2)}) collective-permute-start(f32[784,128]{1,0:T(8,128)} %get-tuple-element.42), channel_id=1, source_target_pairs={{0,1},{1,2},{2,3},{3,0},{4,5},{5,6},{6,7},{7,4},{8,9},{9,10},{10,1... | collective-permute-start | bytes 1204232 | tf_op jit(solution)/shard_map/ppermute | solution.py:499
  9.1 20.5 %collective-permute-start.1 = (f32[784,128]{1,0:T(8,128)}, f32[784,128]{1,0:T(8,128)S(1)}, u32[]{:S(2)}, u32[]{:S(2)}) collective-permute-start(f32[784,128]{1,0:T(8,128)} %get-tuple-element.43), channel_id=1, source_target_pairs={{0,2},{1,3},{2,0},{3,1},{4,6},{5,7},{6,4},{7,5},{8,10},{9,11},{10,... | collective-permute-start | bytes 1204232 | tf_op jit(solution)/shard_map/ppermute | solution.py:499
  11.9 17.8 %collective-permute-start.2 = (f32[784,128]{1,0:T(8,128)}, f32[784,128]{1,0:T(8,128)S(1)}, u32[]{:S(2)}, u32[]{:S(2)}) collective-permute-start(f32[784,128]{1,0:T(8,128)} %get-tuple-element.44), channel_id=1, source_target_pairs={{0,3},{1,0},{2,1},{3,2},{4,7},{5,4},{6,5},{7,6},{8,11},{9,8},{10,9... | collective-permute-start | bytes 1204232 | tf_op jit(solution)/shard_map/ppermute | solution.py:499
  29.7 1.0 copy-start
  33.2 14.2 %collective-permute-start.3 = (f32[784,128]{1,0:T(8,128)S(1)}, f32[784,128]{1,0:T(8,128)S(1)}, u32[]{:S(2)}, u32[]{:S(2)}) collective-permute-start(f32[784,128]{1,0:T(8,128)S(1)} %get-tuple-element.45.b0.refs_0_), channel_id=1, source_target_pairs={{4,0},{5,1},{6,2},{7,3},{8,4},{9,5},{10,6},{11,7},{12,8},{13,9},{1... | collective-permute-start | bytes 1204232 | tf_op jit(solution)/shard_map/ppermute | solution.py:508
  34.5 12.9 %collective-permute-start.4 = (f32[784,128]{1,0:T(8,128)S(1)}, f32[784,128]{1,0:T(8,128)S(1)}, u32[]{:S(2)}, u32[]{:S(2)}) collective-permute-start(f32[784,128]{1,0:T(8,128)S(1)} %get-tuple-element.48.b3.refs_3_), channel_id=1, source_target_pairs={{0,4},{1,5},{2,6},{3,7},{4,8},{5,9},{6,10},{7,11},{8,12},{9,13},{1... | collective-permute-start | bytes 1204232 | tf_op jit(solution)/shard_map/ppermute | solution.py:507
  39.1 4.9 %collective-permute-start.6 = (f32[224,128]{1,0:T(8,128)S(1)}, f32[224,128]{1,0:T(8,128)S(1)}, u32[]{:S(2)}, u32[]{:S(2)}) collective-permute-start(f32[224,128]{1,0:T(8,128)S(1)} %get-tuple-element.49), channel_id=1, source_target_pairs={{0,3},{1,0},{2,1},{3,2},{4,7},{5,4},{6,5},{7,6},{8,11},{9,8},{10,9... | collective-permute-start | bytes 344072 | tf_op jit(solution)/shard_map/ppermute | solution.py:499
  41.4 6.0 %collective-permute-start.5 = (f32[224,128]{1,0:T(8,128)S(1)}, f32[224,128]{1,0:T(8,128)S(1)}, u32[]{:S(2)}, u32[]{:S(2)}) collective-permute-start(f32[224,128]{1,0:T(8,128)S(1)} %get-tuple-element.49), channel_id=1, source_target_pairs={{0,1},{1,2},{2,3},{3,0},{4,5},{5,6},{6,7},{7,4},{8,9},{9,10},{10,1... | collective-permute-start | bytes 344072 | tf_op jit(solution)/shard_map/ppermute | solution.py:499
  53.4 11.2 %collective-permute-start.8 = (f32[64,128]{1,0:T(8,128)S(1)}, f32[64,128]{1,0:T(8,128)S(1)}, u32[]{:S(2)}, u32[]{:S(2)}) collective-permute-start(f32[64,128]{1,0:T(8,128)S(1)} %slice.24), channel_id=1, source_target_pairs={{0,4},{1,5},{2,6},{3,7},{4,8},{5,9},{6,10},{7,11},{8,12},{9,13},{1... | collective-permute-start | bytes 98312 | tf_op jit(solution)/shard_map/ppermute | solution.py:503
  55.1 9.6 %collective-permute-start.9 = (f32[64,128]{1,0:T(8,128)S(1)}, f32[64,128]{1,0:T(8,128)S(1)}, u32[]{:S(2)}, u32[]{:S(2)}) collective-permute-start(f32[64,128]{1,0:T(8,128)S(1)} %slice.24), channel_id=1, source_target_pairs={{0,12},{1,13},{2,14},{3,15},{4,0},{5,1},{6,2},{7,3},{8,4},{9,5},{1... | collective-permute-start | bytes 98312 | tf_op jit(solution)/shard_map/ppermute | solution.py:503
  56.9 7.8 %collective-permute-start.7 = (f32[64,128]{1,0:T(8,128)S(1)}, f32[64,128]{1,0:T(8,128)S(1)}, u32[]{:S(2)}, u32[]{:S(2)}) collective-permute-start(f32[64,128]{1,0:T(8,128)S(1)} %slice.24), channel_id=1, source_target_pairs={{0,8},{1,9},{2,10},{3,11},{4,12},{5,13},{6,14},{7,15},{8,0},{9,1},... | collective-permute-start | bytes 98312 | tf_op jit(solution)/shard_map/ppermute | solution.py:503
  58.8 18.5 %collective-permute-start.13 = (f32[784,128]{1,0:T(8,128)S(1)}, f32[784,128]{1,0:T(8,128)S(1)}, u32[]{:S(2)}, u32[]{:S(2)}) collective-permute-start(f32[784,128]{1,0:T(8,128)S(1)} %get-tuple-element.50.refs_4_), channel_id=1, source_target_pairs={{4,0},{5,1},{6,2},{7,3},{8,4},{9,5},{10,6},{11,7},{12,8},{13,9},{1... | collective-permute-start | bytes 1204232 | tf_op jit(solution)/shard_map/ppermute | solution.py:508
  60.1 17.2 %collective-permute-start.14 = (f32[784,128]{1,0:T(8,128)S(1)}, f32[784,128]{1,0:T(8,128)S(1)}, u32[]{:S(2)}, u32[]{:S(2)}) collective-permute-start(f32[784,128]{1,0:T(8,128)S(1)} %get-tuple-element.53.refs_7_), channel_id=1, source_target_pairs={{0,4},{1,5},{2,6},{3,7},{4,8},{5,9},{6,10},{7,11},{8,12},{9,13},{1... | collective-permute-start | bytes 1204232 | tf_op jit(solution)/shard_map/ppermute | solution.py:507
  64.7 8.8 %collective-permute-start.12 = (f32[288,128]{1,0:T(8,128)S(1)}, f32[288,128]{1,0:T(8,128)S(1)}, u32[]{:S(2)}, u32[]{:S(2)}) collective-permute-start(f32[288,128]{1,0:T(8,128)S(1)} %pad_maximum_fusion), channel_id=1, source_target_pairs={{0,3},{1,0},{2,1},{3,2},{4,7},{5,4},{6,5},{7,6},{8,11},{9,8},{10,9... | collective-permute-start | bytes 442376 | tf_op jit(solution)/shard_map/ppermute | solution.py:499
  68.0 6.7 %collective-permute-start.11 = (f32[288,128]{1,0:T(8,128)S(1)}, f32[288,128]{1,0:T(8,128)S(1)}, u32[]{:S(2)}, u32[]{:S(2)}) collective-permute-start(f32[288,128]{1,0:T(8,128)S(1)} %pad_maximum_fusion), channel_id=1, source_target_pairs={{0,1},{1,2},{2,3},{3,0},{4,5},{5,6},{6,7},{7,4},{8,9},{9,10},{10,1... | collective-permute-start | bytes 442376 | tf_op jit(solution)/shard_map/ppermute | solution.py:499
  68.0 5.5 %collective-permute-start.10 = (f32[64,128]{1,0:T(8,128)S(1)}, f32[64,128]{1,0:T(8,128)S(1)}, u32[]{:S(2)}, u32[]{:S(2)}) collective-permute-start(f32[64,128]{1,0:T(8,128)S(1)} %add_add_fusion.3), channel_id=1, source_target_pairs={{0,2},{1,3},{2,0},{3,1},{4,6},{5,7},{6,4},{7,5},{8,10},{9,11},{10,... | collective-permute-start | bytes 98312 | tf_op jit(solution)/shard_map/ppermute | solution.py:499
  86.8 9.9 %collective-permute-start.16 = (f32[64,128]{1,0:T(8,128)S(1)}, f32[64,128]{1,0:T(8,128)S(1)}, u32[]{:S(2)}, u32[]{:S(2)}) collective-permute-start(f32[64,128]{1,0:T(8,128)S(1)} %slice.28), channel_id=1, source_target_pairs={{0,4},{1,5},{2,6},{3,7},{4,8},{5,9},{6,10},{7,11},{8,12},{9,13},{1... | collective-permute-start | bytes 98312 | tf_op jit(solution)/shard_map/ppermute | solution.py:503
  88.0 8.7 %collective-permute-start.17 = (f32[64,128]{1,0:T(8,128)S(1)}, f32[64,128]{1,0:T(8,128)S(1)}, u32[]{:S(2)}, u32[]{:S(2)}) collective-permute-start(f32[64,128]{1,0:T(8,128)S(1)} %slice.28), channel_id=1, source_target_pairs={{0,12},{1,13},{2,14},{3,15},{4,0},{5,1},{6,2},{7,3},{8,4},{9,5},{1... | collective-permute-start | bytes 98312 | tf_op jit(solution)/shard_map/ppermute | solution.py:503
  90.3 6.4 %collective-permute-start.15 = (f32[64,128]{1,0:T(8,128)S(1)}, f32[64,128]{1,0:T(8,128)S(1)}, u32[]{:S(2)}, u32[]{:S(2)}) collective-permute-start(f32[64,128]{1,0:T(8,128)S(1)} %slice.28), channel_id=1, source_target_pairs={{0,8},{1,9},{2,10},{3,11},{4,12},{5,13},{6,14},{7,15},{8,0},{9,1},... | collective-permute-start | bytes 98312 | tf_op jit(solution)/shard_map/ppermute | solution.py:503
  90.8 17.2 %collective-permute-start.21 = (f32[784,128]{1,0:T(8,128)S(1)}, f32[784,128]{1,0:T(8,128)S(1)}, u32[]{:S(2)}, u32[]{:S(2)}) collective-permute-start(f32[784,128]{1,0:T(8,128)S(1)} %get-tuple-element.61.refs_4_), channel_id=1, source_target_pairs={{4,0},{5,1},{6,2},{7,3},{8,4},{9,5},{10,6},{11,7},{12,8},{13,9},{1... | collective-permute-start | bytes 1204232 | tf_op jit(solution)/shard_map/ppermute | solution.py:508
  92.1 15.9 %collective-permute-start.22 = (f32[784,128]{1,0:T(8,128)S(1)}, f32[784,128]{1,0:T(8,128)S(1)}, u32[]{:S(2)}, u32[]{:S(2)}) collective-permute-start(f32[784,128]{1,0:T(8,128)S(1)} %get-tuple-element.64.refs_7_), channel_id=1, source_target_pairs={{0,4},{1,5},{2,6},{3,7},{4,8},{5,9},{6,10},{7,11},{8,12},{9,13},{1... | collective-permute-start | bytes 1204232 | tf_op jit(solution)/shard_map/ppermute | solution.py:507
  96.8 7.6 %collective-permute-start.20 = (f32[288,128]{1,0:T(8,128)S(1)}, f32[288,128]{1,0:T(8,128)S(1)}, u32[]{:S(2)}, u32[]{:S(2)}) collective-permute-start(f32[288,128]{1,0:T(8,128)S(1)} %pad_maximum_fusion.1), channel_id=1, source_target_pairs={{0,3},{1,0},{2,1},{3,2},{4,7},{5,4},{6,5},{7,6},{8,11},{9,8},{10,9... | collective-permute-start | bytes 442376 | tf_op jit(solution)/shard_map/ppermute | solution.py:499
  98.8 6.7 %collective-permute-start.19 = (f32[288,128]{1,0:T(8,128)S(1)}, f32[288,128]{1,0:T(8,128)S(1)}, u32[]{:S(2)}, u32[]{:S(2)}) collective-permute-start(f32[288,128]{1,0:T(8,128)S(1)} %pad_maximum_fusion.1), channel_id=1, source_target_pairs={{0,1},{1,2},{2,3},{3,0},{4,5},{5,6},{6,7},{7,4},{8,9},{9,10},{10,1... | collective-permute-start | bytes 442376 | tf_op jit(solution)/shard_map/ppermute | solution.py:499
  98.9 5.5 %collective-permute-start.18 = (f32[64,128]{1,0:T(8,128)S(1)}, f32[64,128]{1,0:T(8,128)S(1)}, u32[]{:S(2)}, u32[]{:S(2)}) collective-permute-start(f32[64,128]{1,0:T(8,128)S(1)} %add_add_fusion.2), channel_id=1, source_target_pairs={{0,2},{1,3},{2,0},{3,1},{4,6},{5,7},{6,4},{7,5},{8,10},{9,11},{10,... | collective-permute-start | bytes 98312 | tf_op jit(solution)/shard_map/ppermute | solution.py:499
  117.5 10.7 %collective-permute-start.23 = (f32[832,128]{1,0:T(8,128)S(1)}, f32[832,128]{1,0:T(8,128)S(1)}, u32[]{:S(2)}, u32[]{:S(2)}) collective-permute-start(f32[832,128]{1,0:T(8,128)S(1)} %get-tuple-element.75), channel_id=1, source_target_pairs={{0,16},{16,32},{32,48},{48,64},{64,80},{80,96},{96,112},{112,128},... | collective-permute-start | bytes 1277960 | tf_op jit(solution)/shard_map/ppermute | solution.py:589
  128.6 8.6 %collective-permute-start.25 = (f32[128,128]{1,0:T(8,128)S(1)}, f32[128,128]{1,0:T(8,128)S(1)}, u32[]{:S(2)}, u32[]{:S(2)}) collective-permute-start(f32[128,128]{1,0:T(8,128)S(1)} %pad_maximum_fusion.2), channel_id=1, source_target_pairs={{0,4},{1,5},{2,6},{3,7},{4,8},{5,9},{6,10},{7,11},{8,12},{9,13},{1... | collective-permute-start | bytes 196616 | tf_op jit(solution)/shard_map/ppermute | solution.py:503
  129.6 7.5 %collective-permute-start.26 = (f32[128,128]{1,0:T(8,128)S(1)}, f32[128,128]{1,0:T(8,128)S(1)}, u32[]{:S(2)}, u32[]{:S(2)}) collective-permute-start(f32[128,128]{1,0:T(8,128)S(1)} %pad_maximum_fusion.2), channel_id=1, source_target_pairs={{0,12},{1,13},{2,14},{3,15},{4,0},{5,1},{6,2},{7,3},{8,4},{9,5},{1... | collective-permute-start | bytes 196616 | tf_op jit(solution)/shard_map/ppermute | solution.py:503
  131.9 5.8 %collective-permute-start.24 = (f32[128,128]{1,0:T(8,128)S(1)}, f32[128,128]{1,0:T(8,128)S(1)}, u32[]{:S(2)}, u32[]{:S(2)}) collective-permute-start(f32[128,128]{1,0:T(8,128)S(1)} %pad_maximum_fusion.2), channel_id=1, source_target_pairs={{0,8},{1,9},{2,10},{3,11},{4,12},{5,13},{6,14},{7,15},{8,0},{9,1},... | collective-permute-start | bytes 196616 | tf_op jit(solution)/shard_map/ppermute | solution.py:503
  133.7 25.1 %collective-permute-start.30 = (f32[768,128]{1,0:T(8,128)S(1)}, f32[768,128]{1,0:T(8,128)S(1)}, u32[]{:S(2)}, u32[]{:S(2)}) collective-permute-start(f32[768,128]{1,0:T(8,128)S(1)} %get-tuple-element.72.w1), channel_id=1, source_target_pairs={{0,1},{1,2},{2,3},{3,0},{4,5},{5,6},{6,7},{7,4},{8,9},{9,10},{10,1... | collective-permute-start | bytes 1179656 | tf_op jit(solution)/shard_map/ppermute | solution.py:499
  133.7 25.1 %collective-permute-start.31 = (f32[768,128]{1,0:T(8,128)S(1)}, f32[768,128]{1,0:T(8,128)S(1)}, u32[]{:S(2)}, u32[]{:S(2)}) collective-permute-start(f32[768,128]{1,0:T(8,128)S(1)} %get-tuple-element.73.w2), channel_id=1, source_target_pairs={{0,2},{1,3},{2,0},{3,1},{4,6},{5,7},{6,4},{7,5},{8,10},{9,11},{10,... | collective-permute-start | bytes 1179656 | tf_op jit(solution)/shard_map/ppermute | solution.py:499
  137.1 21.7 %collective-permute-start.32 = (f32[768,128]{1,0:T(8,128)S(1)}, f32[768,128]{1,0:T(8,128)S(1)}, u32[]{:S(2)}, u32[]{:S(2)}) collective-permute-start(f32[768,128]{1,0:T(8,128)S(1)} %get-tuple-element.74.w3), channel_id=1, source_target_pairs={{0,3},{1,0},{2,1},{3,2},{4,7},{5,4},{6,5},{7,6},{8,11},{9,8},{10,9... | collective-permute-start | bytes 1179656 | tf_op jit(solution)/shard_map/ppermute | solution.py:499
  137.7 15.3 %collective-permute-start.29 = (f32[128,128]{1,0:T(8,128)S(1)}, f32[128,128]{1,0:T(8,128)S(1)}, u32[]{:S(2)}, u32[]{:S(2)}) collective-permute-start(f32[128,128]{1,0:T(8,128)S(1)} %add_add_fusion.1), channel_id=1, source_target_pairs={{0,3},{1,0},{2,1},{3,2},{4,7},{5,4},{6,5},{7,6},{8,11},{9,8},{10,9... | collective-permute-start | bytes 196616 | tf_op jit(solution)/shard_map/ppermute | solution.py:499
  139.7 14.1 %collective-permute-start.28 = (f32[128,128]{1,0:T(8,128)S(1)}, f32[128,128]{1,0:T(8,128)S(1)}, u32[]{:S(2)}, u32[]{:S(2)}) collective-permute-start(f32[128,128]{1,0:T(8,128)S(1)} %add_add_fusion.1), channel_id=1, source_target_pairs={{0,1},{1,2},{2,3},{3,0},{4,5},{5,6},{6,7},{7,4},{8,9},{9,10},{10,1... | collective-permute-start | bytes 196616 | tf_op jit(solution)/shard_map/ppermute | solution.py:499
  153.0 5.8 %collective-permute-start.27 = (f32[128,128]{1,0:T(8,128)S(1)}, f32[128,128]{1,0:T(8,128)S(1)}, u32[]{:S(2)}, u32[]{:S(2)}) collective-permute-start(f32[128,128]{1,0:T(8,128)S(1)} %add_add_fusion.1), channel_id=1, source_target_pairs={{0,2},{1,3},{2,0},{3,1},{4,6},{5,7},{6,4},{7,5},{8,10},{9,11},{10,... | collective-permute-start | bytes 196616 | tf_op jit(solution)/shard_map/ppermute | solution.py:499

commit v5 on v4

--- a/solution.py
+++ b/solution.py
@@ -16,6 +16,8 @@
 GROUPS = SLABS // 4
 FROWS = GROUPS * K
 YROWS = FROWS + NX
+AROWS = 4 * K
+BROWS = 8 * K
 ZROWS = 3 * K + 2 * NX
 F32 = jnp.float32
 BF16 = jnp.bfloat16
@@ -80,37 +82,28 @@
     return [jnp.where(by >= 2, items[(i + 2) % 4], items[i]) for i in range(4)]
 
 
-def pack_kernel(scal, v_hbm, fx_hbm, fy_hbm, fz_hbm, m_hbm, p0, p1, p2, p3, v_ref, fx, fy, fz, m, v_sem, f_sem):
+def pack_rows(t, c, v_ref, active, px, outs_ref):
+    big = t & 3
+    values = []
+    for xx in range(4):
+        plane = big * 4 + xx
+        s = v_ref[pl.ds(c * (K * NX) + plane, K, stride=NX), :]
+        values.append(jnp.where(plane < active, s, 0.0))
+    for d, value in enumerate(turn(swap_blocks(values), px)):
+        put(outs_ref[d], t, value)
+
+
+def pack_a_kernel(scal, v_hbm, fx_hbm, fy_hbm, fz_hbm, m_hbm, p0, p1, p2, p3, v_ref, fx, fy, fz, m, v_sem, f_sem):
     active, px, row = scal[0], scal[1], scal[2]
-    whole = K * NX
-
-    def v_copy(c):
-        return pltpu.make_async_copy(v_hbm.at[pl.ds(c * whole, whole), :], v_ref.at[pl.ds(c * whole, whole), :], v_sem.at[c])
-
-    for c in range(3):
-        v_copy(c).start()
+    outs_ref = (p0, p1, p2, p3)
+    v_copy = pltpu.make_async_copy(v_hbm.at[pl.ds(0, K * NX), :], v_ref, v_sem.at[0])
+    v_copy.start()
     copies = [
         pltpu.make_async_copy(src, dst, f_sem.at[j])
         for j, (src, dst) in enumerate(((fx_hbm, fx), (fy_hbm, fy), (fz_hbm, fz), (m_hbm, m)))
     ]
     for copy in copies:
         copy.start()
-    outs_ref = (p0, p1, p2, p3)
-
-    def body(t, carry):
-        c, big = t >> 2, t & 3
-        values = []
-        for xx in range(4):
-            plane = big * 4 + xx
-            s = v_ref[pl.ds(c * whole + plane, K, stride=NX), :]
-            values.append(jnp.where(plane < active, s, 0.0))
-        for d, value in enumerate(turn(swap_blocks(values), px)):
-            put(outs_ref[d], t, value)
-        return carry
-
-    for c in range(3):
-        v_copy(c).wait()
-        lax.fori_loop(c * 4, c * 4 + 4, body, 0)
     for copy in copies:
         copy.wait()
     plane = lax.broadcasted_iota(jnp.int32, (NX, LANES), 0)
@@ -122,7 +115,32 @@
     for j, field in enumerate((fx, fy, fz, m)):
         values = [field[pl.ds(xx, 4, stride=4), :] for xx in range(4)]
         for d, value in enumerate(turn(swap_blocks(values), px)):
-            outs_ref[d][pl.ds(FROWS + 4 * j, 4), :] = value
+            outs_ref[d][pl.ds(AROWS + 4 * j, 4), :] = value
+    v_copy.wait()
+
+    def body(t, carry):
+        pack_rows(t, 0, v_ref, active, px, outs_ref)
+        return carry
+
+    lax.fori_loop(0, 4, body, 0)
+
+
+def pack_b_kernel(scal, v_hbm, p0, p1, p2, p3, v_ref, v_sem):
+    active, px = scal[0], scal[1]
+    whole = K * NX
+
+    def v_copy(c):
+        return pltpu.make_async_copy(v_hbm.at[pl.ds((c + 1) * whole, whole), :], v_ref.at[pl.ds(c * whole, whole), :], v_sem.at[c])
+
+    def body(t, carry):
+        pack_rows(t, t >> 2, v_ref, active, px, (p0, p1, p2, p3))
+        return carry
+
+    for c in range(2):
+        v_copy(c).start()
+    for c in range(2):
+        v_copy(c).wait()
+        lax.fori_loop(4 * c, 4 * c + 4, body, 0)
 
 
 def edges(t, values, z_ref, base):
@@ -137,7 +155,7 @@
     z_ref[at, :] = jnp.where(big == 0, 0.0, z_ref[at, :]) + roll(ends, big * 2)
 
 
-def unpack_kernel(scal, r0, r1, r2, r3, b0, b1, b2, b3, z_ref):
+def unpack_a_kernel(scal, r0, r1, r2, r3, b0, b1, b2, b3, z_ref):
     back = (4 - scal[1]) & 3
     refs = (r0, r3, r2, r1)
     outs = (b0, b1, b2, b3)
@@ -149,12 +167,34 @@
         edges(t, values, z_ref, 0)
         return carry
 
-    lax.fori_loop(0, GROUPS, body, 0)
-    values = turn([r[pl.ds(FROWS, NX), :] for r in refs], back)
+    lax.fori_loop(0, 4, body, 0)
+    values = turn([r[pl.ds(AROWS, NX), :] for r in refs], back)
     for r in range(4):
-        outs[r][pl.ds(FROWS, NX), :] = values[r]
-        z_ref[pl.ds(3 * K + 4 * r, 4), :] = values[r][8:12, :]
+        outs[r][pl.ds(AROWS, NX), :] = values[r]
+        z_ref[pl.ds(K + 4 * r, 4), :] = values[r][8:12, :]
+
+
+def unpack_b_kernel(scal, r0, r1, r2, r3, e0, e1, e2, e3, za_ref, b0, b1, b2, b3, c0, c1, z_ref):
+    back = (4 - scal[1]) & 3
+    refs = (r0, r3, r2, r1)
+    outs = (b0, b1, b2, b3)
+    for r, early in enumerate((e0, e1, e2, e3)):
+        outs[r][0:AROWS, :] = early[0:AROWS, :]
+        outs[r][FROWS:YROWS, :] = early[AROWS : AROWS + NX, :]
+    z_ref[0:K, :] = za_ref[0:K, :]
+    z_ref[pl.ds(3 * K, NX), :] = za_ref[pl.ds(K, NX), :]
     z_ref[pl.ds(3 * K + NX, NX), :] = jnp.zeros((NX, LANES), F32)
+
+    def body(t, carry):
+        values = turn([slab(r, t) for r in refs], back)
+        for r in range(4):
+            put(outs[r], t + 4, values[r])
+        put(c0, t, values[0])
+        put(c1, t, values[3])
+        edges(t + 4, values, z_ref, 0)
+        return carry
+
+    lax.fori_loop(0, 8, body, 0)
 
 
 def line(fld, which, r, big):
@@ -211,8 +251,12 @@
 
 
 def first_kernel(
-    scal, b0, b1, b2, b3, h_up, h_dn, h_before, h_after, a0, a1, a2, a3, fld, near, hz, acc
+    scal, b0, b1, b2, b3, up_a, dn_a, up_b, dn_b, h_before, h_after, a0, a1, a2, a3, fld, near, hz, h_up, h_dn, acc
 ):
+    for whole, early, late in ((h_up, up_a, up_b), (h_dn, dn_a, dn_b)):
+        whole[0:AROWS, :] = early[0:AROWS, :]
+        whole[AROWS:FROWS, :] = late[...]
+        whole[FROWS:YROWS, :] = early[AROWS : AROWS + NX, :]
     join_columns(h_before, h_after, hz)
     active = scal[0]
     v_refs, outs = (b0, b1, b2, b3), (a0, a1, a2, a3)
@@ -449,10 +493,6 @@
     column = lax.broadcasted_iota(jnp.int32, (K, K), 1)
     before = jnp.where(scal[3] == 0, (row == column).astype(F32), raw[:, K : 2 * K])
     factor = inverse_factor(gram[:, 0:K])
-    other = inverse_factor(before)
-    image = small_dot(factor, gram[:, K : 2 * K], ((1,), (1,)))
-    diag_ref[...] = small_dot(image, factor, ((1,), (1,)))
-    off_ref[...] = small_dot(small_dot(factor, raw[:, 0:K]), other, ((1,), (1,)))
     fh, fl = halves(factor)
     matrix = jnp.concatenate([jnp.concatenate([fh, fh], axis=1), jnp.concatenate([fl, fl], axis=1)], axis=0)
     whole = K * NX
@@ -480,6 +520,10 @@
         lax.fori_loop(4 * c, 4 * c + 4, body, 0)
         lax.fori_loop(c * (whole // 128), (c + 1) * (whole // 128), to_bf16, 0)
         copy(c).start()
+    other = inverse_factor(before)
+    image = small_dot(factor, gram[:, K : 2 * K], ((1,), (1,)))
+    diag_ref[...] = small_dot(image, factor, ((1,), (1,)))
+    off_ref[...] = small_dot(small_dot(factor, raw[:, 0:K]), other, ((1,), (1,)))
     for c in range(3):
         copy(c).wait()
 
@@ -544,25 +588,43 @@
     near = f32(K + ZROWS, LANES)
     plane = pltpu.VMEM((NX, LANES), F32)
     columns = pltpu.VMEM((ZROWS, LANES), F32)
+    wide = pltpu.CompilerParams(vmem_limit_bytes=67_000_000)
+    hbm = pl.BlockSpec(memory_space=pl.ANY)
+    msg_a, msg_b = f32(AROWS + NX, LANES), f32(BROWS, LANES)
     packed = call(
-        pack_kernel,
+        pack_a_kernel,
         6,
-        (msg,) * 4,
-        (pltpu.VMEM((3 * K * NX, LANES), F32),)
+        (msg_a,) * 4,
+        (pltpu.VMEM((K * NX, LANES), F32),)
         + (plane,) * 4
-        + (pltpu.SemaphoreType.DMA((3,)), pltpu.SemaphoreType.DMA((4,))),
+        + (pltpu.SemaphoreType.DMA((1,)), pltpu.SemaphoreType.DMA((4,))),
         first=SM,
-        rest=pl.BlockSpec(memory_space=pl.ANY),
-        params=pltpu.CompilerParams(vmem_limit_bytes=67_000_000),
+        rest=hbm,
+        params=wide,
     )(scal, start, *fields)
-    got = to_rows(packed)
-    *v, z_edge = call(unpack_kernel, 5, (msg,) * 4 + (zmsg,), first=SM)(scal, *got)
-    hv = halo_y(v[3], v[0])
+    got_a = to_rows(packed)
+    packed = call(
+        pack_b_kernel,
+        2,
+        (msg_b,) * 4,
+        (pltpu.VMEM((2 * K * NX, LANES), F32), pltpu.SemaphoreType.DMA((2,))),
+        first=SM,
+        rest=hbm,
+        params=wide,
+    )(scal, start)
+    got_b = to_rows(packed)
+    *early, z_a = call(unpack_a_kernel, 5, (msg_a,) * 4 + (f32(K + NX, LANES),), first=SM)(scal, *got_a)
+    hv_a = halo_y(early[3], early[0])
+    *v, edge_dn, edge_up, z_edge = call(
+        unpack_b_kernel, 10, (msg,) * 4 + (msg_b, msg_b, zmsg), first=SM
+    )(scal, *got_b, *early, z_a)
+    hv_b = halo_y(edge_up, edge_dn)
     h_before, h_after = shift_x(z_edge, 1), shift_x(z_edge, 3)
     acc = pltpu.VMEM((4 * K, 2 * K), F32)
-    *av, fld, near_new, hv_z = call(
-        first_kernel, 9, (msg,) * 4 + (f32(10 * NX, LANES), near, zmsg), (acc,), first=SM
-    )(scal, *v, *hv, h_before, h_after)
+    *av, fld, near_new, hv_z, h_up, h_dn = call(
+        first_kernel, 11, (msg,) * 4 + (f32(10 * NX, LANES), near, zmsg, msg, msg), (acc,), first=SM
+    )(scal, *v, *hv_a, *hv_b, h_before, h_after)
+    hv = (h_up, h_dn)
     mat_shape = jax.ShapeDtypeStruct((2 * K, 4 * K), BF16)
     grams, ha = exchange(near_new, av)
     mat = call(matrix_kernel, 1, mat_shape)(grams)

time: 171 us -> 179 us (1.047)
  starting transfers between devices: 56.9 us -> 64.6 us
  waiting for transfers between devices: 60 us -> 56.2 us
  Pallas kernels: 48.4 us -> 51.2 us
    ppermute x3 -> x4, starting transfers between devices: 13.7 us -> 18.3 us  [halo_y(): h_dn = lax.ppermute(y_up, 'dom', [(i, i + 4) for i in range(12)])]
    ppermute x17 -> x20, waiting for transfers between devices: 50.8 us -> 47.3 us  [shift_x(): lax.ppermute(value, 'dom', [(i, (i & 12) + (i + d & 3)) for i in range(16)])]
    pallas_call x3 -> x5, Pallas kernels: 14.1 us -> 17.3 us  [the longest x1 6 us: blocks(): call(first_kernel, 11, (msg,) * 4 + (f32(10 * NX, LANES), near, zmsg, msg...]
    ppermute x17 -> x20, starting transfers between devices: 22.9 us -> 24.9 us  [shift_x(): lax.ppermute(value, 'dom', [(i, (i & 12) + (i + d & 3)) for i in range(16)])]
    ppermute x3 -> x4, starting transfers between devices: 3.87 us -> 5.17 us  [halo_y(): h_up = lax.ppermute(y_dn, 'dom', [(i + 4, i) for i in range(12)])]
  transfers between devices with their start and end apart: 33 -> 38, of which waited for: 12 -> 11; matrix products, arithmetic and copies ran while one was open for 0% -> 0% of each run, Pallas kernels for 3% -> 6%
where the time goes in v5:
time: 179 us; the launch traced here: 176 us
  starting transfers between devices  64.6 us (36%)
  waiting for transfers between devices  56.2 us (31%)
  Pallas kernels  51.2 us (29%)
  local copies, waits for them, and re-layouts  1.88 us (1%)
  between operations  1.82 us (1%)
    ppermute x20, waiting for transfers between devices, shift_x(): lax.ppermute(value, 'dom', [(i, (i & 12) + (i + d & 3)) for i in range(16)])  47.3 us
    ppermute x20, starting transfers between devices, shift_x(): lax.ppermute(value, 'dom', [(i, (i & 12) + (i + d & 3)) for i in range(16)])  24.9 us
    ppermute x4, starting transfers between devices, halo_y(): h_dn = lax.ppermute(y_up, 'dom', [(i, i + 4) for i in range(12)])  18.3 us
    ppermute x9, starting transfers between devices, shift_y(): return lax.ppermute(value, 'dom', [(i, i + 4 * d & 15) for i in range(16)])  14.3 us
    pallas_call x1, Pallas kernels, blocks(): call(functools.partial(step_kernel, False), 18, (msg,) * 8 + (near, msg,...  9.54 us
    pallas_call x1, Pallas kernels, blocks(): pl.pallas_call(out_kernel, out_shape=(jax.ShapeDtypeStruct((3 * K * NX, L...  9.5 us
    pallas_call x1, Pallas kernels, blocks(): call(functools.partial(step_kernel, True), 19, (f32(FROWS + K, LANES), f3...  9.47 us
    ppermute x1, waiting for transfers between devices, blocks(): before = lax.ppermute(img, 'sub', behind)  8.73 us
  transfers between devices with their start and end apart: 38, of which 11 were waited for; matrix products, arithmetic and copies ran while one was open for 0% of the time, Pallas kernels for 6%

profile of v5, /device:TPU:128, one launch (start us, length us, event | category | flops | bytes accessed | tf_op | source)
XLA Modules:
  0.0 176.4 jit_solution(13436089710095708639)
XLA Ops:
  1.9 3.5 %shard_map.86 = (f32[272,128]{1,0:T(8,128)}, f32[272,128]{1,0:T(8,128)}, f32[272,128]{1,0:T(8,128)}, f32[272,128]{1,0:T(8,128)}) custom-call(s32[4]{0:T(128)} %pad_add_fusion.scal, f32[3072,128]{1,0:T(8,128)} %bitcast.13, f32[16,128]{1,0:T(8,128)} %bitcast.15, f32[16,128]{1,0:T(8,128)} %bitcast.16, f32[16,128]{1,0:T(8,128)} %bitcast.17, f32[16,128]{1,0:T(8,128)} %bitcast.18), custom_call_target="tpu_custom_call" | custom-call | tf_op jit(solution)/shard_map/pallas_call | solution.py:594
  5.4 1.6 collective-permute-start.3
  7.0 4.3 %shard_map.85 = (f32[512,128]{1,0:T(8,128)}, f32[512,128]{1,0:T(8,128)}, f32[512,128]{1,0:T(8,128)}, f32[512,128]{1,0:T(8,128)}) custom-call(s32[4]{0:T(128)} %pad_add_fusion.scal, f32[3072,128]{1,0:T(8,128)} %bitcast.14), custom_call_target="tpu_custom_call" | custom-call | tf_op jit(solution)/shard_map/pallas_call | solution.py:606
  11.3 1.6 collective-permute-start
  12.9 1.7 collective-permute-start.1
  14.6 2.2 %collective-permute-start.2 = (f32[512,128]{1,0:T(8,128)}, f32[512,128]{1,0:T(8,128)S(1)}, u32[]{:S(2)}, u32[]{:S(2)}) collective-permute-start(f32[512,128]{1,0:T(8,128)} %get-tuple-element.57), channel_id=1, source_target_pairs={{0,3},{1,0},{2,1},{3,2},{4,7},{5,4},{6,5},{7,6},{8,11},{9,8},{10,9... | collective-permute-start | bytes 786440 | tf_op jit(solution)/shard_map/ppermute | solution.py:543
  17.6 1.7 collective-permute-start.5
  19.3 9.9 %collective-permute-done.4.r2 = f32[272,128]{1,0:T(8,128)S(1)} collective-permute-done((f32[272,128]{1,0:T(8,128)}, f32[272,128]{1,0:T(8,128)S(1)}, u32[]{:S(2)}, u32[]{:S(2)}) %collective-permute-start.4) | collective-permute-done | bytes 139296 | tf_op jit(solution)/shard_map/ppermute | solution.py:543
  29.2 3.6 %collective-permute-done.5.r3 = f32[272,128]{1,0:T(8,128)S(1)} collective-permute-done((f32[272,128]{1,0:T(8,128)}, f32[272,128]{1,0:T(8,128)S(1)}, u32[]{:S(2)}, u32[]{:S(2)}) %collective-permute-start.5) | collective-permute-done | bytes 139296 | tf_op jit(solution)/shard_map/ppermute | solution.py:543
  33.7 1.6 shard_map.87
  35.3 0.9 copy-done
  36.3 1.9 %shard_map.88 = (f32[784,128]{1,0:T(8,128)S(1)}, f32[784,128]{1,0:T(8,128)S(1)}, f32[784,128]{1,0:T(8,128)S(1)}, f32[784,128]{1,0:T(8,128)S(1)}, f32[512,128]{1,...) custom-call(s32[4]{0:T(128)S(1)} %copy-done.2, f32[512,128]{1,0:T(8,128)S(1)} %copy-done, ...), custom_call_target="tpu_custom_call" | custom-call | tf_op jit(solution)/shard_map/pallas_call | solution.py:618
  38.2 1.3 collective-permute-start.8
  39.5 4.6 %collective-permute-start.9 = (f32[512,128]{1,0:T(8,128)S(1)}, f32[512,128]{1,0:T(8,128)S(1)}, u32[]{:S(2)}, u32[]{:S(2)}) collective-permute-start(f32[512,128]{1,0:T(8,128)S(1)} %get-tuple-element.72), channel_id=1, source_target_pairs={{0,4},{1,5},{2,6},{3,7},{4,8},{5,9},{6,10},{7,11},{8,12},{9,13},{1... | collective-permute-start | bytes 786440 | tf_op jit(solution)/shard_map/ppermute | solution.py:551
  44.0 1.3 collective-permute-start.6
  45.3 4.6 %collective-permute-start.7 = (f32[272,128]{1,0:T(8,128)S(1)}, f32[272,128]{1,0:T(8,128)S(1)}, u32[]{:S(2)}, u32[]{:S(2)}) collective-permute-start(f32[272,128]{1,0:T(8,128)S(1)} %get-tuple-element.65.e3), channel_id=1, source_target_pairs={{0,4},{1,5},{2,6},{3,7},{4,8},{5,9},{6,10},{7,11},{8,12},{9,13},{1... | collective-permute-start | bytes 417800 | tf_op jit(solution)/shard_map/ppermute | solution.py:551
  49.9 2.7 %collective-permute-start.11 = (f32[224,128]{1,0:T(8,128)S(1)}, f32[224,128]{1,0:T(8,128)S(1)}, u32[]{:S(2)}, u32[]{:S(2)}) collective-permute-start(f32[224,128]{1,0:T(8,128)S(1)} %get-tuple-element.73), channel_id=1, source_target_pairs={{0,3},{1,0},{2,1},{3,2},{4,7},{5,4},{6,5},{7,6},{8,11},{9,8},{10,9... | collective-permute-start | bytes 344072 | tf_op jit(solution)/shard_map/ppermute | solution.py:543
  52.7 2.3 %collective-permute-done.11.h_after = f32[224,128]{1,0:T(8,128)S(1)} collective-permute-done((f32[224,128]{1,0:T(8,128)S(1)}, f32[224,128]{1,0:T(8,128)S(1)}, u32[]{:S(2)}, u32[]{:S(2)}) %collective-permute-start.11) | collective-permute-done | bytes 114720 | tf_op jit(solution)/shard_map/ppermute | solution.py:543
  55.0 3.6 %collective-permute-done.10.h_before = f32[224,128]{1,0:T(8,128)S(1)} collective-permute-done((f32[224,128]{1,0:T(8,128)S(1)}, f32[224,128]{1,0:T(8,128)S(1)}, u32[]{:S(2)}, u32[]{:S(2)}) %collective-permute-start.10) | collective-permute-done | bytes 114720 | tf_op jit(solution)/shard_map/ppermute | solution.py:543
  58.6 6.0 %shard_map.89 = (f32[784,128]{1,0:T(8,128)S(1)}, f32[784,128]{1,0:T(8,128)S(1)}, f32[784,128]{1,0:T(8,128)S(1)}, f32[784,128]{1,0:T(8,128)S(1)}, f32[160,128]{1,...) custom-call(s32[4]{0:T(128)S(1)} %copy-done.2, ...), custom_call_target="tpu_custom_call" | custom-call | tf_op jit(solution)/shard_map/pallas_call | solution.py:624
  64.6 1.6 collective-permute-start.13
  66.3 1.7 collective-permute-start.14
  67.9 2.0 %collective-permute-start.12 = (f32[64,128]{1,0:T(8,128)S(1)}, f32[64,128]{1,0:T(8,128)S(1)}, u32[]{:S(2)}, u32[]{:S(2)}) collective-permute-start(f32[64,128]{1,0:T(8,128)S(1)} %slice.24), channel_id=1, source_target_pairs={{0,8},{1,9},{2,10},{3,11},{4,12},{5,13},{6,14},{7,15},{8,0},{9,1},... | collective-permute-start | bytes 98312 | tf_op jit(solution)/shard_map/ppermute | solution.py:547
  69.9 1.3 collective-permute-start.18
  71.2 4.6 %collective-permute-start.19 = (f32[784,128]{1,0:T(8,128)S(1)}, f32[784,128]{1,0:T(8,128)S(1)}, u32[]{:S(2)}, u32[]{:S(2)}) collective-permute-start(f32[784,128]{1,0:T(8,128)S(1)} %get-tuple-element.77.refs_7_), channel_id=1, source_target_pairs={{0,4},{1,5},{2,6},{3,7},{4,8},{5,9},{6,10},{7,11},{8,12},{9,13},{1... | collective-permute-start | bytes 1204232 | tf_op jit(solution)/shard_map/ppermute | solution.py:551
  76.0 1.9 %collective-permute-start.16 = (f32[288,128]{1,0:T(8,128)S(1)}, f32[288,128]{1,0:T(8,128)S(1)}, u32[]{:S(2)}, u32[]{:S(2)}) collective-permute-start(f32[288,128]{1,0:T(8,128)S(1)} %pad_maximum_fusion), channel_id=1, source_target_pairs={{0,1},{1,2},{2,3},{3,0},{4,5},{5,6},{6,7},{7,4},{8,9},{9,10},{10,1... | collective-permute-start | bytes 442376 | tf_op jit(solution)/shard_map/ppermute | solution.py:543
  78.0 5.4 %collective-permute-done.15 = f32[64,128]{1,0:T(8,128)S(1)} collective-permute-done((f32[64,128]{1,0:T(8,128)S(1)}, f32[64,128]{1,0:T(8,128)S(1)}, u32[]{:S(2)}, u32[]{:S(2)}) %collective-permute-start.15) | collective-permute-done | bytes 32800 | tf_op jit(solution)/shard_map/ppermute | solution.py:543
  83.4 2.5 %shard_map.90.refs_9_ = bf16[128,256]{1,0:T(8,128)(2,1)S(1)} custom-call(f32[64,128]{1,0:T(8,128)S(1)} %fusion.1.grams), custom_call_target="tpu_custom_call" | custom-call | tf_op jit(solution)/shard_map/pallas_call | solution.py:630
  86.0 9.5 %shard_map.91 = (f32[784,128]{1,0:T(8,128)S(1)}, f32[784,128]{1,0:T(8,128)S(1)}, f32[784,128]{1,0:T(8,128)S(1)}, f32[784,128]{1,0:T(8,128)S(1)}, f32[784,128]{1,...) custom-call(s32[4]{0:T(128)S(1)} %copy-done.2, ...), custom_call_target="tpu_custom_call" | custom-call | tf_op jit(solution)/shard_map/pallas_call | solution.py:631
  95.6 3.2 %collective-permute-start.22 = (f32[64,128]{1,0:T(8,128)S(1)}, f32[64,128]{1,0:T(8,128)S(1)}, u32[]{:S(2)}, u32[]{:S(2)}) collective-permute-start(f32[64,128]{1,0:T(8,128)S(1)} %slice.28), channel_id=1, source_target_pairs={{0,12},{1,13},{2,14},{3,15},{4,0},{5,1},{6,2},{7,3},{8,4},{9,5},{1... | collective-permute-start | bytes 98312 | tf_op jit(solution)/shard_map/ppermute | solution.py:547
  99.2 1.3 collective-permute-start.26
  100.5 4.6 %collective-permute-start.27 = (f32[784,128]{1,0:T(8,128)S(1)}, f32[784,128]{1,0:T(8,128)S(1)}, u32[]{:S(2)}, u32[]{:S(2)}) collective-permute-start(f32[784,128]{1,0:T(8,128)S(1)} %get-tuple-element.90.refs_7_), channel_id=1, source_target_pairs={{0,4},{1,5},{2,6},{3,7},{4,8},{5,9},{6,10},{7,11},{8,12},{9,13},{1... | collective-permute-start | bytes 1204232 | tf_op jit(solution)/shard_map/ppermute | solution.py:551
  105.1 1.4 collective-permute-start.25
  107.2 1.6 collective-permute-start.23
  108.8 3.9 %collective-permute-done.23 = f32[64,128]{1,0:T(8,128)S(1)} collective-permute-done((f32[64,128]{1,0:T(8,128)S(1)}, f32[64,128]{1,0:T(8,128)S(1)}, u32[]{:S(2)}, u32[]{:S(2)}) %collective-permute-start.23) | collective-permute-done | bytes 32800 | tf_op jit(solution)/shard_map/ppermute | solution.py:543
  113.2 2.5 %shard_map.92.refs_9_ = bf16[128,256]{1,0:T(8,128)(2,1)S(1)} custom-call(f32[64,128]{1,0:T(8,128)S(1)} %fusion.grams), custom_call_target="tpu_custom_call" | custom-call | tf_op jit(solution)/shard_map/pallas_call | solution.py:640
  115.8 9.5 %shard_map.93 = (f32[832,128]{1,0:T(8,128)S(1)}, f32[64,128]{1,0:T(8,128)S(1)}, f32[768,128]{1,0:T(8,128)S(1)}, f32[768,128]{1,0:T(8,128)S(1)}, f32[768,128]{1,0:T(8,128)S(1)}, /*index=5*/f32[768,128]{1,0:T(8,128)S(1)}) custom-call(s32[4]{0:T(128)S(1)} %copy-done.2, f32[784,128]{1,0:T(8,128)S(1)} %get-tuple-element.83.refs_0_, ...), custom_call_target="tpu_custom_call" | custom-call | tf_op jit(solution)/shard_map/pallas_call | solution.py:643
  125.2 1.9 %collective-permute-start.28 = (f32[832,128]{1,0:T(8,128)S(1)}, f32[832,128]{1,0:T(8,128)S(1)}, u32[]{:S(2)}, u32[]{:S(2)}) collective-permute-start(f32[832,128]{1,0:T(8,128)S(1)} %get-tuple-element.101), channel_id=1, source_target_pairs={{0,16},{16,32},{32,48},{48,64},{64,80},{80,96},{96,112},{112,128},... | collective-permute-start | bytes 1277960 | tf_op jit(solution)/shard_map/ppermute | solution.py:651
  127.2 8.7 %collective-permute-done.28.img_ref = f32[832,128]{1,0:T(8,128)S(1)} collective-permute-done((f32[832,128]{1,0:T(8,128)S(1)}, f32[832,128]{1,0:T(8,128)S(1)}, u32[]{:S(2)}, u32[]{:S(2)}) %collective-permute-start.28) | collective-permute-done | bytes 426016 | tf_op jit(solution)/shard_map/ppermute | solution.py:651
  136.3 1.2 collective-permute-start.30
  137.5 2.1 %collective-permute-start.31 = (f32[128,128]{1,0:T(8,128)S(1)}, f32[128,128]{1,0:T(8,128)S(1)}, u32[]{:S(2)}, u32[]{:S(2)}) collective-permute-start(f32[128,128]{1,0:T(8,128)S(1)} %pad_maximum_fusion.2), channel_id=1, source_target_pairs={{0,12},{1,13},{2,14},{3,15},{4,0},{5,1},{6,2},{7,3},{8,4},{9,5},{1... | collective-permute-start | bytes 196616 | tf_op jit(solution)/shard_map/ppermute | solution.py:547
  139.6 2.0 %collective-permute-start.29 = (f32[128,128]{1,0:T(8,128)S(1)}, f32[128,128]{1,0:T(8,128)S(1)}, u32[]{:S(2)}, u32[]{:S(2)}) collective-permute-start(f32[128,128]{1,0:T(8,128)S(1)} %pad_maximum_fusion.2), channel_id=1, source_target_pairs={{0,8},{1,9},{2,10},{3,11},{4,12},{5,13},{6,14},{7,15},{8,0},{9,1},... | collective-permute-start | bytes 196616 | tf_op jit(solution)/shard_map/ppermute | solution.py:547
  141.6 3.4 %collective-permute-start.36 = (f32[768,128]{1,0:T(8,128)S(1)}, f32[768,128]{1,0:T(8,128)S(1)}, u32[]{:S(2)}, u32[]{:S(2)}) collective-permute-start(f32[768,128]{1,0:T(8,128)S(1)} %get-tuple-element.99.w2), channel_id=1, source_target_pairs={{0,2},{1,3},{2,0},{3,1},{4,6},{5,7},{6,4},{7,5},{8,10},{9,11},{10,... | collective-permute-start | bytes 1179656 | tf_op jit(solution)/shard_map/ppermute | solution.py:543
  145.4 2.0 %collective-permute-start.34 = (f32[128,128]{1,0:T(8,128)S(1)}, f32[128,128]{1,0:T(8,128)S(1)}, u32[]{:S(2)}, u32[]{:S(2)}) collective-permute-start(f32[128,128]{1,0:T(8,128)S(1)} %add_add_fusion.1), channel_id=1, source_target_pairs={{0,3},{1,0},{2,1},{3,2},{4,7},{5,4},{6,5},{7,6},{8,11},{9,8},{10,9... | collective-permute-start | bytes 196616 | tf_op jit(solution)/shard_map/ppermute | solution.py:543
  147.5 13.4 %collective-permute-done.34 = f32[128,128]{1,0:T(8,128)S(1)} collective-permute-done((f32[128,128]{1,0:T(8,128)S(1)}, f32[128,128]{1,0:T(8,128)S(1)}, u32[]{:S(2)}, u32[]{:S(2)}) %collective-permute-start.34) | collective-permute-done | bytes 65568 | tf_op jit(solution)/shard_map/ppermute | solution.py:543
  160.8 1.0 collective-permute-start.32
  161.9 4.7 %collective-permute-done.32 = f32[128,128]{1,0:T(8,128)S(1)} collective-permute-done((f32[128,128]{1,0:T(8,128)S(1)}, f32[128,128]{1,0:T(8,128)S(1)}, u32[]{:S(2)}, u32[]{:S(2)}) %collective-permute-start.32) | collective-permute-done | bytes 65568 | tf_op jit(solution)/shard_map/ppermute | solution.py:543
  166.7 9.5 %rows.1 = (bf16[3072,128]{1,0:T(8,128)(2,1)}, f32[64,64]{1,0:T(8,128)}, f32[64,64]{1,0:T(8,128)}) custom-call(s32[4]{0:T(128)S(1)} %copy-done.2, f32[128,128]{1,0:T(8,128)S(1)} %add_add_fusion.both, f32[768,128]{1,0:T(8,128)S(1)} %get-tuple-element.97.w0.r0, f32[768,128]{1,0:T(8,128)S(1)} %collective-permute-done.35.r1, ...), custom_call_target="tpu_custom_call" | custom-call | tf_op jit(solution)/shard_map/rows/pallas_call | solution.py:657
  (59 shorter events, 5.2 us)
Async XLA Ops:
  1.9 30.9 %copy-start.2 = (s32[4]{0:T(128)S(1)}, s32[4]{0:T(128)}, u32[]{:S(2)}) copy-start(s32[4]{0:T(128)} %pad_add_fusion.scal) | copy-start | bytes 52
  5.4 12.2 %collective-permute-start.3 = (f32[272,128]{1,0:T(8,128)}, f32[272,128]{1,0:T(8,128)}, u32[]{:S(2)}, u32[]{:S(2)}) collective-permute-start(f32[272,128]{1,0:T(8,128)} %get-tuple-element.59), channel_id=1, source_target_pairs={{0,1},{1,2},{2,3},{3,0},{4,5},{5,6},{6,7},{7,4},{8,9},{9,10},{10,1... | collective-permute-start | bytes 417800 | tf_op jit(solution)/shard_map/ppermute | solution.py:543
  11.3 24.0 %collective-permute-start = (f32[512,128]{1,0:T(8,128)}, f32[512,128]{1,0:T(8,128)S(1)}, u32[]{:S(2)}, u32[]{:S(2)}) collective-permute-start(f32[512,128]{1,0:T(8,128)} %get-tuple-element.55), channel_id=1, source_target_pairs={{0,1},{1,2},{2,3},{3,0},{4,5},{5,6},{6,7},{7,4},{8,9},{9,10},{10,1... | collective-permute-start | bytes 786440 | tf_op jit(solution)/shard_map/ppermute | solution.py:543
  12.9 22.4 %collective-permute-start.1 = (f32[512,128]{1,0:T(8,128)}, f32[512,128]{1,0:T(8,128)S(1)}, u32[]{:S(2)}, u32[]{:S(2)}) collective-permute-start(f32[512,128]{1,0:T(8,128)} %get-tuple-element.56), channel_id=1, source_target_pairs={{0,2},{1,3},{2,0},{3,1},{4,6},{5,7},{6,4},{7,5},{8,10},{9,11},{10,... | collective-permute-start | bytes 786440 | tf_op jit(solution)/shard_map/ppermute | solution.py:543
  14.6 20.7 %collective-permute-start.2 = (f32[512,128]{1,0:T(8,128)}, f32[512,128]{1,0:T(8,128)S(1)}, u32[]{:S(2)}, u32[]{:S(2)}) collective-permute-start(f32[512,128]{1,0:T(8,128)} %get-tuple-element.57), channel_id=1, source_target_pairs={{0,3},{1,0},{2,1},{3,2},{4,7},{5,4},{6,5},{7,6},{8,11},{9,8},{10,9... | collective-permute-start | bytes 786440 | tf_op jit(solution)/shard_map/ppermute | solution.py:543
  16.8 12.4 %collective-permute-start.4 = (f32[272,128]{1,0:T(8,128)}, f32[272,128]{1,0:T(8,128)S(1)}, u32[]{:S(2)}, u32[]{:S(2)}) collective-permute-start(f32[272,128]{1,0:T(8,128)} %get-tuple-element.60), channel_id=1, source_target_pairs={{0,2},{1,3},{2,0},{3,1},{4,6},{5,7},{6,4},{7,5},{8,10},{9,11},{10,... | collective-permute-start | bytes 417800 | tf_op jit(solution)/shard_map/ppermute | solution.py:543
  17.6 15.2 %collective-permute-start.5 = (f32[272,128]{1,0:T(8,128)}, f32[272,128]{1,0:T(8,128)S(1)}, u32[]{:S(2)}, u32[]{:S(2)}) collective-permute-start(f32[272,128]{1,0:T(8,128)} %get-tuple-element.61), channel_id=1, source_target_pairs={{0,3},{1,0},{2,1},{3,2},{4,7},{5,4},{6,5},{7,6},{8,11},{9,8},{10,9... | collective-permute-start | bytes 417800 | tf_op jit(solution)/shard_map/ppermute | solution.py:543
  32.8 0.9 copy-start.1
  35.3 1.0 copy-start
  38.2 20.4 %collective-permute-start.8 = (f32[512,128]{1,0:T(8,128)S(1)}, f32[512,128]{1,0:T(8,128)S(1)}, u32[]{:S(2)}, u32[]{:S(2)}) collective-permute-start(f32[512,128]{1,0:T(8,128)S(1)} %get-tuple-element.71), channel_id=1, source_target_pairs={{4,0},{5,1},{6,2},{7,3},{8,4},{9,5},{10,6},{11,7},{12,8},{13,9},{1... | collective-permute-start | bytes 786440 | tf_op jit(solution)/shard_map/ppermute | solution.py:552
  39.5 19.2 %collective-permute-start.9 = (f32[512,128]{1,0:T(8,128)S(1)}, f32[512,128]{1,0:T(8,128)S(1)}, u32[]{:S(2)}, u32[]{:S(2)}) collective-permute-start(f32[512,128]{1,0:T(8,128)S(1)} %get-tuple-element.72), channel_id=1, source_target_pairs={{0,4},{1,5},{2,6},{3,7},{4,8},{5,9},{6,10},{7,11},{8,12},{9,13},{1... | collective-permute-start | bytes 786440 | tf_op jit(solution)/shard_map/ppermute | solution.py:551
  44.0 8.6 %collective-permute-start.6 = (f32[272,128]{1,0:T(8,128)S(1)}, f32[272,128]{1,0:T(8,128)S(1)}, u32[]{:S(2)}, u32[]{:S(2)}) collective-permute-start(f32[272,128]{1,0:T(8,128)S(1)} %get-tuple-element.62.e0), channel_id=1, source_target_pairs={{4,0},{5,1},{6,2},{7,3},{8,4},{9,5},{10,6},{11,7},{12,8},{13,9},{1... | collective-permute-start | bytes 417800 | tf_op jit(solution)/shard_map/ppermute | solution.py:552
  45.3 7.4 %collective-permute-start.7 = (f32[272,128]{1,0:T(8,128)S(1)}, f32[272,128]{1,0:T(8,128)S(1)}, u32[]{:S(2)}, u32[]{:S(2)}) collective-permute-start(f32[272,128]{1,0:T(8,128)S(1)} %get-tuple-element.65.e3), channel_id=1, source_target_pairs={{0,4},{1,5},{2,6},{3,7},{4,8},{5,9},{6,10},{7,11},{8,12},{9,13},{1... | collective-permute-start | bytes 417800 | tf_op jit(solution)/shard_map/ppermute | solution.py:551
  49.9 5.1 %collective-permute-start.11 = (f32[224,128]{1,0:T(8,128)S(1)}, f32[224,128]{1,0:T(8,128)S(1)}, u32[]{:S(2)}, u32[]{:S(2)}) collective-permute-start(f32[224,128]{1,0:T(8,128)S(1)} %get-tuple-element.73), channel_id=1, source_target_pairs={{0,3},{1,0},{2,1},{3,2},{4,7},{5,4},{6,5},{7,6},{8,11},{9,8},{10,9... | collective-permute-start | bytes 344072 | tf_op jit(solution)/shard_map/ppermute | solution.py:543
  52.6 6.0 %collective-permute-start.10 = (f32[224,128]{1,0:T(8,128)S(1)}, f32[224,128]{1,0:T(8,128)S(1)}, u32[]{:S(2)}, u32[]{:S(2)}) collective-permute-start(f32[224,128]{1,0:T(8,128)S(1)} %get-tuple-element.73), channel_id=1, source_target_pairs={{0,1},{1,2},{2,3},{3,0},{4,5},{5,6},{6,7},{7,4},{8,9},{9,10},{10,1... | collective-permute-start | bytes 344072 | tf_op jit(solution)/shard_map/ppermute | solution.py:543
  64.6 11.2 %collective-permute-start.13 = (f32[64,128]{1,0:T(8,128)S(1)}, f32[64,128]{1,0:T(8,128)S(1)}, u32[]{:S(2)}, u32[]{:S(2)}) collective-permute-start(f32[64,128]{1,0:T(8,128)S(1)} %slice.24), channel_id=1, source_target_pairs={{0,4},{1,5},{2,6},{3,7},{4,8},{5,9},{6,10},{7,11},{8,12},{9,13},{1... | collective-permute-start | bytes 98312 | tf_op jit(solution)/shard_map/ppermute | solution.py:547
  66.3 9.6 %collective-permute-start.14 = (f32[64,128]{1,0:T(8,128)S(1)}, f32[64,128]{1,0:T(8,128)S(1)}, u32[]{:S(2)}, u32[]{:S(2)}) collective-permute-start(f32[64,128]{1,0:T(8,128)S(1)} %slice.24), channel_id=1, source_target_pairs={{0,12},{1,13},{2,14},{3,15},{4,0},{5,1},{6,2},{7,3},{8,4},{9,5},{1... | collective-permute-start | bytes 98312 | tf_op jit(solution)/shard_map/ppermute | solution.py:547
  67.9 7.9 %collective-permute-start.12 = (f32[64,128]{1,0:T(8,128)S(1)}, f32[64,128]{1,0:T(8,128)S(1)}, u32[]{:S(2)}, u32[]{:S(2)}) collective-permute-start(f32[64,128]{1,0:T(8,128)S(1)} %slice.24), channel_id=1, source_target_pairs={{0,8},{1,9},{2,10},{3,11},{4,12},{5,13},{6,14},{7,15},{8,0},{9,1},... | collective-permute-start | bytes 98312 | tf_op jit(solution)/shard_map/ppermute | solution.py:547
  69.9 16.0 %collective-permute-start.18 = (f32[784,128]{1,0:T(8,128)S(1)}, f32[784,128]{1,0:T(8,128)S(1)}, u32[]{:S(2)}, u32[]{:S(2)}) collective-permute-start(f32[784,128]{1,0:T(8,128)S(1)} %get-tuple-element.74.refs_4_), channel_id=1, source_target_pairs={{4,0},{5,1},{6,2},{7,3},{8,4},{9,5},{10,6},{11,7},{12,8},{13,9},{1... | collective-permute-start | bytes 1204232 | tf_op jit(solution)/shard_map/ppermute | solution.py:552
  71.2 14.7 %collective-permute-start.19 = (f32[784,128]{1,0:T(8,128)S(1)}, f32[784,128]{1,0:T(8,128)S(1)}, u32[]{:S(2)}, u32[]{:S(2)}) collective-permute-start(f32[784,128]{1,0:T(8,128)S(1)} %get-tuple-element.77.refs_7_), channel_id=1, source_target_pairs={{0,4},{1,5},{2,6},{3,7},{4,8},{5,9},{6,10},{7,11},{8,12},{9,13},{1... | collective-permute-start | bytes 1204232 | tf_op jit(solution)/shard_map/ppermute | solution.py:551
  75.9 7.5 %collective-permute-start.17 = (f32[288,128]{1,0:T(8,128)S(1)}, f32[288,128]{1,0:T(8,128)S(1)}, u32[]{:S(2)}, u32[]{:S(2)}) collective-permute-start(f32[288,128]{1,0:T(8,128)S(1)} %pad_maximum_fusion), channel_id=1, source_target_pairs={{0,3},{1,0},{2,1},{3,2},{4,7},{5,4},{6,5},{7,6},{8,11},{9,8},{10,9... | collective-permute-start | bytes 442376 | tf_op jit(solution)/shard_map/ppermute | solution.py:543
  76.0 7.4 %collective-permute-start.16 = (f32[288,128]{1,0:T(8,128)S(1)}, f32[288,128]{1,0:T(8,128)S(1)}, u32[]{:S(2)}, u32[]{:S(2)}) collective-permute-start(f32[288,128]{1,0:T(8,128)S(1)} %pad_maximum_fusion), channel_id=1, source_target_pairs={{0,1},{1,2},{2,3},{3,0},{4,5},{5,6},{6,7},{7,4},{8,9},{9,10},{10,1... | collective-permute-start | bytes 442376 | tf_op jit(solution)/shard_map/ppermute | solution.py:543
  78.0 5.4 %collective-permute-start.15 = (f32[64,128]{1,0:T(8,128)S(1)}, f32[64,128]{1,0:T(8,128)S(1)}, u32[]{:S(2)}, u32[]{:S(2)}) collective-permute-start(f32[64,128]{1,0:T(8,128)S(1)} %add_add_fusion.3), channel_id=1, source_target_pairs={{0,2},{1,3},{2,0},{3,1},{4,6},{5,7},{6,4},{7,5},{8,10},{9,11},{10,... | collective-permute-start | bytes 98312 | tf_op jit(solution)/shard_map/ppermute | solution.py:543
  95.5 9.6 %collective-permute-start.21 = (f32[64,128]{1,0:T(8,128)S(1)}, f32[64,128]{1,0:T(8,128)S(1)}, u32[]{:S(2)}, u32[]{:S(2)}) collective-permute-start(f32[64,128]{1,0:T(8,128)S(1)} %slice.28), channel_id=1, source_target_pairs={{0,4},{1,5},{2,6},{3,7},{4,8},{5,9},{6,10},{7,11},{8,12},{9,13},{1... | collective-permute-start | bytes 98312 | tf_op jit(solution)/shard_map/ppermute | solution.py:547
  95.6 9.5 %collective-permute-start.22 = (f32[64,128]{1,0:T(8,128)S(1)}, f32[64,128]{1,0:T(8,128)S(1)}, u32[]{:S(2)}, u32[]{:S(2)}) collective-permute-start(f32[64,128]{1,0:T(8,128)S(1)} %slice.28), channel_id=1, source_target_pairs={{0,12},{1,13},{2,14},{3,15},{4,0},{5,1},{6,2},{7,3},{8,4},{9,5},{1... | collective-permute-start | bytes 98312 | tf_op jit(solution)/shard_map/ppermute | solution.py:547
  98.8 6.3 %collective-permute-start.20 = (f32[64,128]{1,0:T(8,128)S(1)}, f32[64,128]{1,0:T(8,128)S(1)}, u32[]{:S(2)}, u32[]{:S(2)}) collective-permute-start(f32[64,128]{1,0:T(8,128)S(1)} %slice.28), channel_id=1, source_target_pairs={{0,8},{1,9},{2,10},{3,11},{4,12},{5,13},{6,14},{7,15},{8,0},{9,1},... | collective-permute-start | bytes 98312 | tf_op jit(solution)/shard_map/ppermute | solution.py:547
  99.2 16.5 %collective-permute-start.26 = (f32[784,128]{1,0:T(8,128)S(1)}, f32[784,128]{1,0:T(8,128)S(1)}, u32[]{:S(2)}, u32[]{:S(2)}) collective-permute-start(f32[784,128]{1,0:T(8,128)S(1)} %get-tuple-element.87.refs_4_), channel_id=1, source_target_pairs={{4,0},{5,1},{6,2},{7,3},{8,4},{9,5},{10,6},{11,7},{12,8},{13,9},{1... | collective-permute-start | bytes 1204232 | tf_op jit(solution)/shard_map/ppermute | solution.py:552
  100.5 15.2 %collective-permute-start.27 = (f32[784,128]{1,0:T(8,128)S(1)}, f32[784,128]{1,0:T(8,128)S(1)}, u32[]{:S(2)}, u32[]{:S(2)}) collective-permute-start(f32[784,128]{1,0:T(8,128)S(1)} %get-tuple-element.90.refs_7_), channel_id=1, source_target_pairs={{0,4},{1,5},{2,6},{3,7},{4,8},{5,9},{6,10},{7,11},{8,12},{9,13},{1... | collective-permute-start | bytes 1204232 | tf_op jit(solution)/shard_map/ppermute | solution.py:551
  105.1 7.6 %collective-permute-start.25 = (f32[288,128]{1,0:T(8,128)S(1)}, f32[288,128]{1,0:T(8,128)S(1)}, u32[]{:S(2)}, u32[]{:S(2)}) collective-permute-start(f32[288,128]{1,0:T(8,128)S(1)} %pad_maximum_fusion.1), channel_id=1, source_target_pairs={{0,3},{1,0},{2,1},{3,2},{4,7},{5,4},{6,5},{7,6},{8,11},{9,8},{10,9... | collective-permute-start | bytes 442376 | tf_op jit(solution)/shard_map/ppermute | solution.py:543
  106.5 6.7 %collective-permute-start.24 = (f32[288,128]{1,0:T(8,128)S(1)}, f32[288,128]{1,0:T(8,128)S(1)}, u32[]{:S(2)}, u32[]{:S(2)}) collective-permute-start(f32[288,128]{1,0:T(8,128)S(1)} %pad_maximum_fusion.1), channel_id=1, source_target_pairs={{0,1},{1,2},{2,3},{3,0},{4,5},{5,6},{6,7},{7,4},{8,9},{9,10},{10,1... | collective-permute-start | bytes 442376 | tf_op jit(solution)/shard_map/ppermute | solution.py:543
  107.2 5.5 %collective-permute-start.23 = (f32[64,128]{1,0:T(8,128)S(1)}, f32[64,128]{1,0:T(8,128)S(1)}, u32[]{:S(2)}, u32[]{:S(2)}) collective-permute-start(f32[64,128]{1,0:T(8,128)S(1)} %add_add_fusion.2), channel_id=1, source_target_pairs={{0,2},{1,3},{2,0},{3,1},{4,6},{5,7},{6,4},{7,5},{8,10},{9,11},{10,... | collective-permute-start | bytes 98312 | tf_op jit(solution)/shard_map/ppermute | solution.py:543
  125.2 10.7 %collective-permute-start.28 = (f32[832,128]{1,0:T(8,128)S(1)}, f32[832,128]{1,0:T(8,128)S(1)}, u32[]{:S(2)}, u32[]{:S(2)}) collective-permute-start(f32[832,128]{1,0:T(8,128)S(1)} %get-tuple-element.101), channel_id=1, source_target_pairs={{0,16},{16,32},{32,48},{48,64},{64,80},{80,96},{96,112},{112,128},... | collective-permute-start | bytes 1277960 | tf_op jit(solution)/shard_map/ppermute | solution.py:651
  136.3 8.7 %collective-permute-start.30 = (f32[128,128]{1,0:T(8,128)S(1)}, f32[128,128]{1,0:T(8,128)S(1)}, u32[]{:S(2)}, u32[]{:S(2)}) collective-permute-start(f32[128,128]{1,0:T(8,128)S(1)} %pad_maximum_fusion.2), channel_id=1, source_target_pairs={{0,4},{1,5},{2,6},{3,7},{4,8},{5,9},{6,10},{7,11},{8,12},{9,13},{1... | collective-permute-start | bytes 196616 | tf_op jit(solution)/shard_map/ppermute | solution.py:547
  137.5 7.8 %collective-permute-start.31 = (f32[128,128]{1,0:T(8,128)S(1)}, f32[128,128]{1,0:T(8,128)S(1)}, u32[]{:S(2)}, u32[]{:S(2)}) collective-permute-start(f32[128,128]{1,0:T(8,128)S(1)} %pad_maximum_fusion.2), channel_id=1, source_target_pairs={{0,12},{1,13},{2,14},{3,15},{4,0},{5,1},{6,2},{7,3},{8,4},{9,5},{1... | collective-permute-start | bytes 196616 | tf_op jit(solution)/shard_map/ppermute | solution.py:547
  139.6 5.8 %collective-permute-start.29 = (f32[128,128]{1,0:T(8,128)S(1)}, f32[128,128]{1,0:T(8,128)S(1)}, u32[]{:S(2)}, u32[]{:S(2)}) collective-permute-start(f32[128,128]{1,0:T(8,128)S(1)} %pad_maximum_fusion.2), channel_id=1, source_target_pairs={{0,8},{1,9},{2,10},{3,11},{4,12},{5,13},{6,14},{7,15},{8,0},{9,1},... | collective-permute-start | bytes 196616 | tf_op jit(solution)/shard_map/ppermute | solution.py:547
  141.6 25.1 %collective-permute-start.35 = (f32[768,128]{1,0:T(8,128)S(1)}, f32[768,128]{1,0:T(8,128)S(1)}, u32[]{:S(2)}, u32[]{:S(2)}) collective-permute-start(f32[768,128]{1,0:T(8,128)S(1)} %get-tuple-element.98.w1), channel_id=1, source_target_pairs={{0,1},{1,2},{2,3},{3,0},{4,5},{5,6},{6,7},{7,4},{8,9},{9,10},{10,1... | collective-permute-start | bytes 1179656 | tf_op jit(solution)/shard_map/ppermute | solution.py:543
  141.6 25.1 %collective-permute-start.36 = (f32[768,128]{1,0:T(8,128)S(1)}, f32[768,128]{1,0:T(8,128)S(1)}, u32[]{:S(2)}, u32[]{:S(2)}) collective-permute-start(f32[768,128]{1,0:T(8,128)S(1)} %get-tuple-element.99.w2), channel_id=1, source_target_pairs={{0,2},{1,3},{2,0},{3,1},{4,6},{5,7},{6,4},{7,5},{8,10},{9,11},{10,... | collective-permute-start | bytes 1179656 | tf_op jit(solution)/shard_map/ppermute | solution.py:543
  145.0 21.7 %collective-permute-start.37 = (f32[768,128]{1,0:T(8,128)S(1)}, f32[768,128]{1,0:T(8,128)S(1)}, u32[]{:S(2)}, u32[]{:S(2)}) collective-permute-start(f32[768,128]{1,0:T(8,128)S(1)} %get-tuple-element.100.w3), channel_id=1, source_target_pairs={{0,3},{1,0},{2,1},{3,2},{4,7},{5,4},{6,5},{7,6},{8,11},{9,8},{10,9... | collective-permute-start | bytes 1179656 | tf_op jit(solution)/shard_map/ppermute | solution.py:543
  145.4 15.5 %collective-permute-start.34 = (f32[128,128]{1,0:T(8,128)S(1)}, f32[128,128]{1,0:T(8,128)S(1)}, u32[]{:S(2)}, u32[]{:S(2)}) collective-permute-start(f32[128,128]{1,0:T(8,128)S(1)} %add_add_fusion.1), channel_id=1, source_target_pairs={{0,3},{1,0},{2,1},{3,2},{4,7},{5,4},{6,5},{7,6},{8,11},{9,8},{10,9... | collective-permute-start | bytes 196616 | tf_op jit(solution)/shard_map/ppermute | solution.py:543
  147.4 14.5 %collective-permute-start.33 = (f32[128,128]{1,0:T(8,128)S(1)}, f32[128,128]{1,0:T(8,128)S(1)}, u32[]{:S(2)}, u32[]{:S(2)}) collective-permute-start(f32[128,128]{1,0:T(8,128)S(1)} %add_add_fusion.1), channel_id=1, source_target_pairs={{0,1},{1,2},{2,3},{3,0},{4,5},{5,6},{6,7},{7,4},{8,9},{9,10},{10,1... | collective-permute-start | bytes 196616 | tf_op jit(solution)/shard_map/ppermute | solution.py:543
  160.8 5.8 %collective-permute-start.32 = (f32[128,128]{1,0:T(8,128)S(1)}, f32[128,128]{1,0:T(8,128)S(1)}, u32[]{:S(2)}, u32[]{:S(2)}) collective-permute-start(f32[128,128]{1,0:T(8,128)S(1)} %add_add_fusion.1), channel_id=1, source_target_pairs={{0,2},{1,3},{2,0},{3,1},{4,6},{5,7},{6,4},{7,5},{8,10},{9,11},{10,... | collective-permute-start | bytes 196616 | tf_op jit(solution)/shard_map/ppermute | solution.py:543
